TPU v7x, 32 devices: a whole 2x2x4 slice. The times are simulated.
32 devices in a mesh: mom: 8 (over z, x), row: 2 (over core), col: 2 (over y).
Axes of the slice: x: 2, y: 2, z: 4, core: 2. Of those that a mesh axis runs over, the one named last changes fastest.
Arguments:
- left_part: bfloat16 [8, 1536, 1536], P('mom', 'row', 'col'), may hold values from -0.15625 to 0.15625
- vertex: bfloat16 [8, 1536, 1536], P('mom', 'row', 'col'), may hold values from -6 to 6
- bubble: float32 [8, 1536], P('mom'), may hold values from 0.25 to 2
- cross_map: int32 [1536, 8], P(('col', 'mom')), may hold values from 0 to 7, each once within a row
Outputs:
- crossed: bfloat16 [1536, 8, 1536], P(('col', 'mom'), None, 'row')
Inputs may be any that keep to these rules, and one draw needn't show every extreme that they name: Each row cross_map[b, :] is a permutation of the 8 transfer momenta.
All inputs are finite; a program needn't handle non-finite values.
Results may differ from a plain program's by a relative error of at most 0.0055.
Values may be sent and summed in bfloat16 or wider, within the bound.
No kernel may reach another device: no remote copies, remote signals or barrier semaphores. Data moves between devices by JAX's collectives and lax.ppermute only.
A program may use at most 64 MiB of HBM per device.

v0:
```python
import jax
import jax.numpy as jnp
from jax import lax
from jax.sharding import PartitionSpec as P


def on_device(left_part, vertex, bubble, cross_map):
    left_full = lax.all_gather(left_part, "col", axis=2, tiled=True)
    weighted = (left_full.astype(jnp.float32) * bubble[:, None, :]).astype(jnp.bfloat16)
    local_q = vertex.shape[0]
    col_count = vertex.shape[2]
    row_count = weighted.shape[1]
    momenta = lax.axis_size("mom")
    per_device = col_count // momenta
    sliced = weighted
    first_term = jnp.einsum(
        "qkb,qak->qba",
        lax.all_gather(vertex, "row", axis=1, tiled=True),
        sliced,
        preferred_element_type=jnp.float32,
    )
    first_round = first_term.astype(jnp.bfloat16)
    flipped = jnp.swapaxes(vertex, 1, 2).astype(jnp.float32)
    sliced = weighted
    second_term = jnp.einsum(
        "qbk,qak->qba",
        lax.all_gather(first_round, "row", axis=2, tiled=True),
        sliced,
        preferred_element_type=jnp.float32,
    )
    summed = (flipped + first_term + second_term).astype(jnp.bfloat16)
    summed = summed.reshape(local_q, momenta, per_device, row_count)
    received = lax.all_to_all(summed, "mom", split_axis=1, concat_axis=0, tiled=True)
    regrouped = received.reshape(-1, per_device, received.shape[-1])
    which = jnp.arange(per_device, dtype=jnp.int32)[:, None]
    return regrouped[cross_map, which]


def solution(mesh):
    in_specs = (
        P("mom", "row", "col"),
        P("mom", "row", "col"),
        P("mom", None),
        P(("col", "mom"), None),
    )
    out_specs = P(("col", "mom"), None, "row")
    return jax.shard_map(
        on_device, mesh=mesh, in_specs=in_specs, out_specs=out_specs, check_vma=False
    )
```

profile of v0, /device:TPU:0, one launch (start us, length us, event | category | flops | bytes accessed | tf_op | source)
XLA Modules:
  0.0 135.0 jit_solution(14771618672102993497)
XLA Ops:
  6.5 0.0 copy-start.1
  6.5 0.0 all-gather.5.cloned.1.call-start
  6.5 0.7 all-gather.5.cloned.1.call-update
  7.3 0.0 all-gather.7.cloned.1.call-start
  7.3 0.7 all-gather.7.cloned.1.call-update
  8.0 0.0 all-gather.9.cloned.1.call-start
  8.1 0.0 copy-done.1
  8.1 0.0 copy-start
  8.1 39.6 %all-gather.5.cloned.1.call-done = bf16[1,768,1536]{2,1,0:T(8,128)(2,1)} async-done(((bf16[1,768,768]{2,1,0:T(8,128)(2,1)}), bf16[1,768,1536]{2,1,0:T(8,128)(2,1)}) %all-gather.5.cloned.1.call-update) | async-done | bytes 2359312 | tf_op jit(solution)/shard_map/all_gather | solution.py:8
  47.7 12.5 %all-gather.7.cloned.1.call-done = bf16[1,1536,768]{2,1,0:T(8,128)(2,1)} async-done(((bf16[1,768,768]{2,1,0:T(8,128)(2,1)}), bf16[1,1536,768]{2,1,0:T(8,128)(2,1)}) %all-gather.7.cloned.1.call-update) | async-done | bytes 2359312 | tf_op jit(solution)/shard_map/all_gather | solution.py:18
  60.2 6.2 %bitcast_convert_fusion = (bf16[768,768]{1,0:T(8,128)(2,1)}, f32[768,768]{0,1:T(8,128)}) fusion(bf16[1,1536,768]{2,1,0:T(8,128)(2,1)} %all-gather.7.cloned.1.call-done, bf16[1,768,1536]{2,1,0:T(8,128)(2,1)} %all-gather.5.cloned.1.call-done, f32[1536]{0:T(1024)S(1)} %reduce), kind=kOutput, calls=%fused_computation.6 | convolution fusion | flops 1816068096 | bytes 8263680 | tf_op jit(solution)/shard_map/qkb,qak->qba/dot_general | solution.py:16
  66.4 0.0 all-gather.9.cloned.1.call-update
  66.5 0.0 copy-done
  66.5 0.6 copy.8
  67.1 11.6 %all-gather.9.cloned.1.call-done = bf16[768,1536]{1,0:T(8,128)(2,1)} async-done(((bf16[768,768]{1,0:T(8,128)(2,1)}), bf16[768,1536]{1,0:T(8,128)(2,1)}) %all-gather.9.cloned.1.call-update) | async-done | bytes 2359312 | tf_op jit(solution)/shard_map/all_gather | solution.py:27
  78.7 6.1 %fusion.2 = bf16[1,768,768]{2,1,0:T(8,128)(2,1)} fusion(f32[768,768]{0,1:T(8,128)} %get-tuple-element.6, bf16[1,768,768]{1,2,0:T(8,128)(2,1)S(1)} %copy.8, bf16[768,1536]{1,0:T(8,128)(2,1)} %all-gather.9.cloned.1.call-done, bf16[1,768,1536]{2,1,0:T(8,128)(2,1)} %all-gather.5.cloned.1.call-done, f32[1536]{0:T(1024)S(1)} %reduce), kind=kOutput, calls=%fused_computation.5 | convolution fusion | flops 1817837568 | bytes 9443328 | tf_op jit(solution)/shard_map/qbk,qak->qba/dot_general | solution.py:25
  84.9 0.0 copy-start.2
  84.9 5.9 %all-to-all-start = ((bf16[1,8,96,768]{3,2,0,1:T(8,128)(2,1)}), bf16[1,8,96,768]{3,2,0,1:T(8,128)(2,1)S(1)}, u32[]{:S(2)}, u32[]{:S(2)}) async-start(bf16[1,8,96,768]{3,2,0,1:T(8,128)(2,1)} %bitcast.7), calls=%async_computation | async-start | bytes 2359296 | tf_op jit(solution)/shard_map/all_to_all | solution.py:33
  90.8 0.0 copy-done.2
  90.8 0.1 copy.10
  90.9 0.1 reshape.33
  91.0 28.8 %all-to-all-done = bf16[1,8,96,768]{3,2,0,1:T(8,128)(2,1)S(1)} async-done(((bf16[1,8,96,768]{3,2,0,1:T(8,128)(2,1)}), bf16[1,8,96,768]{3,2,0,1:T(8,128)(2,1)S(1)}, u32[]{:S(2)}, u32[]{:S(2)}) %all-to-all-start) | async-done | bytes 1179680 | tf_op jit(solution)/shard_map/all_to_all | solution.py:33
  119.8 8.7 %gather_fusion = bf16[768,768]{1,0:T(8,128)(2,1)} fusion(bf16[8,96,768]{2,1,0:T(8,128)(2,1)S(1)} %bitcast.38, s32[768]{0:T(1024)S(1)} %reshape.33), kind=kCustom, calls=%fused_computation | custom fusion | bytes 2365440 | tf_op jit(solution)/shard_map/gather | solution.py:36
  (2 shorter events, 0.0 us)
Async XLA Ops:
  6.5 1.5 %copy-start.1 = (f32[1,1536]{1,0:T(1,128)S(1)}, f32[1,1536]{1,0:T(1,128)}, u32[]{:S(2)}) copy-start(f32[1,1536]{1,0:T(1,128)} %param.6) | copy-start | bytes 18436
  6.5 41.1 %all-gather.5.cloned.1.call-start = ((), (), s32[]{:S(2)}) async-start(), calls=%async_computation.1 | async-start | bytes 3538944 | tf_op jit(solution)/shard_map/all_gather | solution.py:8
  7.3 53.0 %all-gather.7.cloned.1.call-start = ((), (), s32[]{:S(2)}) async-start(), calls=%async_computation.2 | async-start | bytes 3538944 | tf_op jit(solution)/shard_map/all_gather | solution.py:18
  8.0 70.7 %all-gather.9.cloned.1.call-start = ((), (), s32[]{:S(2)}) async-start(), calls=%async_computation.3 | async-start | bytes 3538944 | tf_op jit(solution)/shard_map/all_gather | solution.py:27
  8.1 58.4 %copy-start = (bf16[1,768,768]{2,1,0:T(8,128)(2,1)S(1)}, bf16[1,768,768]{2,1,0:T(8,128)(2,1)}, u32[]{:S(2)}) copy-start(bf16[1,768,768]{2,1,0:T(8,128)(2,1)} %param.5) | copy-start | bytes 3538948
  84.9 5.9 %copy-start.2 = (s32[96,8]{0,1:T(8,128)S(1)}, s32[96,8]{0,1:T(8,128)}, u32[]{:S(2)}) copy-start(s32[96,8]{0,1:T(8,128)} %param.7) | copy-start | bytes 9220
  84.9 34.9 %all-to-all-start = ((bf16[1,8,96,768]{3,2,0,1:T(8,128)(2,1)}), bf16[1,8,96,768]{3,2,0,1:T(8,128)(2,1)S(1)}, u32[]{:S(2)}, u32[]{:S(2)}) async-start(bf16[1,8,96,768]{3,2,0,1:T(8,128)(2,1)} %bitcast.7), calls=%async_computation | async-start | bytes 2359296 | tf_op jit(solution)/shard_map/all_to_all | solution.py:33
Sparse Core Ops, SparseCore 0:
  8.9 38.7 all-gather.4
  49.2 10.9 all-gather.6
  66.6 12.1 all-gather.8
where the time goes:
time: 135 us
  waiting for transfers between devices  94 us (70%)
  between operations  13.2 us (10%)
  matrix products  12.3 us (9%)
  local copies, waits for them, and re-layouts  9.52 us (7%)
  starting transfers between devices  5.99 us (4%)
    all_gather x1, waiting for transfers between devices, on_device(): left_full = lax.all_gather(left_part, 'col', axis=2, tiled=True)  39.6 us
    all_to_all x1, waiting for transfers between devices, on_device(): lax.all_to_all(summed, 'mom', split_axis=1, concat_axis=0, tiled=True)  28.8 us
    all_gather x1, waiting for transfers between devices, on_device(): lax.all_gather(vertex, 'row', axis=1, tiled=True)  12.5 us
    all_gather x1, waiting for transfers between devices, on_device(): lax.all_gather(first_round, 'row', axis=2, tiled=True)  11.6 us
    gather x1, local copies, waits for them, and re-layouts, on_device(): return regrouped[cross_map, which]  8.68 us
    dot_general x1, matrix products, on_device(): jnp.einsum('qkb,qak->qba', lax.all_gather(vertex, 'row', axis=1, tiled=Tr...  6.21 us
    dot_general x1, matrix products, on_device(): jnp.einsum('qbk,qak->qba', lax.all_gather(first_round, 'row', axis=2, til...  6.14 us
    all_to_all x1, starting transfers between devices, on_device(): lax.all_to_all(summed, 'mom', split_axis=1, concat_axis=0, tiled=True)  5.91 us
  transfers between devices with their start and end apart: 4, of which 4 were waited for; matrix products, arithmetic and copies ran while one was open for 1% of the time, Pallas kernels for 0%

commit v1 on v0

v1 whole, which is shorter than its diff:
```python
import jax
import jax.numpy as jnp
from jax import lax
from jax.sharding import PartitionSpec as P


def swap(value, axis):
    return lax.ppermute(value, axis, [(0, 1), (1, 0)])


def nt(x, y):
    return lax.dot_general(
        x, y, (((1,), (1,)), ((), ())), preferred_element_type=jnp.float32
    )


def on_device(left_part, vertex, bubble, cross_map):
    momenta = lax.axis_size("mom")
    col = lax.axis_index("col")
    same = lax.axis_index("row") == col
    left, vert = left_part[0], vertex[0]
    half = left.shape[1]
    columns = vert.shape[1]
    per_device = columns // momenta

    left_far = swap(left, "col")
    flipped = vert.T
    flipped_far = swap(flipped, "row")
    scale = bubble.reshape(2, half)
    near_scale = lax.dynamic_index_in_dim(scale, col, 0, keepdims=True)
    far_scale = lax.dynamic_index_in_dim(scale, 1 - col, 0, keepdims=True)
    near = (left.astype(jnp.float32) * near_scale).astype(jnp.bfloat16)
    far = (left_far.astype(jnp.float32) * far_scale).astype(jnp.bfloat16)

    first = nt(jnp.where(same, flipped, flipped_far), near)
    first = first + nt(jnp.where(same, flipped_far, flipped), far)
    rounded = first.astype(jnp.bfloat16)
    rounded_far = swap(rounded, "row")
    second = nt(jnp.where(same, rounded, rounded_far), near)
    second = second + nt(jnp.where(same, rounded_far, rounded), far)
    summed = (flipped.astype(jnp.float32) + first + second).astype(jnp.bfloat16)

    summed = summed.reshape(momenta, per_device, -1)
    received = lax.all_to_all(summed, "mom", split_axis=0, concat_axis=0, tiled=True)
    column = jnp.arange(per_device, dtype=jnp.int32)[:, None]
    source = (cross_map * per_device + column).reshape(-1, 1)
    pick = source == jnp.arange(columns, dtype=jnp.int32)[None, :]
    crossed = jnp.dot(
        pick.astype(jnp.bfloat16),
        received.reshape(columns, -1),
        preferred_element_type=jnp.float32,
    )
    return crossed.astype(jnp.bfloat16).reshape(per_device, momenta, -1)


def solution(mesh):
    in_specs = (
        P("mom", "row", "col"),
        P("mom", "row", "col"),
        P("mom", None),
        P(("col", "mom"), None),
    )
    out_specs = P(("col", "mom"), None, "row")
    return jax.shard_map(
        on_device, mesh=mesh, in_specs=in_specs, out_specs=out_specs, check_vma=False
    )
```

time: 135 us -> 80.1 us (0.59)
  waiting for transfers between devices: 94 us -> 58.1 us
  between operations: 13.2 us -> 0.08 us
  local copies, waits for them, and re-layouts: 9.52 us -> 1.89 us
  starting transfers between devices: 5.99 us -> 9.38 us
  matrix products: 12.3 us -> 10.3 us
    all_gather x3 -> x0, waiting for transfers between devices: 63.7 us -> none  [the longest x1 39.6 us: on_device(): left_full = lax.all_gather(left_part, 'col', axis=2, tiled=True)]
    ppermute x0 -> x3, waiting for transfers between devices: none -> 29.4 us  [swap(): return lax.ppermute(value, axis, [(0, 1), (1, 0)])]
    gather x1 -> x0, local copies, waits for them, and re-layouts: 8.68 us -> none  [on_device(): return regrouped[cross_map, which]]
    ppermute x0 -> x3, starting transfers between devices: none -> 3.22 us  [swap(): return lax.ppermute(value, axis, [(0, 1), (1, 0)])]
    dot_general x2 -> x5, matrix products: 12.3 us -> 10.3 us  [the longest x4 8.11 us: nt(): lax.dot_general(x, y, (((1,), (1,)), ((), ())), preferred_element_type=jn...]
    unnamed x3 -> x0, waiting for transfers between devices: 1.42 us -> none
  transfers between devices with their start and end apart: 4 -> 4, of which waited for: 4 -> 3; matrix products, arithmetic and copies ran while one was open for 1% -> 0% of each run, Pallas kernels for 0% -> 0%
where the time goes in v1:
time: 80.1 us; the launch traced here: 79.8 us
  waiting for transfers between devices  58.1 us (73%)
  matrix products  10.3 us (13%)
  starting transfers between devices  9.38 us (12%)
  local copies, waits for them, and re-layouts  1.89 us (2%)
    ppermute x3, waiting for transfers between devices, swap(): return lax.ppermute(value, axis, [(0, 1), (1, 0)])  29.4 us
    all_to_all x1, waiting for transfers between devices, on_device(): lax.all_to_all(summed, 'mom', split_axis=0, concat_axis=0, tiled=True)  28.7 us
    dot_general x4, matrix products, nt(): lax.dot_general(x, y, (((1,), (1,)), ((), ())), preferred_element_type=jn...  8.11 us
    all_to_all x1, starting transfers between devices, on_device(): lax.all_to_all(summed, 'mom', split_axis=0, concat_axis=0, tiled=True)  6.16 us
    ppermute x3, starting transfers between devices, swap(): return lax.ppermute(value, axis, [(0, 1), (1, 0)])  3.22 us
    dot_general x1, matrix products, on_device(): jnp.dot(pick.astype(jnp.bfloat16), received.reshape(columns, -1), preferr...  2.21 us
    unnamed x7, local copies, waits for them, and re-layouts  1.67 us
  transfers between devices with their start and end apart: 4, of which 3 were waited for; matrix products, arithmetic and copies ran while one was open for 0% of the time, Pallas kernels for 0%

profile of v1, /device:TPU:0, one launch (start us, length us, event | category | flops | bytes accessed | tf_op | source)
XLA Modules:
  0.0 79.8 jit_solution(12050796102690497546)
XLA Ops:
  0.0 0.0 copy-start
  0.0 0.0 copy-start.1
  0.0 1.7 %copy.7 = bf16[1,768,768]{1,2,0:T(8,128)(2,1)S(1)} copy(bf16[1,768,768]{2,1,0:T(8,128)(2,1)} %param.5) | data formatting | bytes 2359296 | tf_op args[1]
  1.7 0.6 collective-permute-start
  2.2 0.0 copy-done
  2.2 2.6 %collective-permute-start.1 = (bf16[768,768]{1,0:T(8,128)(2,1)S(1)}, bf16[768,768]{1,0:T(8,128)(2,1)}, u32[]{:S(2)}, u32[]{:S(2)}) collective-permute-start(bf16[768,768]{1,0:T(8,128)(2,1)S(1)} %bitcast.31), channel_id=1, source_target_pairs={{0,1},{1,0},{2,3},{3,2},{4,5},{5,4},{6,7},{7,6},{8,9},{9,8},{10,11... | collective-permute-start | bytes 3538952 | tf_op jit(solution)/shard_map/ppermute | solution.py:8
  4.8 0.0 copy-done.1
  4.9 0.0 collective-permute-done
  4.9 26.6 %collective-permute-done.1 = bf16[768,768]{1,0:T(8,128)(2,1)} collective-permute-done((bf16[768,768]{1,0:T(8,128)(2,1)S(1)}, bf16[768,768]{1,0:T(8,128)(2,1)}, u32[]{:S(2)}, u32[]{:S(2)}) %collective-permute-start.1) | collective-permute-done | bytes 1179680 | tf_op jit(solution)/shard_map/ppermute | solution.py:8
  31.5 2.4 %fusion.6 = f32[768,768]{1,0:T(8,128)S(1)} fusion(bf16[768,768]{1,0:T(8,128)(2,1)S(1)} %collective-permute-done, pred[]{:T(512)S(6)} %eq.22, bf16[768,768]{1,0:T(8,128)(2,1)} %collective-permute-done.1, f32[768]{0:T(1024)S(1)} %get-tuple-element.6, bf16[1,768,768]{1,2,0:T(8,128)(2,1)S(1)} %copy.7), kind=kOutput, calls=%fused_computation.11 | convolution fusion | flops 908328960 | bytes 5901313 | tf_op jit(solution)/shard_map/dot_general | solution.py:12
  33.9 1.2 %fusion.18 = (bf16[768,768]{1,0:T(8,128)(2,1)S(1)}, f32[768,768]{1,0:T(8,128)S(1)}) fusion(f32[768,768]{1,0:T(8,128)S(1)} %fusion.6, f32[768]{0:T(1024)S(1)} %get-tuple-element.5, bf16[1,768,768]{2,1,0:T(8,128)(2,1)S(1)} %copy-done, bf16[768,768]{1,0:T(8,128)(2,1)S(1)} %collective-permute-done, pred[]{:T(512)S(6)} %eq.22, bf16[1,768,768]{1,2,0:T(8,128)(2,1)S(1)} %copy.7), kind=kOutput, calls=%fused_computation.26 | convolution fusion | flops 909508608 | bytes 9440257 | tf_op jit(solution)/shard_map/dot_general | solution.py:12
  35.1 0.1 collective-permute-start.2
  35.1 2.8 %collective-permute-done.2 = bf16[768,768]{1,0:T(8,128)(2,1)S(1)} collective-permute-done((bf16[768,768]{1,0:T(8,128)(2,1)S(1)}, bf16[768,768]{1,0:T(8,128)(2,1)S(1)}, u32[]{:S(2)}, u32[]{:S(2)}) %collective-permute-start.2) | collective-permute-done | bytes 1179680 | tf_op jit(solution)/shard_map/ppermute | solution.py:8
  38.0 2.4 %fusion.3 = f32[768,768]{1,0:T(8,128)S(1)} fusion(bf16[768,768]{1,0:T(8,128)(2,1)S(1)} %collective-permute-done.2, bf16[768,768]{1,0:T(8,128)(2,1)S(1)} %get-tuple-element.7, pred[]{:T(512)S(6)} %eq.22, bf16[768,768]{1,0:T(8,128)(2,1)} %collective-permute-done.1, f32[768]{0:T(1024)S(1)} %get-tuple-element.6), kind=kOutput, calls=%fused_computation.8 | convolution fusion | flops 908328960 | bytes 5901313 | tf_op jit(solution)/shard_map/dot_general | solution.py:12
  40.4 2.2 %add_convert_fusion = bf16[768,768]{1,0:T(8,128)(2,1)} fusion(f32[768,768]{1,0:T(8,128)S(1)} %fusion.3, f32[768,768]{1,0:T(8,128)S(1)} %get-tuple-element.8, bf16[768,768]{1,0:T(8,128)(2,1)S(1)} %get-tuple-element.7, bf16[768,768]{1,0:T(8,128)(2,1)S(1)} %collective-permute-done.2, pred[]{:T(512)S(6)} %eq.22, f32[768]{0:T(1024)S(1)} %get-tuple-element.5, ...), kind=kOutput, calls=%fused_computation | convolution fusion | flops 911278080 | bytes 10619905 | tf_op jit(solution)/shard_map/dot_general | solution.py:12
  42.5 0.0 copy-start.2
  42.5 6.2 %all-to-all-start = ((bf16[8,96,768]{2,1,0:T(8,128)(2,1)}), bf16[8,96,768]{2,1,0:T(8,128)(2,1)S(1)}, u32[]{:S(2)}, u32[]{:S(2)}) async-start(bf16[8,96,768]{2,1,0:T(8,128)(2,1)} %bitcast.4), calls=%async_computation | async-start | bytes 2359296 | tf_op jit(solution)/shard_map/all_to_all | solution.py:44
  48.7 0.0 copy-done.2
  48.7 0.1 copy.6
  48.8 0.1 eq.18
  48.9 28.7 %all-to-all-done = bf16[8,96,768]{2,1,0:T(8,128)(2,1)S(1)} async-done(((bf16[8,96,768]{2,1,0:T(8,128)(2,1)}), bf16[8,96,768]{2,1,0:T(8,128)(2,1)S(1)}, u32[]{:S(2)}, u32[]{:S(2)}) %all-to-all-start) | async-done | bytes 1179680 | tf_op jit(solution)/shard_map/all_to_all | solution.py:44
  77.6 2.2 %fusion.2 = bf16[96,8,768]{2,1,0:T(8,128)(2,1)} fusion(bf16[768,768]{1,0:T(8,128)(2,1)S(1)} %bitcast.32, s32[768]{0:T(1024)S(1)} %eq.18), kind=kOutput, calls=%fused_computation.7 | convolution fusion | flops 907149312 | bytes 2362368 | tf_op jit(solution)/shard_map/dot_general | solution.py:48
  (4 shorter events, 0.1 us)
Async XLA Ops:
  0.0 2.2 %copy-start = (bf16[1,768,768]{2,1,0:T(8,128)(2,1)S(1)}, bf16[1,768,768]{2,1,0:T(8,128)(2,1)}, u32[]{:S(2)}) copy-start(bf16[1,768,768]{2,1,0:T(8,128)(2,1)} %param.4) | copy-start | bytes 3538948
  0.0 4.8 %copy-start.1 = (f32[1,1536]{1,0:T(1,128)S(1)}, f32[1,1536]{1,0:T(1,128)}, u32[]{:S(2)}) copy-start(f32[1,1536]{1,0:T(1,128)} %param.6) | copy-start | bytes 18436
  1.7 3.2 %collective-permute-start = (bf16[768,768]{1,0:T(8,128)(2,1)S(1)}, bf16[768,768]{1,0:T(8,128)(2,1)S(1)}, u32[]{:S(2)}, u32[]{:S(2)}) collective-permute-start(bf16[768,768]{1,0:T(8,128)(2,1)S(1)} %bitcast.30), channel_id=1, source_target_pairs={{0,2},{2,0},{1,3},{3,1},{4,6},{6,4},{5,7},{7,5},{8,10},{10,8},{9,1... | collective-permute-start | bytes 3538952 | tf_op jit(solution)/shard_map/ppermute | solution.py:8
  2.2 29.2 %collective-permute-start.1 = (bf16[768,768]{1,0:T(8,128)(2,1)S(1)}, bf16[768,768]{1,0:T(8,128)(2,1)}, u32[]{:S(2)}, u32[]{:S(2)}) collective-permute-start(bf16[768,768]{1,0:T(8,128)(2,1)S(1)} %bitcast.31), channel_id=1, source_target_pairs={{0,1},{1,0},{2,3},{3,2},{4,5},{5,4},{6,7},{7,6},{8,9},{9,8},{10,11... | collective-permute-start | bytes 3538952 | tf_op jit(solution)/shard_map/ppermute | solution.py:8
  35.1 2.9 %collective-permute-start.2 = (bf16[768,768]{1,0:T(8,128)(2,1)S(1)}, bf16[768,768]{1,0:T(8,128)(2,1)S(1)}, u32[]{:S(2)}, u32[]{:S(2)}) collective-permute-start(bf16[768,768]{1,0:T(8,128)(2,1)S(1)} %get-tuple-element.7), channel_id=1, source_target_pairs={{0,2},{2,0},{1,3},{3,1},{4,6},{6,4},{5,7},{7,5},{8,10},{10,8},{9,1... | collective-permute-start | bytes 3538952 | tf_op jit(solution)/shard_map/ppermute | solution.py:8
  42.5 6.2 %copy-start.2 = (s32[96,8]{0,1:T(8,128)S(1)}, s32[96,8]{0,1:T(8,128)}, u32[]{:S(2)}) copy-start(s32[96,8]{0,1:T(8,128)} %param.7) | copy-start | bytes 9220
  42.5 35.0 %all-to-all-start = ((bf16[8,96,768]{2,1,0:T(8,128)(2,1)}), bf16[8,96,768]{2,1,0:T(8,128)(2,1)S(1)}, u32[]{:S(2)}, u32[]{:S(2)}) async-start(bf16[8,96,768]{2,1,0:T(8,128)(2,1)} %bitcast.4), calls=%async_computation | async-start | bytes 2359296 | tf_op jit(solution)/shard_map/all_to_all | solution.py:44

commit v2 on v1

v2 whole, which is shorter than its diff:
```python
import jax
import jax.numpy as jnp
from jax import lax
from jax.experimental import pallas as pl
from jax.experimental.pallas import tpu as pltpu
from jax.sharding import PartitionSpec as P


LIMIT = pltpu.CompilerParams(vmem_limit_bytes=16 << 20)
VMEM = pl.BlockSpec(memory_space=pltpu.VMEM)
HBM = pl.BlockSpec(memory_space=pltpu.HBM)
ANY = pl.BlockSpec(memory_space=pl.ANY)
BF, F32 = jnp.bfloat16, jnp.float32


def swap(value, axis):
    return lax.ppermute(value, axis, [(0, 1), (1, 0)])


def nt(x, y):
    return lax.dot_general(
        x, y, (((1,), (1,)), ((), ())), preferred_element_type=F32
    )


def local(body, outs, *arrays, aliases=None, flops=0, scratch=()):
    arrays = [pltpu.with_memory_space_constraint(a, pltpu.VMEM) for a in arrays]
    many = isinstance(outs, list)
    return pl.pallas_call(
        body,
        out_shape=outs,
        in_specs=[VMEM] * len(arrays),
        out_specs=[VMEM] * len(outs) if many else VMEM,
        scratch_shapes=scratch,
        input_output_aliases=aliases or {},
        compiler_params=LIMIT,
        cost_estimate=pl.CostEstimate(
            flops=flops, bytes_accessed=1 << 20, transcendentals=0
        ),
    )(*arrays)


def fetch(array, spans):
    def body(source, *refs):
        outs, sem = refs[:-1], refs[-1]
        copies = [
            pltpu.make_async_copy(source.at[s:e, :], out, sem.at[i])
            for i, (out, (s, e)) in enumerate(zip(outs, spans))
        ]
        for copy in copies:
            copy.start()
        for copy in copies:
            copy.wait()

    return pl.pallas_call(
        body,
        out_shape=[
            pltpu.VMEM((e - s, array.shape[1]), array.dtype) for s, e in spans
        ],
        in_specs=[HBM],
        out_specs=[VMEM] * len(spans),
        scratch_shapes=[pltpu.SemaphoreType.DMA((len(spans),))],
        compiler_params=LIMIT,
    )(pltpu.with_memory_space_constraint(array, pltpu.HBM))


def flip_body(vert, out):
    out[...] = vert[...].T


def near_body(left, bubble, flipped, flipped_far, halves, first, other):
    row, col = lax.axis_index("row"), lax.axis_index("col")
    half = left.shape[1]
    scale = bubble[:, pl.ds(pl.multiple_of(col * half, half), half)]
    near = (left[...].astype(F32) * scale).astype(BF)
    halves[col] = near

    @pl.when(row == col)
    def _():
        first[...] = nt(flipped[...], near)
        other[...] = flipped_far[...]

    @pl.when(row != col)
    def _():
        first[...] = nt(flipped_far[...], near)
        other[...] = flipped[...]


def chunk_body(start, stop):
    def body(far, bubble, other, _, __, halves, first, rounded):
        col = 1 - lax.axis_index("col")
        half = far.shape[1]
        scale = bubble[:, pl.ds(pl.multiple_of(col * half, half), half)]
        scaled = (far[...].astype(F32) * scale).astype(BF)
        halves[col, start:stop, :] = scaled
        total = first[:, start:stop] + nt(other[...], scaled)
        first[:, start:stop] = total
        rounded[...] = total.astype(BF)

    return body


def early_body(cuts):
    def body(halves, own0, own1, far0, far1, out):
        row = lax.axis_index("row")
        a, b, _ = cuts
        total = nt(own0[...], halves[row, :b, :a])
        total += nt(far0[...], halves[1 - row, :b, :a])
        total += nt(own1[...], halves[row, :b, a:b])
        total += nt(far1[...], halves[1 - row, :b, a:b])
        out[...] = total

    return body


def late_body(cuts):
    def body(halves, own0, own1, own2, far0, far1, early, flipped, first, out):
        row = lax.axis_index("row")
        a, b, c = cuts
        out[:, :b] = (
            early[...]
            + nt(own2[...], halves[row, :b, b:c])
            + (flipped[:, :b].astype(F32) + first[:, :b])
        )
        total = flipped[:, b:].astype(F32) + first[:, b:]
        total += nt(own0[...], halves[row, b:, :a])
        total += nt(own1[...], halves[row, b:, a:b])
        total += nt(own2[...], halves[row, b:, b:c])
        total += nt(far0[...], halves[1 - row, b:, :a])
        total += nt(far1[...], halves[1 - row, b:, a:b])
        out[:, b:] = total

    return body


def last_body(cuts, partners):
    def body(halves, far2, late, *refs):
        row, mom = lax.axis_index("row"), lax.axis_index("mom")
        _, b, c = cuts
        outs, done = refs[:-1], refs[-1]
        done[...] = (
            late[...] + nt(far2[...], halves[1 - row, :, b:c])
        ).astype(BF)
        size = outs[0].shape[0]
        for out, partner in zip(outs, partners):
            begin = (mom ^ partner) * size if len(outs) > 1 else 0
            out[...] = done[pl.ds(pl.multiple_of(begin, size), size), :]

    return body


def cross_body(partners, momenta, group):
    def body(pick, *refs):
        blocks, (out, gathered, result, sem) = refs[:-4], refs[-4:]
        mom = lax.axis_index("mom")
        per = blocks[0].shape[0]
        copies = []
        for i in range(per // group):
            for block, partner in zip(blocks, partners):
                begin = pl.multiple_of((mom ^ partner) * group, group)
                gathered[i, pl.ds(begin, group), :] = block[
                    i * group : (i + 1) * group, :
                ]
            size = group * momenta
            span = slice(i * size, (i + 1) * size)
            result[span, :] = jnp.dot(
                pick[span, :], gathered[i], preferred_element_type=F32
            ).astype(BF)
            copy = pltpu.make_async_copy(
                result.at[span, :], out.at[span, :], sem.at[i]
            )
            copy.start()
            copies.append(copy)
        for copy in copies:
            copy.wait()

    return body


def xor_partners(momenta):
    def key(k):
        return (-k.bit_length(), int(format(k, "b")[::-1], 2))

    return [0] + sorted(range(1, momenta), key=key)


def pick_body(group):
    def body(cross_map, out):
        momenta, per = cross_map.shape
        wide = (momenta * per, per)
        line = lax.broadcasted_iota(jnp.int32, wide, 0) // momenta
        spread = (line == lax.broadcasted_iota(jnp.int32, wide, 1)).astype(BF)
        known = nt(spread, cross_map[...].astype(F32).astype(BF))
        tall = (momenta * per, momenta)
        line = lax.broadcasted_iota(jnp.int32, tall, 0)
        mine = line % momenta == lax.broadcasted_iota(jnp.int32, tall, 1)
        wanted = jnp.sum(jnp.where(mine, known, 0.0), axis=1, keepdims=True)
        column = (line[:, :1] // momenta) % group
        wanted = wanted.astype(jnp.int32) * group + column
        spot = lax.broadcasted_iota(jnp.int32, out.shape, 1)
        out[...] = jnp.where(spot == wanted, 1.0, 0.0).astype(BF)

    return body


def on_device(left_part, vertex, bubble, cross_map):
    momenta = lax.axis_size("mom")
    left, vert = left_part[0], vertex[0]
    rows, half = left.shape
    columns = vert.shape[1]
    per_device = columns // momenta
    cuts = (rows // 2, rows // 2 + rows // 3, rows)
    square = 2 * columns * half
    starts = (0,) + cuts[:-1]
    spans = list(zip(starts, cuts))

    pieces = fetch(left, spans[:1])
    pieces += fetch(left, spans[1:])
    fars = []
    for piece in pieces:
        fars.append(swap(piece, "col"))
    flipped = local(flip_body, pltpu.VMEM((columns, rows), BF), vert)
    flipped_far = swap(flipped, "row")
    halves, first, other = local(
        near_body,
        [
            pltpu.VMEM((2, rows, half), BF),
            pltpu.VMEM((columns, rows), F32),
            pltpu.VMEM((columns, half), BF),
        ],
        left,
        bubble,
        flipped,
        flipped_far,
        flops=square * rows,
    )
    direct = per_device % 16 == 0 and momenta & (momenta - 1) == 0
    group = 16 * (2 - per_device // 16 % 2) if direct else per_device
    pick = local(
        pick_body(group),
        pltpu.VMEM((columns, momenta * group), BF),
        cross_map.T,
    )
    own, others = [], []

    def arrive(i, halves, first):
        s, e = spans[i]
        halves, first, rounded = local(
            chunk_body(s, e),
            [
                pltpu.VMEM((2, rows, half), BF),
                pltpu.VMEM((columns, rows), F32),
                pltpu.VMEM((columns, e - s), BF),
            ],
            fars[i],
            bubble,
            other,
            halves,
            first,
            aliases={3: 0, 4: 1},
            flops=square * (e - s),
        )
        own.append(rounded)
        others.append(swap(rounded, "row"))
        return halves, first

    halves, first = arrive(0, halves, first)
    halves, first = arrive(1, halves, first)
    early = local(
        early_body(cuts),
        pltpu.VMEM((columns, cuts[1]), F32),
        halves,
        *own,
        *others,
        flops=square * 2 * cuts[1],
    )
    halves, first = arrive(2, halves, first)
    late = local(
        late_body(cuts),
        pltpu.VMEM((columns, rows), F32),
        halves,
        *own,
        *others[:2],
        early,
        flipped,
        first,
        flops=square * (rows - cuts[1]) * 3,
    )
    partners = xor_partners(momenta) if direct else [0]
    size = per_device if direct else columns
    sent = local(
        last_body(cuts, partners),
        [pltpu.VMEM((size, rows), BF)] * len(partners),
        halves,
        others[2],
        late,
        scratch=[pltpu.VMEM((columns, rows), BF)],
    )
    if not direct:
        received = lax.all_to_all(
            sent[0].reshape(momenta, per_device, rows),
            "mom",
            split_axis=0,
            concat_axis=0,
            tiled=True,
        )
        crossed = jnp.dot(
            pick, received.reshape(columns, rows), preferred_element_type=F32
        )
        return crossed.astype(BF).reshape(per_device, momenta, rows)

    got = [sent[0]]
    for block, k in zip(sent[1:], partners[1:]):
        pairs = [(i, i ^ k) for i in range(momenta)]
        got.append(lax.ppermute(block, "mom", pairs))
    crossed = pl.pallas_call(
        cross_body(partners, momenta, group),
        out_shape=jax.ShapeDtypeStruct((columns, rows), BF),
        in_specs=[VMEM] * (1 + momenta),
        out_specs=ANY,
        scratch_shapes=[
            pltpu.VMEM((per_device // group, momenta * group, rows), BF),
            pltpu.VMEM((columns, rows), BF),
            pltpu.SemaphoreType.DMA((per_device // group,)),
        ],
        compiler_params=LIMIT,
    )(*[pltpu.with_memory_space_constraint(a, pltpu.VMEM) for a in (pick, *got)])
    return crossed.reshape(per_device, momenta, rows)


def solution(mesh):
    in_specs = (
        P("mom", "row", "col"),
        P("mom", "row", "col"),
        P("mom", None),
        P(("col", "mom"), None),
    )
    out_specs = P(("col", "mom"), None, "row")
    return jax.shard_map(
        on_device, mesh=mesh, in_specs=in_specs, out_specs=out_specs, check_vma=False
    )
```

time: 80.1 us -> 70.6 us (0.88)
  waiting for transfers between devices: 58.1 us -> 39.7 us
  Pallas kernels: 0 us -> 11 us
  matrix products: 10.3 us -> 0 us
  starting transfers between devices: 9.38 us -> 18.4 us
    all_to_all x1 -> x0, waiting for transfers between devices: 28.7 us -> none  [on_device(): lax.all_to_all(summed, 'mom', split_axis=0, concat_axis=0, tiled=True)]
    ppermute x0 -> x7, waiting for transfers between devices: none -> 16.9 us  [on_device(): got.append(lax.ppermute(block, 'mom', pairs))]
    ppermute x0 -> x7, starting transfers between devices: none -> 13.1 us  [on_device(): got.append(lax.ppermute(block, 'mom', pairs))]
    pallas_call x0 -> x12, Pallas kernels: none -> 11 us  [the longest x9 7.49 us: local(): pl.pallas_call(body, out_shape=outs, in_specs=[VMEM] * len(arrays), out_s...]
    dot_general x5 -> x0, matrix products: 10.3 us -> none  [the longest x4 8.11 us: nt(): lax.dot_general(x, y, (((1,), (1,)), ((), ())), preferred_element_type=jn...]
    ppermute x3 -> x7, waiting for transfers between devices: 29.4 us -> 22.8 us  [swap(): return lax.ppermute(value, axis, [(0, 1), (1, 0)])]
    all_to_all x1 -> x0, starting transfers between devices: 6.16 us -> none  [on_device(): lax.all_to_all(summed, 'mom', split_axis=0, concat_axis=0, tiled=True)]
    ppermute x3 -> x7, starting transfers between devices: 3.22 us -> 5.24 us  [swap(): return lax.ppermute(value, axis, [(0, 1), (1, 0)])]
  transfers between devices with their start and end apart: 4 -> 14, of which waited for: 3 -> 9; matrix products, arithmetic and copies ran while one was open for 0% -> 0% of each run, Pallas kernels for 0% -> 12%
where the time goes in v2:
time: 70.6 us; the launch traced here: 70.4 us
  waiting for transfers between devices  39.7 us (56%)
  starting transfers between devices  18.4 us (26%)
  Pallas kernels  11 us (16%)
  local copies, waits for them, and re-layouts  1.28 us (2%)
    ppermute x7, waiting for transfers between devices, swap(): return lax.ppermute(value, axis, [(0, 1), (1, 0)])  22.8 us
    ppermute x7, waiting for transfers between devices, on_device(): got.append(lax.ppermute(block, 'mom', pairs))  16.9 us
    ppermute x7, starting transfers between devices, on_device(): got.append(lax.ppermute(block, 'mom', pairs))  13.1 us
    pallas_call x9, Pallas kernels, local(): pl.pallas_call(body, out_shape=outs, in_specs=[VMEM] * len(arrays), out_s...  7.49 us
    ppermute x7, starting transfers between devices, swap(): return lax.ppermute(value, axis, [(0, 1), (1, 0)])  5.24 us
    pallas_call x2, Pallas kernels, fetch(): pl.pallas_call(body, out_shape=[pltpu.VMEM((e - s, array.shape[1]), array...  2.13 us
  transfers between devices with their start and end apart: 14, of which 9 were waited for; matrix products, arithmetic and copies ran while one was open for 0% of the time, Pallas kernels for 12%

profile of v2, /device:TPU:0, one launch (start us, length us, event | category | flops | bytes accessed | tf_op | source)
XLA Modules:
  0.0 70.4 jit_solution(14376537010521312202)
XLA Ops:
  0.0 1.3 %copy-done.1 = bf16[1,768,768]{2,1,0:T(8,128)(2,1)S(1)} copy-done((bf16[1,768,768]{2,1,0:T(8,128)(2,1)S(1)}, bf16[1,768,768]{2,1,0:T(8,128)(2,1)}, u32[]{:S(2)}) %copy-start.1) | copy-done | bytes 1179672
  1.6 0.6 collective-permute-start.1
  2.2 1.1 %shard_map.50 = bf16[384,768]{1,0:T(8,128)(2,1)S(1)} custom-call(bf16[768,768]{1,0:T(8,128)(2,1)} %bitcast.4), custom_call_target="tpu_custom_call" | custom-call | tf_op jit(solution)/shard_map/pallas_call | solution.py:55
  3.3 2.6 %collective-permute-start.3 = (bf16[384,768]{1,0:T(8,128)(2,1)S(1)}, bf16[384,768]{1,0:T(8,128)(2,1)S(1)}, u32[]{:S(2)}, u32[]{:S(2)}) collective-permute-start(bf16[384,768]{1,0:T(8,128)(2,1)S(1)} %shard_map.50), channel_id=1, source_target_pairs={{0,1},{1,0},{2,3},{3,2},{4,5},{5,4},{6,7},{7,6},{8,9},{9,8},{10,11... | collective-permute-start | bytes 1769480 | tf_op jit(solution)/shard_map/ppermute | solution.py:17
  5.9 1.1 %shard_map.47 = (bf16[256,768]{1,0:T(8,128)(2,1)S(1)}, bf16[128,768]{1,0:T(8,128)(2,1)S(1)}) custom-call(bf16[768,768]{1,0:T(8,128)(2,1)} %bitcast.5), custom_call_target="tpu_custom_call" | custom-call | tf_op jit(solution)/shard_map/pallas_call | solution.py:55
  7.0 1.4 %shard_map.49 = (bf16[2,768,768]{2,1,0:T(8,128)(2,1)S(1)}, f32[768,768]{1,0:T(8,128)S(1)}, bf16[768,768]{1,0:T(8,128)(2,1)S(1)}) custom-call(bf16[768,768]{1,0:T(8,128)(2,1)S(1)} %bitcast.6, f32[1,1536]{1,0:T(1,128)S(1)} %copy-done.2, bf16[768,768]{1,0:T(8,128)(2,1)S(1)} %shard_map.48.flipped, bf16[768,768]{1,0:T(8,128)(2,1)S(1)} %collective-permute-done.1.flipped_far), custom_call_target="tpu_custom_call" | custom-call | flops 905969664 | bytes 1048576 | tf_op jit(solution)/shard_map/pallas_call | solution.py:29
  8.4 11.6 %collective-permute-done.3.far = bf16[384,768]{1,0:T(8,128)(2,1)S(1)} collective-permute-done((bf16[384,768]{1,0:T(8,128)(2,1)S(1)}, bf16[384,768]{1,0:T(8,128)(2,1)S(1)}, u32[]{:S(2)}, u32[]{:S(2)}) %collective-permute-start.3) | collective-permute-done | bytes 589856 | tf_op jit(solution)/shard_map/ppermute | solution.py:17
  20.0 0.8 %shard_map.51 = (bf16[2,768,768]{2,1,0:T(8,128)(2,1)S(1)}, f32[768,768]{1,0:T(8,128)S(1)}, bf16[768,384]{1,0:T(8,128)(2,1)S(1)}) custom-call(bf16[384,768]{1,0:T(8,128)(2,1)S(1)} %collective-permute-done.3.far, f32[1,1536]{1,0:T(1,128)S(1)} %copy-done.2, bf16[768,768]{1,0:T(8,128)(2,1)S(1)} %get-tuple-element.28.other, ...), custom_call_target="tpu_custom_call", output_to_operand_aliasing={{0}: (3, {}), {1}: (4, {})} | custom-call | flops 452984832 | bytes 1048576 | tf_op jit(solution)/shard_map/pallas_call | solution.py:29
  20.9 7.3 %collective-permute-done.2.far = bf16[256,768]{1,0:T(8,128)(2,1)S(1)} collective-permute-done((bf16[256,768]{1,0:T(8,128)(2,1)S(1)}, bf16[256,768]{1,0:T(8,128)(2,1)S(1)}, u32[]{:S(2)}, u32[]{:S(2)}) %collective-permute-start.2) | collective-permute-done | bytes 393248 | tf_op jit(solution)/shard_map/ppermute | solution.py:17
  28.9 1.8 %collective-permute-start = (bf16[128,768]{1,0:T(8,128)(2,1)S(1)}, bf16[128,768]{1,0:T(8,128)(2,1)S(1)}, u32[]{:S(2)}, u32[]{:S(2)}) collective-permute-start(bf16[128,768]{1,0:T(8,128)(2,1)S(1)} %get-tuple-element.27), channel_id=1, source_target_pairs={{0,1},{1,0},{2,3},{3,2},{4,5},{5,4},{6,7},{7,6},{8,9},{9,8},{10,11... | collective-permute-start | bytes 589832 | tf_op jit(solution)/shard_map/ppermute | solution.py:17
  30.7 2.0 %shard_map.54.early = f32[768,640]{1,0:T(8,128)S(1)} custom-call(bf16[2,768,768]{2,1,0:T(8,128)(2,1)S(1)} %get-tuple-element.34._.halves, bf16[768,384]{1,0:T(8,128)(2,1)S(1)} %get-tuple-element.38.own0, bf16[768,256]{1,0:T(8,128)(2,1)S(1)} %get-tuple-element.39.own1, bf16[768,384]{1,0:T(8,128)(2,1)S(1)} %collective-permute-done.5.far0, ...), custom_call_target="tpu_custom_call" | custom-call | flops 1509949440 | bytes 1048576 | tf_op jit(solution)/shard_map/pallas_call | solution.py:29
  32.6 3.5 %collective-permute-done.far = bf16[128,768]{1,0:T(8,128)(2,1)S(1)} collective-permute-done((bf16[128,768]{1,0:T(8,128)(2,1)S(1)}, bf16[128,768]{1,0:T(8,128)(2,1)S(1)}, u32[]{:S(2)}, u32[]{:S(2)}) %collective-permute-start) | collective-permute-done | bytes 196640 | tf_op jit(solution)/shard_map/ppermute | solution.py:17
  36.7 1.1 %shard_map.55.late = f32[768,768]{1,0:T(8,128)S(1)} custom-call(bf16[2,768,768]{2,1,0:T(8,128)(2,1)S(1)} %get-tuple-element.36.halves, bf16[768,384]{1,0:T(8,128)(2,1)S(1)} %get-tuple-element.38.own0, bf16[768,256]{1,0:T(8,128)(2,1)S(1)} %get-tuple-element.39.own1, bf16[768,128]{1,0:T(8,128)(2,1)S(1)} %get-tuple-element.37.own2, ...), custom_call_target="tpu_custom_call" | custom-call | flops 452984832 | bytes 1048576 | tf_op jit(solution)/shard_map/pallas_call | solution.py:29
  38.7 4.8 %collective-permute-start.10 = (bf16[96,768]{1,0:T(8,128)(2,1)S(1)}, bf16[96,768]{1,0:T(8,128)(2,1)S(1)}, u32[]{:S(2)}, u32[]{:S(2)}) collective-permute-start(bf16[96,768]{1,0:T(8,128)(2,1)S(1)} %get-tuple-element.45), channel_id=1, source_target_pairs={{0,28},{4,24},{8,20},{12,16},{16,12},{20,8},{24,4},{28,0},{1,29},{... | collective-permute-start | bytes 442376 | tf_op jit(solution)/shard_map/ppermute | solution.py:315
  43.5 2.0 %collective-permute-start.12 = (bf16[96,768]{1,0:T(8,128)(2,1)S(1)}, bf16[96,768]{1,0:T(8,128)(2,1)S(1)}, u32[]{:S(2)}, u32[]{:S(2)}) collective-permute-start(bf16[96,768]{1,0:T(8,128)(2,1)S(1)} %get-tuple-element.47), channel_id=1, source_target_pairs={{0,12},{4,8},{8,4},{12,0},{16,28},{20,24},{24,20},{28,16},{1,13},{... | collective-permute-start | bytes 442376 | tf_op jit(solution)/shard_map/ppermute | solution.py:315
  45.5 1.5 %collective-permute-start.13 = (bf16[96,768]{1,0:T(8,128)(2,1)S(1)}, bf16[96,768]{1,0:T(8,128)(2,1)S(1)}, u32[]{:S(2)}, u32[]{:S(2)}) collective-permute-start(bf16[96,768]{1,0:T(8,128)(2,1)S(1)} %get-tuple-element.48), channel_id=1, source_target_pairs={{0,4},{4,0},{8,12},{12,8},{16,20},{20,16},{24,28},{28,24},{1,5},{5... | collective-permute-start | bytes 442376 | tf_op jit(solution)/shard_map/ppermute | solution.py:315
  47.0 1.3 %collective-permute-done.10.refs_4_ = bf16[96,768]{1,0:T(8,128)(2,1)S(1)} collective-permute-done((bf16[96,768]{1,0:T(8,128)(2,1)S(1)}, bf16[96,768]{1,0:T(8,128)(2,1)S(1)}, u32[]{:S(2)}, u32[]{:S(2)}) %collective-permute-start.10) | collective-permute-done | bytes 147488 | tf_op jit(solution)/shard_map/ppermute | solution.py:315
  48.3 3.8 %collective-permute-start.8 = (bf16[96,768]{1,0:T(8,128)(2,1)S(1)}, bf16[96,768]{1,0:T(8,128)(2,1)S(1)}, u32[]{:S(2)}, u32[]{:S(2)}) collective-permute-start(bf16[96,768]{1,0:T(8,128)(2,1)S(1)} %get-tuple-element.43), channel_id=1, source_target_pairs={{0,24},{4,28},{8,16},{12,20},{16,8},{20,12},{24,0},{28,4},{1,25},{... | collective-permute-start | bytes 442376 | tf_op jit(solution)/shard_map/ppermute | solution.py:315
  52.1 1.5 %collective-permute-done.11.refs_5_ = bf16[96,768]{1,0:T(8,128)(2,1)S(1)} collective-permute-done((bf16[96,768]{1,0:T(8,128)(2,1)S(1)}, bf16[96,768]{1,0:T(8,128)(2,1)S(1)}, u32[]{:S(2)}, u32[]{:S(2)}) %collective-permute-start.11) | collective-permute-done | bytes 147488 | tf_op jit(solution)/shard_map/ppermute | solution.py:315
  53.6 1.0 %collective-permute-start.9 = (bf16[96,768]{1,0:T(8,128)(2,1)S(1)}, bf16[96,768]{1,0:T(8,128)(2,1)S(1)}, u32[]{:S(2)}, u32[]{:S(2)}) collective-permute-start(bf16[96,768]{1,0:T(8,128)(2,1)S(1)} %get-tuple-element.44), channel_id=1, source_target_pairs={{0,20},{4,16},{8,28},{12,24},{16,4},{20,0},{24,12},{28,8},{1,21},{... | collective-permute-start | bytes 442376 | tf_op jit(solution)/shard_map/ppermute | solution.py:315
  55.0 2.7 %collective-permute-done.12.refs_6_ = bf16[96,768]{1,0:T(8,128)(2,1)S(1)} collective-permute-done((bf16[96,768]{1,0:T(8,128)(2,1)S(1)}, bf16[96,768]{1,0:T(8,128)(2,1)S(1)}, u32[]{:S(2)}, u32[]{:S(2)}) %collective-permute-start.12) | collective-permute-done | bytes 147488 | tf_op jit(solution)/shard_map/ppermute | solution.py:315
  57.7 6.5 %collective-permute-done.7.refs_1_ = bf16[96,768]{1,0:T(8,128)(2,1)S(1)} collective-permute-done((bf16[96,768]{1,0:T(8,128)(2,1)S(1)}, bf16[96,768]{1,0:T(8,128)(2,1)S(1)}, u32[]{:S(2)}, u32[]{:S(2)}) %collective-permute-start.7) | collective-permute-done | bytes 147488 | tf_op jit(solution)/shard_map/ppermute | solution.py:315
  64.2 4.9 %collective-permute-done.9.refs_3_ = bf16[96,768]{1,0:T(8,128)(2,1)S(1)} collective-permute-done((bf16[96,768]{1,0:T(8,128)(2,1)S(1)}, bf16[96,768]{1,0:T(8,128)(2,1)S(1)}, u32[]{:S(2)}, u32[]{:S(2)}) %collective-permute-start.9) | collective-permute-done | bytes 147488 | tf_op jit(solution)/shard_map/ppermute | solution.py:315
  69.1 1.4 %shard_map.57 = bf16[768,768]{1,0:T(8,128)(2,1)} custom-call(bf16[768,256]{1,0:T(8,128)(2,1)S(1)} %shard_map.46.pick, bf16[96,768]{1,0:T(8,128)(2,1)S(1)} %get-tuple-element.41.refs_0_, bf16[96,768]{1,0:T(8,128)(2,1)S(1)} %collective-permute-done.7.refs_1_, bf16[96,768]{1,0:T(8,128)(2,1)S(1)} %collective-permute-done.8.refs_2_, ...), custom_call_target="tpu_custom_call" | custom-call | tf_op jit(solution)/shard_map/pallas_call | solution.py:316
  (24 shorter events, 2.9 us)
Async XLA Ops:
  0.0 1.3 %copy-start.1 = (bf16[1,768,768]{2,1,0:T(8,128)(2,1)S(1)}, bf16[1,768,768]{2,1,0:T(8,128)(2,1)}, u32[]{:S(2)}) copy-start(bf16[1,768,768]{2,1,0:T(8,128)(2,1)} %param.5) | copy-start | bytes 3538948
  1.3 5.7 %copy-start = (bf16[1,768,768]{2,1,0:T(8,128)(2,1)S(1)}, bf16[1,768,768]{2,1,0:T(8,128)(2,1)}, u32[]{:S(2)}) copy-start(bf16[1,768,768]{2,1,0:T(8,128)(2,1)} %param.4) | copy-start | bytes 3538948
  1.3 5.8 %copy-start.2 = (f32[1,1536]{1,0:T(1,128)S(1)}, f32[1,1536]{1,0:T(1,128)}, u32[]{:S(2)}) copy-start(f32[1,1536]{1,0:T(1,128)} %bubble.7) | copy-start | bytes 18436
  1.6 5.4 %collective-permute-start.1 = (bf16[768,768]{1,0:T(8,128)(2,1)S(1)}, bf16[768,768]{1,0:T(8,128)(2,1)S(1)}, u32[]{:S(2)}, u32[]{:S(2)}) collective-permute-start(bf16[768,768]{1,0:T(8,128)(2,1)S(1)} %shard_map.48.flipped), channel_id=1, source_target_pairs={{0,2},{2,0},{1,3},{3,1},{4,6},{6,4},{5,7},{7,5},{8,10},{10,8},{9,1... | collective-permute-start | bytes 3538952 | tf_op jit(solution)/shard_map/ppermute | solution.py:17
  3.3 16.8 %collective-permute-start.3 = (bf16[384,768]{1,0:T(8,128)(2,1)S(1)}, bf16[384,768]{1,0:T(8,128)(2,1)S(1)}, u32[]{:S(2)}, u32[]{:S(2)}) collective-permute-start(bf16[384,768]{1,0:T(8,128)(2,1)S(1)} %shard_map.50), channel_id=1, source_target_pairs={{0,1},{1,0},{2,3},{3,2},{4,5},{5,4},{6,7},{7,6},{8,9},{9,8},{10,11... | collective-permute-start | bytes 1769480 | tf_op jit(solution)/shard_map/ppermute | solution.py:17
  6.9 21.3 %collective-permute-start.2 = (bf16[256,768]{1,0:T(8,128)(2,1)S(1)}, bf16[256,768]{1,0:T(8,128)(2,1)S(1)}, u32[]{:S(2)}, u32[]{:S(2)}) collective-permute-start(bf16[256,768]{1,0:T(8,128)(2,1)S(1)} %get-tuple-element.29), channel_id=1, source_target_pairs={{0,1},{1,0},{2,3},{3,2},{4,5},{5,4},{6,7},{7,6},{8,9},{9,8},{10,11... | collective-permute-start | bytes 1179656 | tf_op jit(solution)/shard_map/ppermute | solution.py:17
  20.9 9.8 %collective-permute-start.5 = (bf16[768,384]{1,0:T(8,128)(2,1)S(1)}, bf16[768,384]{1,0:T(8,128)(2,1)S(1)}, u32[]{:S(2)}, u32[]{:S(2)}) collective-permute-start(bf16[768,384]{1,0:T(8,128)(2,1)S(1)} %get-tuple-element.38.own0), channel_id=1, source_target_pairs={{0,2},{2,0},{1,3},{3,1},{4,6},{6,4},{5,7},{7,5},{8,10},{10,8},{9,1... | collective-permute-start | bytes 1769480 | tf_op jit(solution)/shard_map/ppermute | solution.py:17
  28.8 1.9 %collective-permute-start.6 = (bf16[768,256]{1,0:T(8,128)(2,1)S(1)}, bf16[768,256]{1,0:T(8,128)(2,1)S(1)}, u32[]{:S(2)}, u32[]{:S(2)}) collective-permute-start(bf16[768,256]{1,0:T(8,128)(2,1)S(1)} %get-tuple-element.39.own1), channel_id=1, source_target_pairs={{0,2},{2,0},{1,3},{3,1},{4,6},{6,4},{5,7},{7,5},{8,10},{10,8},{9,1... | collective-permute-start | bytes 1179656 | tf_op jit(solution)/shard_map/ppermute | solution.py:17
  28.9 7.3 %collective-permute-start = (bf16[128,768]{1,0:T(8,128)(2,1)S(1)}, bf16[128,768]{1,0:T(8,128)(2,1)S(1)}, u32[]{:S(2)}, u32[]{:S(2)}) collective-permute-start(bf16[128,768]{1,0:T(8,128)(2,1)S(1)} %get-tuple-element.27), channel_id=1, source_target_pairs={{0,1},{1,0},{2,3},{3,2},{4,5},{5,4},{6,7},{7,6},{8,9},{9,8},{10,11... | collective-permute-start | bytes 589832 | tf_op jit(solution)/shard_map/ppermute | solution.py:17
  36.7 1.5 %collective-permute-start.4 = (bf16[768,128]{1,0:T(8,128)(2,1)S(1)}, bf16[768,128]{1,0:T(8,128)(2,1)S(1)}, u32[]{:S(2)}, u32[]{:S(2)}) collective-permute-start(bf16[768,128]{1,0:T(8,128)(2,1)S(1)} %get-tuple-element.37.own2), channel_id=1, source_target_pairs={{0,2},{2,0},{1,3},{3,1},{4,6},{6,4},{5,7},{7,5},{8,10},{10,8},{9,1... | collective-permute-start | bytes 589832 | tf_op jit(solution)/shard_map/ppermute | solution.py:17
  37.8 16.8 %copy-start.3 = (s32[96,8]{0,1:T(8,128)S(1)}, s32[96,8]{0,1:T(8,128)}, u32[]{:S(2)}) copy-start(s32[96,8]{0,1:T(8,128)} %param.7) | copy-start | bytes 9220
  38.7 9.6 %collective-permute-start.10 = (bf16[96,768]{1,0:T(8,128)(2,1)S(1)}, bf16[96,768]{1,0:T(8,128)(2,1)S(1)}, u32[]{:S(2)}, u32[]{:S(2)}) collective-permute-start(bf16[96,768]{1,0:T(8,128)(2,1)S(1)} %get-tuple-element.45), channel_id=1, source_target_pairs={{0,28},{4,24},{8,20},{12,16},{16,12},{20,8},{24,4},{28,0},{1,29},{... | collective-permute-start | bytes 442376 | tf_op jit(solution)/shard_map/ppermute | solution.py:315
  43.5 10.0 %collective-permute-start.11 = (bf16[96,768]{1,0:T(8,128)(2,1)S(1)}, bf16[96,768]{1,0:T(8,128)(2,1)S(1)}, u32[]{:S(2)}, u32[]{:S(2)}) collective-permute-start(bf16[96,768]{1,0:T(8,128)(2,1)S(1)} %get-tuple-element.46), channel_id=1, source_target_pairs={{0,8},{4,12},{8,0},{12,4},{16,24},{20,28},{24,16},{28,20},{1,9},{5... | collective-permute-start | bytes 442376 | tf_op jit(solution)/shard_map/ppermute | solution.py:315
  43.5 14.1 %collective-permute-start.12 = (bf16[96,768]{1,0:T(8,128)(2,1)S(1)}, bf16[96,768]{1,0:T(8,128)(2,1)S(1)}, u32[]{:S(2)}, u32[]{:S(2)}) collective-permute-start(bf16[96,768]{1,0:T(8,128)(2,1)S(1)} %get-tuple-element.47), channel_id=1, source_target_pairs={{0,12},{4,8},{8,4},{12,0},{16,28},{20,24},{24,20},{28,16},{1,13},{... | collective-permute-start | bytes 442376 | tf_op jit(solution)/shard_map/ppermute | solution.py:315
  45.5 12.1 %collective-permute-start.13 = (bf16[96,768]{1,0:T(8,128)(2,1)S(1)}, bf16[96,768]{1,0:T(8,128)(2,1)S(1)}, u32[]{:S(2)}, u32[]{:S(2)}) collective-permute-start(bf16[96,768]{1,0:T(8,128)(2,1)S(1)} %get-tuple-element.48), channel_id=1, source_target_pairs={{0,4},{4,0},{8,12},{12,8},{16,20},{20,16},{24,28},{28,24},{1,5},{5... | collective-permute-start | bytes 442376 | tf_op jit(solution)/shard_map/ppermute | solution.py:315
  47.0 17.1 %collective-permute-start.7 = (bf16[96,768]{1,0:T(8,128)(2,1)S(1)}, bf16[96,768]{1,0:T(8,128)(2,1)S(1)}, u32[]{:S(2)}, u32[]{:S(2)}) collective-permute-start(bf16[96,768]{1,0:T(8,128)(2,1)S(1)} %get-tuple-element.42), channel_id=1, source_target_pairs={{0,16},{4,20},{8,24},{12,28},{16,0},{20,4},{24,8},{28,12},{1,17},{... | collective-permute-start | bytes 442376 | tf_op jit(solution)/shard_map/ppermute | solution.py:315
  48.3 15.9 %collective-permute-start.8 = (bf16[96,768]{1,0:T(8,128)(2,1)S(1)}, bf16[96,768]{1,0:T(8,128)(2,1)S(1)}, u32[]{:S(2)}, u32[]{:S(2)}) collective-permute-start(bf16[96,768]{1,0:T(8,128)(2,1)S(1)} %get-tuple-element.43), channel_id=1, source_target_pairs={{0,24},{4,28},{8,16},{12,20},{16,8},{20,12},{24,0},{28,4},{1,25},{... | collective-permute-start | bytes 442376 | tf_op jit(solution)/shard_map/ppermute | solution.py:315
  53.6 15.5 %collective-permute-start.9 = (bf16[96,768]{1,0:T(8,128)(2,1)S(1)}, bf16[96,768]{1,0:T(8,128)(2,1)S(1)}, u32[]{:S(2)}, u32[]{:S(2)}) collective-permute-start(bf16[96,768]{1,0:T(8,128)(2,1)S(1)} %get-tuple-element.44), channel_id=1, source_target_pairs={{0,20},{4,16},{8,28},{12,24},{16,4},{20,0},{24,12},{28,8},{1,21},{... | collective-permute-start | bytes 442376 | tf_op jit(solution)/shard_map/ppermute | solution.py:315

commit v3 on v2

--- a/solution.py
+++ b/solution.py
@@ -54,9 +54,7 @@
 
     return pl.pallas_call(
         body,
-        out_shape=[
-            pltpu.VMEM((e - s, array.shape[1]), array.dtype) for s, e in spans
-        ],
+        out_shape=[pltpu.VMEM((e - s, array.shape[1]), array.dtype) for s, e in spans],
         in_specs=[HBM],
         out_specs=[VMEM] * len(spans),
         scratch_shapes=[pltpu.SemaphoreType.DMA((len(spans),))],
@@ -86,14 +84,34 @@
         other[...] = flipped[...]
 
 
-def chunk_body(start, stop):
-    def body(far, bubble, other, _, __, halves, first, rounded):
+def team(mom):
+    return ((mom >> 1) ^ (mom >> 2)) & 1
+
+
+def gated(turn, body):
+    def run(*refs):
+        @pl.when(team(lax.axis_index("mom")) == turn)
+        def _():
+            body(*refs)
+
+    return body if turn is None else run
+
+
+def chunk_body(start, stop, count):
+    def body(*refs):
+        fars, (bubble, other, _, __, halves, first, rounded) = (
+            refs[:count],
+            refs[count:],
+        )
         col = 1 - lax.axis_index("col")
-        half = far.shape[1]
+        half = fars[0].shape[1]
         scale = bubble[:, pl.ds(pl.multiple_of(col * half, half), half)]
-        scaled = (far[...].astype(F32) * scale).astype(BF)
-        halves[col, start:stop, :] = scaled
-        total = first[:, start:stop] + nt(other[...], scaled)
+        begin = start
+        for far in fars:
+            end = begin + far.shape[0]
+            halves[col, begin:end, :] = (far[...].astype(F32) * scale).astype(BF)
+            begin = end
+        total = first[:, start:stop] + nt(other[...], halves[col, start:stop, :])
         first[:, start:stop] = total
         rounded[...] = total.astype(BF)
 
@@ -143,24 +161,33 @@
         ).astype(BF)
         size = outs[0].shape[0]
         for out, partner in zip(outs, partners):
-            begin = (mom ^ partner) * size if len(outs) > 1 else 0
-            out[...] = done[pl.ds(pl.multiple_of(begin, size), size), :]
-
-    return body
-
-
-def cross_body(partners, momenta, group):
+            begin = pl.multiple_of((mom ^ partner) * size, size)
+            out[...] = done[pl.ds(begin, size), :]
+
+    return body
+
+
+def cross_body(partners, group):
+    momenta = len(partners)
+
     def body(pick, *refs):
-        blocks, (out, gathered, result, sem) = refs[:-4], refs[-4:]
+        turns = refs[:momenta], refs[momenta : 2 * momenta]
+        out, gathered, result, sem = refs[2 * momenta :]
         mom = lax.axis_index("mom")
-        per = blocks[0].shape[0]
-        copies = []
-        for i in range(per // group):
+        groups = out.shape[0] // (momenta * group)
+        for turn, blocks in enumerate(turns):
             for block, partner in zip(blocks, partners):
                 begin = pl.multiple_of((mom ^ partner) * group, group)
-                gathered[i, pl.ds(begin, group), :] = block[
-                    i * group : (i + 1) * group, :
-                ]
+
+                @pl.when(team(mom ^ partner) == turn)
+                def _():
+                    for i in range(groups):
+                        gathered[i, pl.ds(begin, group), :] = block[
+                            i * group : (i + 1) * group, :
+                        ]
+
+        copies = []
+        for i in range(groups):
             size = group * momenta
             span = slice(i * size, (i + 1) * size)
             result[span, :] = jnp.dot(
@@ -203,22 +230,86 @@
     return body
 
 
-def on_device(left_part, vertex, bubble, cross_map):
+def plain(left_part, vertex, bubble, cross_map):
+    momenta = lax.axis_size("mom")
+    col = lax.axis_index("col")
+    same = lax.axis_index("row") == col
+    left, flipped = left_part[0], vertex[0].T
+    half = left.shape[1]
+    columns = flipped.shape[0]
+    per_device = columns // momenta
+
+    left_far, flipped_far = swap(left, "col"), swap(flipped, "row")
+    scale = bubble.reshape(2, half)
+    near_scale = lax.dynamic_index_in_dim(scale, col, 0, keepdims=True)
+    far_scale = lax.dynamic_index_in_dim(scale, 1 - col, 0, keepdims=True)
+    near = (left.astype(F32) * near_scale).astype(BF)
+    far = (left_far.astype(F32) * far_scale).astype(BF)
+    first = nt(jnp.where(same, flipped, flipped_far), near)
+    first = first + nt(jnp.where(same, flipped_far, flipped), far)
+    rounded = first.astype(BF)
+    rounded_far = swap(rounded, "row")
+    second = nt(jnp.where(same, rounded, rounded_far), near)
+    second = second + nt(jnp.where(same, rounded_far, rounded), far)
+    summed = (flipped.astype(F32) + first + second).astype(BF)
+
+    summed = summed.reshape(momenta, per_device, -1)
+    received = lax.all_to_all(summed, "mom", split_axis=0, concat_axis=0, tiled=True)
+    column = jnp.arange(per_device, dtype=jnp.int32)[:, None]
+    source = (cross_map * per_device + column).reshape(-1, 1)
+    pick = source == jnp.arange(columns, dtype=jnp.int32)[None, :]
+    crossed = jnp.dot(
+        pick.astype(BF), received.reshape(columns, -1), preferred_element_type=F32
+    )
+    return crossed.astype(BF).reshape(per_device, momenta, -1)
+
+
+def staggered(left_part, vertex, bubble, cross_map):
     momenta = lax.axis_size("mom")
     left, vert = left_part[0], vertex[0]
     rows, half = left.shape
     columns = vert.shape[1]
     per_device = columns // momenta
+    square = 2 * columns * half
     cuts = (rows // 2, rows // 2 + rows // 3, rows)
-    square = 2 * columns * half
-    starts = (0,) + cuts[:-1]
-    spans = list(zip(starts, cuts))
-
-    pieces = fetch(left, spans[:1])
-    pieces += fetch(left, spans[1:])
-    fars = []
-    for piece in pieces:
-        fars.append(swap(piece, "col"))
+    spans = list(zip((0,) + cuts[:-1], cuts))
+    relay = cuts[0] + rows // 4
+    teams = [[m for m in range(momenta) if team(m) == t] for t in (0, 1)]
+    everyone = list(range(momenta))
+
+    def send(value, axes, members, place):
+        pairs = [
+            (m * 2 + i, place(m, i)[0] * 2 + place(m, i)[1])
+            for m in members
+            for i in range(2)
+        ]
+        return lax.ppermute(value, ("mom", axes), pairs)
+
+    def across(m, i):
+        return m, 1 - i
+
+    head, detour = fetch(left, [spans[0], (cuts[0], relay)])
+    short, tail, wide = fetch(left, [(relay, cuts[1]), spans[2], spans[1]])
+    head = send(head, "col", everyone, across)
+    detour = send(detour, "col", teams[0], lambda m, i: (m ^ 2, 1 - i))
+    arrivals = [
+        [
+            None,
+            send(short, "col", teams[0], across),
+            send(tail, "col", teams[0], across),
+        ],
+        [
+            None,
+            send(wide, "col", teams[1], across),
+            send(tail, "col", teams[1], across),
+        ],
+    ]
+    detour = send(detour, "col", teams[1], lambda m, i: (m ^ 2, i))
+    arrivals = [
+        [None, [detour, arrivals[0][1]], [arrivals[0][2]]],
+        [None, [arrivals[1][1]], [arrivals[1][2]]],
+    ]
+
     flipped = local(flip_body, pltpu.VMEM((columns, rows), BF), vert)
     flipped_far = swap(flipped, "row")
     halves, first, other = local(
@@ -234,89 +325,79 @@
         flipped_far,
         flops=square * rows,
     )
-    direct = per_device % 16 == 0 and momenta & (momenta - 1) == 0
-    group = 16 * (2 - per_device // 16 % 2) if direct else per_device
+    group = 16 * (2 - per_device // 16 % 2)
     pick = local(
-        pick_body(group),
-        pltpu.VMEM((columns, momenta * group), BF),
-        cross_map.T,
+        pick_body(group), pltpu.VMEM((columns, momenta * group), BF), cross_map.T
     )
-    own, others = [], []
-
-    def arrive(i, halves, first):
+
+    def arrive(i, turn, fars, halves, first):
         s, e = spans[i]
         halves, first, rounded = local(
-            chunk_body(s, e),
+            gated(turn, chunk_body(s, e, len(fars))),
             [
                 pltpu.VMEM((2, rows, half), BF),
                 pltpu.VMEM((columns, rows), F32),
                 pltpu.VMEM((columns, e - s), BF),
             ],
-            fars[i],
+            *fars,
             bubble,
             other,
             halves,
             first,
-            aliases={3: 0, 4: 1},
+            aliases={len(fars) + 2: 0, len(fars) + 3: 1},
             flops=square * (e - s),
         )
-        own.append(rounded)
-        others.append(swap(rounded, "row"))
-        return halves, first
-
-    halves, first = arrive(0, halves, first)
-    halves, first = arrive(1, halves, first)
-    early = local(
-        early_body(cuts),
-        pltpu.VMEM((columns, cuts[1]), F32),
-        halves,
-        *own,
-        *others,
-        flops=square * 2 * cuts[1],
-    )
-    halves, first = arrive(2, halves, first)
-    late = local(
-        late_body(cuts),
-        pltpu.VMEM((columns, rows), F32),
-        halves,
-        *own,
-        *others[:2],
-        early,
-        flipped,
-        first,
-        flops=square * (rows - cuts[1]) * 3,
-    )
-    partners = xor_partners(momenta) if direct else [0]
-    size = per_device if direct else columns
-    sent = local(
-        last_body(cuts, partners),
-        [pltpu.VMEM((size, rows), BF)] * len(partners),
-        halves,
-        others[2],
-        late,
-        scratch=[pltpu.VMEM((columns, rows), BF)],
-    )
-    if not direct:
-        received = lax.all_to_all(
-            sent[0].reshape(momenta, per_device, rows),
-            "mom",
-            split_axis=0,
-            concat_axis=0,
-            tiled=True,
-        )
-        crossed = jnp.dot(
-            pick, received.reshape(columns, rows), preferred_element_type=F32
-        )
-        return crossed.astype(BF).reshape(per_device, momenta, rows)
-
-    got = [sent[0]]
-    for block, k in zip(sent[1:], partners[1:]):
-        pairs = [(i, i ^ k) for i in range(momenta)]
-        got.append(lax.ppermute(block, "mom", pairs))
+        members = everyone if turn is None else teams[turn]
+        return halves, first, rounded, send(rounded, "row", members, across)
+
+    halves, first, own0, far0 = arrive(0, None, [head], halves, first)
+    partners = xor_partners(momenta)
+    received = []
+    for turn in (0, 1):
+        own, others = [own0], [far0]
+        for i in (1, 2):
+            halves, first, mine, theirs = arrive(
+                i, turn, arrivals[turn][i], halves, first
+            )
+            own.append(mine)
+            others.append(theirs)
+            if i == 1:
+                early = local(
+                    gated(turn, early_body(cuts)),
+                    pltpu.VMEM((columns, cuts[1]), F32),
+                    halves,
+                    *own,
+                    *others,
+                    flops=square * 2 * cuts[1],
+                )
+        late = local(
+            gated(turn, late_body(cuts)),
+            pltpu.VMEM((columns, rows), F32),
+            halves,
+            *own,
+            *others[:2],
+            early,
+            flipped,
+            first,
+            flops=square * (rows - cuts[1]) * 3,
+        )
+        sent = local(
+            gated(turn, last_body(cuts, partners)),
+            [pltpu.VMEM((per_device, rows), BF)] * momenta,
+            halves,
+            others[2],
+            late,
+            scratch=[pltpu.VMEM((columns, rows), BF)],
+        )
+        received.append(sent[0])
+        for block, k in zip(sent[1:], partners[1:]):
+            pairs = [(m, m ^ k) for m in teams[turn]]
+            received.append(lax.ppermute(block, "mom", pairs))
+    arrays = [pick, *received]
     crossed = pl.pallas_call(
-        cross_body(partners, momenta, group),
+        cross_body(partners, group),
         out_shape=jax.ShapeDtypeStruct((columns, rows), BF),
-        in_specs=[VMEM] * (1 + momenta),
+        in_specs=[VMEM] * len(arrays),
         out_specs=ANY,
         scratch_shapes=[
             pltpu.VMEM((per_device // group, momenta * group, rows), BF),
@@ -324,7 +405,7 @@
             pltpu.SemaphoreType.DMA((per_device // group,)),
         ],
         compiler_params=LIMIT,
-    )(*[pltpu.with_memory_space_constraint(a, pltpu.VMEM) for a in (pick, *got)])
+    )(*[pltpu.with_memory_space_constraint(a, pltpu.VMEM) for a in arrays])
     return crossed.reshape(per_device, momenta, rows)
 
 
@@ -336,6 +417,18 @@
         P(("col", "mom"), None),
     )
     out_specs = P(("col", "mom"), None, "row")
-    return jax.shard_map(
-        on_device, mesh=mesh, in_specs=in_specs, out_specs=out_specs, check_vma=False
-    )
+
+    def step(body):
+        return jax.shard_map(
+            body, mesh=mesh, in_specs=in_specs, out_specs=out_specs, check_vma=False
+        )
+
+    momenta = mesh.shape["mom"]
+
+    def run(left_part, *rest):
+        per_device = left_part.shape[1] // momenta
+        if per_device % 16 or momenta & (momenta - 1) or momenta < 4:
+            return step(plain)(left_part, *rest)
+        return step(staggered)(left_part, *rest)
+
+    return run

time: 70.6 us -> 100 us (1.42)
  starting transfers between devices: 18.4 us -> 56.3 us
  waiting for transfers between devices: 39.7 us -> 30.1 us
    ppermute x7 -> x26, starting transfers between devices: 13.1 us -> 55.8 us  [the longest x14 34.6 us: staggered(): received.append(lax.ppermute(block, 'mom', pairs))]
    ppermute x7 -> x1, waiting for transfers between devices: 22.8 us -> 0.01 us  [swap(): return lax.ppermute(value, axis, [(0, 1), (1, 0)])]
    ppermute x7 -> x26, waiting for transfers between devices: 16.9 us -> 30.1 us  [the longest x14 15.6 us: staggered(): received.append(lax.ppermute(block, 'mom', pairs))]
    ppermute x7 -> x1, starting transfers between devices: 5.24 us -> 0.56 us  [swap(): return lax.ppermute(value, axis, [(0, 1), (1, 0)])]
    pallas_call x9 -> x14, Pallas kernels: 7.49 us -> 7.53 us  [local(): pl.pallas_call(body, out_shape=outs, in_specs=[VMEM] * len(arrays), out_s...]
  transfers between devices with their start and end apart: 14 -> 27, of which waited for: 9 -> 12; matrix products, arithmetic and copies ran while one was open for 0% -> 0% of each run, Pallas kernels for 12% -> 10%
where the time goes in v3:
time: 100 us; the launch traced here: 99.6 us
  starting transfers between devices  56.3 us (56%)
  waiting for transfers between devices  30.1 us (30%)
  Pallas kernels  11.4 us (11%)
  local copies, waits for them, and re-layouts  1.38 us (1%)
    ppermute x14, starting transfers between devices, staggered(): received.append(lax.ppermute(block, 'mom', pairs))  34.6 us
    ppermute x12, starting transfers between devices, send(): return lax.ppermute(value, ('mom', axes), pairs)  21.2 us
    ppermute x14, waiting for transfers between devices, staggered(): received.append(lax.ppermute(block, 'mom', pairs))  15.6 us
    ppermute x12, waiting for transfers between devices, send(): return lax.ppermute(value, ('mom', axes), pairs)  14.5 us
    pallas_call x14, Pallas kernels, local(): pl.pallas_call(body, out_shape=outs, in_specs=[VMEM] * len(arrays), out_s...  7.53 us
    pallas_call x2, Pallas kernels, fetch(): pl.pallas_call(body, out_shape=[pltpu.VMEM((e - s, array.shape[1]), array...  2.33 us
  transfers between devices with their start and end apart: 27, of which 12 were waited for; matrix products, arithmetic and copies ran while one was open for 0% of the time, Pallas kernels for 10%

profile of v3, /device:TPU:0, one launch (start us, length us, event | category | flops | bytes accessed | tf_op | source)
XLA Modules:
  0.0 99.6 jit_solution(8469215061975062929)
XLA Ops:
  0.0 1.4 %copy-done.1 = bf16[1,768,768]{2,1,0:T(8,128)(2,1)S(1)} copy-done((bf16[1,768,768]{2,1,0:T(8,128)(2,1)S(1)}, bf16[1,768,768]{2,1,0:T(8,128)(2,1)}, u32[]{:S(2)}) %copy-start.1) | copy-done | bytes 1179672
  3.5 2.6 %collective-permute-start.5 = (bf16[384,768]{1,0:T(8,128)(2,1)S(1)}, bf16[384,768]{1,0:T(8,128)(2,1)S(1)}, u32[]{:S(2)}, u32[]{:S(2)}) collective-permute-start(bf16[384,768]{1,0:T(8,128)(2,1)S(1)} %get-tuple-element.48), channel_id=1, source_target_pairs={{0,1},{1,0},{4,5},{5,4},{8,9},{9,8},{12,13},{13,12},{16,17},{17,16... | collective-permute-start | bytes 1769480 | tf_op jit(solution)/shard_map/ppermute | solution.py:286
  6.0 3.4 %collective-permute-start.2 = (bf16[192,768]{1,0:T(8,128)(2,1)S(1)}, bf16[192,768]{1,0:T(8,128)(2,1)S(1)}, u32[]{:S(2)}, u32[]{:S(2)}) collective-permute-start(bf16[192,768]{1,0:T(8,128)(2,1)S(1)} %get-tuple-element.46), channel_id=1, source_target_pairs={{0,9},{1,8},{4,13},{5,12},{24,17},{25,16},{28,21},{29,20},{2,11},{... | collective-permute-start | bytes 884744 | tf_op jit(solution)/shard_map/ppermute | solution.py:286
  9.5 6.7 %collective-permute-done.2 = bf16[192,768]{1,0:T(8,128)(2,1)S(1)} collective-permute-done((bf16[192,768]{1,0:T(8,128)(2,1)S(1)}, bf16[192,768]{1,0:T(8,128)(2,1)S(1)}, u32[]{:S(2)}, u32[]{:S(2)}) %collective-permute-start.2) | collective-permute-done | bytes 294944 | tf_op jit(solution)/shard_map/ppermute | solution.py:286
  17.4 1.4 %shard_map.49 = (bf16[2,768,768]{2,1,0:T(8,128)(2,1)S(1)}, f32[768,768]{1,0:T(8,128)S(1)}, bf16[768,768]{1,0:T(8,128)(2,1)S(1)}) custom-call(bf16[768,768]{1,0:T(8,128)(2,1)S(1)} %bitcast.6, f32[1,1536]{1,0:T(1,128)S(1)} %copy-done.2, bf16[768,768]{1,0:T(8,128)(2,1)S(1)} %shard_map.48.flipped.refs_7_, bf16[768,768]{1,0:T(8,128)(2,1)S(1)} %collective-permute-done.1.flipped_far), custom_call_target="tpu_custom_call" | custom-call | flops 905969664 | bytes 1048576 | tf_op jit(solution)/shard_map/pallas_call | solution.py:29
  22.1 3.6 %collective-permute-start.4 = (bf16[64,768]{1,0:T(8,128)(2,1)S(1)}, bf16[64,768]{1,0:T(8,128)(2,1)S(1)}, u32[]{:S(2)}, u32[]{:S(2)}) collective-permute-start(bf16[64,768]{1,0:T(8,128)(2,1)S(1)} %get-tuple-element.47), channel_id=1, source_target_pairs={{0,1},{1,0},{4,5},{5,4},{24,25},{25,24},{28,29},{29,28},{2,3},{3,2... | collective-permute-start | bytes 294920 | tf_op jit(solution)/shard_map/ppermute | solution.py:286
  25.8 3.4 %collective-permute-done.4.refs_1_ = bf16[64,768]{1,0:T(8,128)(2,1)S(1)} collective-permute-done((bf16[64,768]{1,0:T(8,128)(2,1)S(1)}, bf16[64,768]{1,0:T(8,128)(2,1)S(1)}, u32[]{:S(2)}, u32[]{:S(2)}) %collective-permute-start.4) | collective-permute-done | bytes 98336 | tf_op jit(solution)/shard_map/ppermute | solution.py:286
  29.7 1.9 %collective-permute-start.8 = (bf16[768,256]{1,0:T(8,128)(2,1)S(1)}, bf16[768,256]{1,0:T(8,128)(2,1)S(1)}, u32[]{:S(2)}, u32[]{:S(2)}) collective-permute-start(bf16[768,256]{1,0:T(8,128)(2,1)S(1)} %get-tuple-element.58.refs_2_), channel_id=1, source_target_pairs={{0,2},{2,0},{4,6},{6,4},{24,26},{26,24},{28,30},{30,28},{1,3},{3,1... | collective-permute-start | bytes 1179656 | tf_op jit(solution)/shard_map/ppermute | solution.py:286
  31.7 3.6 %collective-permute-start = (bf16[128,768]{1,0:T(8,128)(2,1)S(1)}, bf16[128,768]{1,0:T(8,128)(2,1)S(1)}, u32[]{:S(2)}, u32[]{:S(2)}) collective-permute-start(bf16[128,768]{1,0:T(8,128)(2,1)S(1)} %get-tuple-element.44), channel_id=1, source_target_pairs={{0,1},{1,0},{4,5},{5,4},{24,25},{25,24},{28,29},{29,28},{2,3},{3,2... | collective-permute-start | bytes 589832 | tf_op jit(solution)/shard_map/ppermute | solution.py:286
  36.0 2.0 %shard_map.54.refs_6_ = f32[768,640]{1,0:T(8,128)S(1)} custom-call(bf16[2,768,768]{2,1,0:T(8,128)(2,1)S(1)} %get-tuple-element.53.refs_3_.refs_0_, bf16[768,384]{1,0:T(8,128)(2,1)S(1)} %get-tuple-element.57.refs_1_, bf16[768,256]{1,0:T(8,128)(2,1)S(1)} %get-tuple-element.58.refs_2_, bf16[768,384]{1,0:T(8,128)(2,1)S(1)} %collective-permute-done.7.refs_3_.refs_4_, ...), custom_call_target="tpu_custom_call" | custom-call | flops 1509949440 | bytes 1048576 | tf_op jit(solution)/shard_map/pallas_call | solution.py:29
  38.0 2.9 %collective-permute-done.refs_0_ = bf16[128,768]{1,0:T(8,128)(2,1)S(1)} collective-permute-done((bf16[128,768]{1,0:T(8,128)(2,1)S(1)}, bf16[128,768]{1,0:T(8,128)(2,1)S(1)}, u32[]{:S(2)}, u32[]{:S(2)}) %collective-permute-start) | collective-permute-done | bytes 196640 | tf_op jit(solution)/shard_map/ppermute | solution.py:286
  41.3 1.9 %collective-permute-start.6 = (bf16[768,128]{1,0:T(8,128)(2,1)S(1)}, bf16[768,128]{1,0:T(8,128)(2,1)S(1)}, u32[]{:S(2)}, u32[]{:S(2)}) collective-permute-start(bf16[768,128]{1,0:T(8,128)(2,1)S(1)} %get-tuple-element.56.refs_3_), channel_id=1, source_target_pairs={{0,2},{2,0},{4,6},{6,4},{24,26},{26,24},{28,30},{30,28},{1,3},{3,1... | collective-permute-start | bytes 589832 | tf_op jit(solution)/shard_map/ppermute | solution.py:286
  47.4 5.7 %collective-permute-start.10 = (bf16[96,768]{1,0:T(8,128)(2,1)S(1)}, bf16[96,768]{1,0:T(8,128)(2,1)S(1)}, u32[]{:S(2)}, u32[]{:S(2)}) collective-permute-start(bf16[96,768]{1,0:T(8,128)(2,1)S(1)} %get-tuple-element.62), channel_id=1, source_target_pairs={{0,24},{4,28},{24,0},{28,4},{1,25},{5,29},{25,1},{29,5},{2,26},{6,... | collective-permute-start | bytes 442376 | tf_op jit(solution)/shard_map/ppermute | solution.py:395
  53.1 11.2 %collective-permute-start.11 = (bf16[96,768]{1,0:T(8,128)(2,1)S(1)}, bf16[96,768]{1,0:T(8,128)(2,1)S(1)}, u32[]{:S(2)}, u32[]{:S(2)}) collective-permute-start(bf16[96,768]{1,0:T(8,128)(2,1)S(1)} %get-tuple-element.63), channel_id=1, source_target_pairs={{0,20},{4,16},{24,12},{28,8},{1,21},{5,17},{25,13},{29,9},{2,22},{... | collective-permute-start | bytes 442376 | tf_op jit(solution)/shard_map/ppermute | solution.py:395
  64.3 3.2 %collective-permute-start.12 = (bf16[96,768]{1,0:T(8,128)(2,1)S(1)}, bf16[96,768]{1,0:T(8,128)(2,1)S(1)}, u32[]{:S(2)}, u32[]{:S(2)}) collective-permute-start(bf16[96,768]{1,0:T(8,128)(2,1)S(1)} %get-tuple-element.64), channel_id=1, source_target_pairs={{0,28},{4,24},{24,4},{28,0},{1,29},{5,25},{25,5},{29,1},{2,30},{6,... | collective-permute-start | bytes 442376 | tf_op jit(solution)/shard_map/ppermute | solution.py:395
  67.6 1.3 %collective-permute-start.13 = (bf16[96,768]{1,0:T(8,128)(2,1)S(1)}, bf16[96,768]{1,0:T(8,128)(2,1)S(1)}, u32[]{:S(2)}, u32[]{:S(2)}) collective-permute-start(bf16[96,768]{1,0:T(8,128)(2,1)S(1)} %get-tuple-element.65), channel_id=1, source_target_pairs={{0,8},{4,12},{24,16},{28,20},{1,9},{5,13},{25,17},{29,21},{2,10},{... | collective-permute-start | bytes 442376 | tf_op jit(solution)/shard_map/ppermute | solution.py:395
  68.9 1.3 %collective-permute-start.14 = (bf16[96,768]{1,0:T(8,128)(2,1)S(1)}, bf16[96,768]{1,0:T(8,128)(2,1)S(1)}, u32[]{:S(2)}, u32[]{:S(2)}) collective-permute-start(bf16[96,768]{1,0:T(8,128)(2,1)S(1)} %get-tuple-element.66), channel_id=1, source_target_pairs={{0,12},{4,8},{24,20},{28,16},{1,13},{5,9},{25,21},{29,17},{2,14},{... | collective-permute-start | bytes 442376 | tf_op jit(solution)/shard_map/ppermute | solution.py:395
  70.3 3.4 %collective-permute-start.15 = (bf16[96,768]{1,0:T(8,128)(2,1)S(1)}, bf16[96,768]{1,0:T(8,128)(2,1)S(1)}, u32[]{:S(2)}, u32[]{:S(2)}) collective-permute-start(bf16[96,768]{1,0:T(8,128)(2,1)S(1)} %get-tuple-element.67), channel_id=1, source_target_pairs={{0,4},{4,0},{24,28},{28,24},{1,5},{5,1},{25,29},{29,25},{2,6},{6,2... | collective-permute-start | bytes 442376 | tf_op jit(solution)/shard_map/ppermute | solution.py:395
  73.7 1.3 %collective-permute-start.9 = (bf16[96,768]{1,0:T(8,128)(2,1)S(1)}, bf16[96,768]{1,0:T(8,128)(2,1)S(1)}, u32[]{:S(2)}, u32[]{:S(2)}) collective-permute-start(bf16[96,768]{1,0:T(8,128)(2,1)S(1)} %get-tuple-element.61), channel_id=1, source_target_pairs={{0,16},{4,20},{24,8},{28,12},{1,17},{5,21},{25,9},{29,13},{2,18},{... | collective-permute-start | bytes 442376 | tf_op jit(solution)/shard_map/ppermute | solution.py:395
  82.0 4.7 %collective-permute-done.20.refs_9_ = bf16[96,768]{1,0:T(8,128)(2,1)S(1)} collective-permute-done((bf16[96,768]{1,0:T(8,128)(2,1)S(1)}, bf16[96,768]{1,0:T(8,128)(2,1)S(1)}, u32[]{:S(2)}, u32[]{:S(2)}) %collective-permute-start.20) | collective-permute-done | bytes 147488 | tf_op jit(solution)/shard_map/ppermute | solution.py:395
  89.0 4.8 %collective-permute-done.22.refs_11_ = bf16[96,768]{1,0:T(8,128)(2,1)S(1)} collective-permute-done((bf16[96,768]{1,0:T(8,128)(2,1)S(1)}, bf16[96,768]{1,0:T(8,128)(2,1)S(1)}, u32[]{:S(2)}, u32[]{:S(2)}) %collective-permute-start.22) | collective-permute-done | bytes 147488 | tf_op jit(solution)/shard_map/ppermute | solution.py:395
  93.8 1.8 %collective-permute-done.24.refs_13_ = bf16[96,768]{1,0:T(8,128)(2,1)S(1)} collective-permute-done((bf16[96,768]{1,0:T(8,128)(2,1)S(1)}, bf16[96,768]{1,0:T(8,128)(2,1)S(1)}, u32[]{:S(2)}, u32[]{:S(2)}) %collective-permute-start.24) | collective-permute-done | bytes 147488 | tf_op jit(solution)/shard_map/ppermute | solution.py:395
  95.7 2.5 %collective-permute-done.25.refs_14_ = bf16[96,768]{1,0:T(8,128)(2,1)S(1)} collective-permute-done((bf16[96,768]{1,0:T(8,128)(2,1)S(1)}, bf16[96,768]{1,0:T(8,128)(2,1)S(1)}, u32[]{:S(2)}, u32[]{:S(2)}) %collective-permute-start.25) | collective-permute-done | bytes 147488 | tf_op jit(solution)/shard_map/ppermute | solution.py:395
  98.1 1.5 %shard_map.62 = bf16[768,768]{1,0:T(8,128)(2,1)} custom-call(bf16[768,256]{1,0:T(8,128)(2,1)S(1)} %shard_map.46.pick, bf16[96,768]{1,0:T(8,128)(2,1)S(1)} %get-tuple-element.60.refs_0_, bf16[96,768]{1,0:T(8,128)(2,1)S(1)} %collective-permute-done.9.refs_1_, bf16[96,768]{1,0:T(8,128)(2,1)S(1)} %collective-permute-done.10.refs_2_, ...), custom_call_target="tpu_custom_call" | custom-call | tf_op jit(solution)/shard_map/pallas_call | solution.py:397
  (55 shorter events, 21.7 us)
Async XLA Ops:
  1.7 15.7 %collective-permute-start.1 = (bf16[768,768]{1,0:T(8,128)(2,1)S(1)}, bf16[768,768]{1,0:T(8,128)(2,1)S(1)}, u32[]{:S(2)}, u32[]{:S(2)}) collective-permute-start(bf16[768,768]{1,0:T(8,128)(2,1)S(1)} %shard_map.48.flipped.refs_7_), channel_id=1, source_target_pairs={{0,2},{2,0},{1,3},{3,1},{4,6},{6,4},{5,7},{7,5},{8,10},{10,8},{9,1... | collective-permute-start | bytes 3538952 | tf_op jit(solution)/shard_map/ppermute | solution.py:17
  3.5 16.6 %collective-permute-start.5 = (bf16[384,768]{1,0:T(8,128)(2,1)S(1)}, bf16[384,768]{1,0:T(8,128)(2,1)S(1)}, u32[]{:S(2)}, u32[]{:S(2)}) collective-permute-start(bf16[384,768]{1,0:T(8,128)(2,1)S(1)} %get-tuple-element.48), channel_id=1, source_target_pairs={{0,1},{1,0},{4,5},{5,4},{8,9},{9,8},{12,13},{13,12},{16,17},{17,16... | collective-permute-start | bytes 1769480 | tf_op jit(solution)/shard_map/ppermute | solution.py:286
  6.0 10.1 %collective-permute-start.2 = (bf16[192,768]{1,0:T(8,128)(2,1)S(1)}, bf16[192,768]{1,0:T(8,128)(2,1)S(1)}, u32[]{:S(2)}, u32[]{:S(2)}) collective-permute-start(bf16[192,768]{1,0:T(8,128)(2,1)S(1)} %get-tuple-element.46), channel_id=1, source_target_pairs={{0,9},{1,8},{4,13},{5,12},{24,17},{25,16},{28,21},{29,20},{2,11},{... | collective-permute-start | bytes 884744 | tf_op jit(solution)/shard_map/ppermute | solution.py:286
  16.1 13.1 %collective-permute-start.3 = (bf16[192,768]{1,0:T(8,128)(2,1)S(1)}, bf16[192,768]{1,0:T(8,128)(2,1)S(1)}, u32[]{:S(2)}, u32[]{:S(2)}) collective-permute-start(bf16[192,768]{1,0:T(8,128)(2,1)S(1)} %collective-permute-done.2), channel_id=1, source_target_pairs={{8,0},{9,1},{12,4},{13,5},{16,24},{17,25},{20,28},{21,29},{10,2},{... | collective-permute-start | bytes 884744 | tf_op jit(solution)/shard_map/ppermute | solution.py:286
  20.8 15.2 %collective-permute-start.7 = (bf16[768,384]{1,0:T(8,128)(2,1)S(1)}, bf16[768,384]{1,0:T(8,128)(2,1)S(1)}, u32[]{:S(2)}, u32[]{:S(2)}) collective-permute-start(bf16[768,384]{1,0:T(8,128)(2,1)S(1)} %get-tuple-element.57.refs_1_), channel_id=1, source_target_pairs={{0,2},{2,0},{4,6},{6,4},{8,10},{10,8},{12,14},{14,12},{16,18},{18,... | collective-permute-start | bytes 1769480 | tf_op jit(solution)/shard_map/ppermute | solution.py:286
  22.1 7.1 %collective-permute-start.4 = (bf16[64,768]{1,0:T(8,128)(2,1)S(1)}, bf16[64,768]{1,0:T(8,128)(2,1)S(1)}, u32[]{:S(2)}, u32[]{:S(2)}) collective-permute-start(bf16[64,768]{1,0:T(8,128)(2,1)S(1)} %get-tuple-element.47), channel_id=1, source_target_pairs={{0,1},{1,0},{4,5},{5,4},{24,25},{25,24},{28,29},{29,28},{2,3},{3,2... | collective-permute-start | bytes 294920 | tf_op jit(solution)/shard_map/ppermute | solution.py:286
  29.7 6.3 %collective-permute-start.8 = (bf16[768,256]{1,0:T(8,128)(2,1)S(1)}, bf16[768,256]{1,0:T(8,128)(2,1)S(1)}, u32[]{:S(2)}, u32[]{:S(2)}) collective-permute-start(bf16[768,256]{1,0:T(8,128)(2,1)S(1)} %get-tuple-element.58.refs_2_), channel_id=1, source_target_pairs={{0,2},{2,0},{4,6},{6,4},{24,26},{26,24},{28,30},{30,28},{1,3},{3,1... | collective-permute-start | bytes 1179656 | tf_op jit(solution)/shard_map/ppermute | solution.py:286
  31.7 9.2 %collective-permute-start = (bf16[128,768]{1,0:T(8,128)(2,1)S(1)}, bf16[128,768]{1,0:T(8,128)(2,1)S(1)}, u32[]{:S(2)}, u32[]{:S(2)}) collective-permute-start(bf16[128,768]{1,0:T(8,128)(2,1)S(1)} %get-tuple-element.44), channel_id=1, source_target_pairs={{0,1},{1,0},{4,5},{5,4},{24,25},{25,24},{28,29},{29,28},{2,3},{3,2... | collective-permute-start | bytes 589832 | tf_op jit(solution)/shard_map/ppermute | solution.py:286
  35.3 9.9 %collective-permute-start.17 = (bf16[256,768]{1,0:T(8,128)(2,1)S(1)}, bf16[256,768]{1,0:T(8,128)(2,1)S(1)}, u32[]{:S(2)}, u32[]{:S(2)}) collective-permute-start(bf16[256,768]{1,0:T(8,128)(2,1)S(1)} %get-tuple-element.68), channel_id=1, source_target_pairs={{8,9},{9,8},{12,13},{13,12},{16,17},{17,16},{20,21},{21,20},{10,11... | collective-permute-start | bytes 1179656 | tf_op jit(solution)/shard_map/ppermute | solution.py:286
  46.7 22.2 %collective-permute-start.18 = (bf16[768,128]{1,0:T(8,128)(2,1)S(1)}, bf16[768,128]{1,0:T(8,128)(2,1)S(1)}, u32[]{:S(2)}, u32[]{:S(2)}) collective-permute-start(bf16[768,128]{1,0:T(8,128)(2,1)S(1)} %get-tuple-element.72.refs_3_), channel_id=1, source_target_pairs={{8,10},{10,8},{12,14},{14,12},{16,18},{18,16},{20,22},{22,20},{9,1... | collective-permute-start | bytes 589832 | tf_op jit(solution)/shard_map/ppermute | solution.py:286
  47.4 22.9 %collective-permute-start.10 = (bf16[96,768]{1,0:T(8,128)(2,1)S(1)}, bf16[96,768]{1,0:T(8,128)(2,1)S(1)}, u32[]{:S(2)}, u32[]{:S(2)}) collective-permute-start(bf16[96,768]{1,0:T(8,128)(2,1)S(1)} %get-tuple-element.62), channel_id=1, source_target_pairs={{0,24},{4,28},{24,0},{28,4},{1,25},{5,29},{25,1},{29,5},{2,26},{6,... | collective-permute-start | bytes 442376 | tf_op jit(solution)/shard_map/ppermute | solution.py:395
  53.1 20.5 %collective-permute-start.11 = (bf16[96,768]{1,0:T(8,128)(2,1)S(1)}, bf16[96,768]{1,0:T(8,128)(2,1)S(1)}, u32[]{:S(2)}, u32[]{:S(2)}) collective-permute-start(bf16[96,768]{1,0:T(8,128)(2,1)S(1)} %get-tuple-element.63), channel_id=1, source_target_pairs={{0,20},{4,16},{24,12},{28,8},{1,21},{5,17},{25,13},{29,9},{2,22},{... | collective-permute-start | bytes 442376 | tf_op jit(solution)/shard_map/ppermute | solution.py:395
  64.3 11.3 %collective-permute-start.12 = (bf16[96,768]{1,0:T(8,128)(2,1)S(1)}, bf16[96,768]{1,0:T(8,128)(2,1)S(1)}, u32[]{:S(2)}, u32[]{:S(2)}) collective-permute-start(bf16[96,768]{1,0:T(8,128)(2,1)S(1)} %get-tuple-element.64), channel_id=1, source_target_pairs={{0,28},{4,24},{24,4},{28,0},{1,29},{5,25},{25,5},{29,1},{2,30},{6,... | collective-permute-start | bytes 442376 | tf_op jit(solution)/shard_map/ppermute | solution.py:395
  67.6 9.4 %collective-permute-start.13 = (bf16[96,768]{1,0:T(8,128)(2,1)S(1)}, bf16[96,768]{1,0:T(8,128)(2,1)S(1)}, u32[]{:S(2)}, u32[]{:S(2)}) collective-permute-start(bf16[96,768]{1,0:T(8,128)(2,1)S(1)} %get-tuple-element.65), channel_id=1, source_target_pairs={{0,8},{4,12},{24,16},{28,20},{1,9},{5,13},{25,17},{29,21},{2,10},{... | collective-permute-start | bytes 442376 | tf_op jit(solution)/shard_map/ppermute | solution.py:395
  68.9 9.2 %collective-permute-start.14 = (bf16[96,768]{1,0:T(8,128)(2,1)S(1)}, bf16[96,768]{1,0:T(8,128)(2,1)S(1)}, u32[]{:S(2)}, u32[]{:S(2)}) collective-permute-start(bf16[96,768]{1,0:T(8,128)(2,1)S(1)} %get-tuple-element.66), channel_id=1, source_target_pairs={{0,12},{4,8},{24,20},{28,16},{1,13},{5,9},{25,21},{29,17},{2,14},{... | collective-permute-start | bytes 442376 | tf_op jit(solution)/shard_map/ppermute | solution.py:395
  70.3 9.1 %collective-permute-start.15 = (bf16[96,768]{1,0:T(8,128)(2,1)S(1)}, bf16[96,768]{1,0:T(8,128)(2,1)S(1)}, u32[]{:S(2)}, u32[]{:S(2)}) collective-permute-start(bf16[96,768]{1,0:T(8,128)(2,1)S(1)} %get-tuple-element.67), channel_id=1, source_target_pairs={{0,4},{4,0},{24,28},{28,24},{1,5},{5,1},{25,29},{29,25},{2,6},{6,2... | collective-permute-start | bytes 442376 | tf_op jit(solution)/shard_map/ppermute | solution.py:395
  73.7 7.1 %collective-permute-start.9 = (bf16[96,768]{1,0:T(8,128)(2,1)S(1)}, bf16[96,768]{1,0:T(8,128)(2,1)S(1)}, u32[]{:S(2)}, u32[]{:S(2)}) collective-permute-start(bf16[96,768]{1,0:T(8,128)(2,1)S(1)} %get-tuple-element.61), channel_id=1, source_target_pairs={{0,16},{4,20},{24,8},{28,12},{1,17},{5,21},{25,9},{29,13},{2,18},{... | collective-permute-start | bytes 442376 | tf_op jit(solution)/shard_map/ppermute | solution.py:395
  75.6 11.1 %collective-permute-start.20 = (bf16[96,768]{1,0:T(8,128)(2,1)S(1)}, bf16[96,768]{1,0:T(8,128)(2,1)S(1)}, u32[]{:S(2)}, u32[]{:S(2)}) collective-permute-start(bf16[96,768]{1,0:T(8,128)(2,1)S(1)} %get-tuple-element.76), channel_id=1, source_target_pairs={{8,24},{12,28},{16,0},{20,4},{9,25},{13,29},{17,1},{21,5},{10,26},... | collective-permute-start | bytes 442376 | tf_op jit(solution)/shard_map/ppermute | solution.py:395
  76.9 11.0 %collective-permute-start.21 = (bf16[96,768]{1,0:T(8,128)(2,1)S(1)}, bf16[96,768]{1,0:T(8,128)(2,1)S(1)}, u32[]{:S(2)}, u32[]{:S(2)}) collective-permute-start(bf16[96,768]{1,0:T(8,128)(2,1)S(1)} %get-tuple-element.77), channel_id=1, source_target_pairs={{8,16},{12,20},{16,8},{20,12},{9,17},{13,21},{17,9},{21,13},{10,18... | collective-permute-start | bytes 442376 | tf_op jit(solution)/shard_map/ppermute | solution.py:395
  78.1 15.7 %collective-permute-start.22 = (bf16[96,768]{1,0:T(8,128)(2,1)S(1)}, bf16[96,768]{1,0:T(8,128)(2,1)S(1)}, u32[]{:S(2)}, u32[]{:S(2)}) collective-permute-start(bf16[96,768]{1,0:T(8,128)(2,1)S(1)} %get-tuple-element.78), channel_id=1, source_target_pairs={{8,28},{12,24},{16,4},{20,0},{9,29},{13,25},{17,5},{21,1},{10,30},... | collective-permute-start | bytes 442376 | tf_op jit(solution)/shard_map/ppermute | solution.py:395
  79.4 14.4 %collective-permute-start.23 = (bf16[96,768]{1,0:T(8,128)(2,1)S(1)}, bf16[96,768]{1,0:T(8,128)(2,1)S(1)}, u32[]{:S(2)}, u32[]{:S(2)}) collective-permute-start(bf16[96,768]{1,0:T(8,128)(2,1)S(1)} %get-tuple-element.79), channel_id=1, source_target_pairs={{8,20},{12,16},{16,12},{20,8},{9,21},{13,17},{17,13},{21,9},{10,22... | collective-permute-start | bytes 442376 | tf_op jit(solution)/shard_map/ppermute | solution.py:395
  80.7 14.9 %collective-permute-start.24 = (bf16[96,768]{1,0:T(8,128)(2,1)S(1)}, bf16[96,768]{1,0:T(8,128)(2,1)S(1)}, u32[]{:S(2)}, u32[]{:S(2)}) collective-permute-start(bf16[96,768]{1,0:T(8,128)(2,1)S(1)} %get-tuple-element.80), channel_id=1, source_target_pairs={{8,0},{12,4},{16,24},{20,28},{9,1},{13,5},{17,25},{21,29},{10,2},{... | collective-permute-start | bytes 442376 | tf_op jit(solution)/shard_map/ppermute | solution.py:395
  86.7 11.4 %collective-permute-start.25 = (bf16[96,768]{1,0:T(8,128)(2,1)S(1)}, bf16[96,768]{1,0:T(8,128)(2,1)S(1)}, u32[]{:S(2)}, u32[]{:S(2)}) collective-permute-start(bf16[96,768]{1,0:T(8,128)(2,1)S(1)} %get-tuple-element.81), channel_id=1, source_target_pairs={{8,4},{12,0},{16,28},{20,24},{9,5},{13,1},{17,29},{21,25},{10,6},{... | collective-permute-start | bytes 442376 | tf_op jit(solution)/shard_map/ppermute | solution.py:395
  88.0 10.1 %collective-permute-start.26 = (bf16[96,768]{1,0:T(8,128)(2,1)S(1)}, bf16[96,768]{1,0:T(8,128)(2,1)S(1)}, u32[]{:S(2)}, u32[]{:S(2)}) collective-permute-start(bf16[96,768]{1,0:T(8,128)(2,1)S(1)} %get-tuple-element.82), channel_id=1, source_target_pairs={{8,12},{12,8},{16,20},{20,16},{9,13},{13,9},{17,21},{21,17},{10,14... | collective-permute-start | bytes 442376 | tf_op jit(solution)/shard_map/ppermute | solution.py:395
  (7 other events, 60.1 us)

commit v4 on v2

--- a/solution.py
+++ b/solution.py
@@ -54,9 +54,7 @@
 
     return pl.pallas_call(
         body,
-        out_shape=[
-            pltpu.VMEM((e - s, array.shape[1]), array.dtype) for s, e in spans
-        ],
+        out_shape=[pltpu.VMEM((e - s, array.shape[1]), array.dtype) for s, e in spans],
         in_specs=[HBM],
         out_specs=[VMEM] * len(spans),
         scratch_shapes=[pltpu.SemaphoreType.DMA((len(spans),))],
@@ -100,68 +98,57 @@
     return body
 
 
-def early_body(cuts):
-    def body(halves, own0, own1, far0, far1, out):
+def add_body(spans, i, final):
+    def body(*refs):
         row = lax.axis_index("row")
-        a, b, _ = cuts
-        total = nt(own0[...], halves[row, :b, :a])
-        total += nt(far0[...], halves[1 - row, :b, :a])
-        total += nt(own1[...], halves[row, :b, a:b])
-        total += nt(far1[...], halves[1 - row, :b, a:b])
-        out[...] = total
-
-    return body
-
-
-def late_body(cuts):
-    def body(halves, own0, own1, own2, far0, far1, early, flipped, first, out):
-        row = lax.axis_index("row")
-        a, b, c = cuts
-        out[:, :b] = (
-            early[...]
-            + nt(own2[...], halves[row, :b, b:c])
-            + (flipped[:, :b].astype(F32) + first[:, :b])
-        )
-        total = flipped[:, b:].astype(F32) + first[:, b:]
-        total += nt(own0[...], halves[row, b:, :a])
-        total += nt(own1[...], halves[row, b:, a:b])
-        total += nt(own2[...], halves[row, b:, b:c])
-        total += nt(far0[...], halves[1 - row, b:, :a])
-        total += nt(far1[...], halves[1 - row, b:, a:b])
-        out[:, b:] = total
-
-    return body
-
-
-def last_body(cuts, partners):
-    def body(halves, far2, late, *refs):
+        count = i + 1
+        own, refs = refs[:count], refs[count:]
+        far, refs = refs[: count - final], refs[count - final :]
+        halves, flipped, first, total = refs[0], refs[1], refs[2], refs[-1]
+        start, stop = spans[i]
+        for s, e in [(0, start)] if start else []:
+            part = total[:, s:e] + nt(own[i][...], halves[row, s:e, start:stop])
+            if not final:
+                part += nt(far[i][...], halves[1 - row, s:e, start:stop])
+            total[:, s:e] = part
+        part = flipped[:, start:stop].astype(F32) + first[:, start:stop]
+        for half, terms in ((row, own), (1 - row, far)):
+            for term, (s, e) in zip(terms, spans):
+                part += nt(term[...], halves[half, start:stop, s:e])
+        total[:, start:stop] = part
+
+    return body
+
+
+def last_body(span, partners):
+    def body(halves, far, total, *outs):
         row, mom = lax.axis_index("row"), lax.axis_index("mom")
-        _, b, c = cuts
-        outs, done = refs[:-1], refs[-1]
-        done[...] = (
-            late[...] + nt(far2[...], halves[1 - row, :, b:c])
-        ).astype(BF)
+        s, e = span
         size = outs[0].shape[0]
+        weights = halves[1 - row, :, s:e]
         for out, partner in zip(outs, partners):
-            begin = (mom ^ partner) * size if len(outs) > 1 else 0
-            out[...] = done[pl.ds(pl.multiple_of(begin, size), size), :]
-
-    return body
-
-
-def cross_body(partners, momenta, group):
+            begin = pl.multiple_of((mom ^ partner) * size, size)
+            lines = pl.ds(begin, size)
+            out[...] = (total[lines, :] + nt(far[lines, :], weights)).astype(BF)
+
+    return body
+
+
+def cross_body(partners, group):
+    momenta = len(partners)
+
     def body(pick, *refs):
-        blocks, (out, gathered, result, sem) = refs[:-4], refs[-4:]
+        blocks, (out, gathered, result, sem) = refs[:momenta], refs[momenta:]
         mom = lax.axis_index("mom")
-        per = blocks[0].shape[0]
+        groups = out.shape[0] // (momenta * group)
+        size = group * momenta
         copies = []
-        for i in range(per // group):
+        for i in range(groups):
             for block, partner in zip(blocks, partners):
                 begin = pl.multiple_of((mom ^ partner) * group, group)
                 gathered[i, pl.ds(begin, group), :] = block[
                     i * group : (i + 1) * group, :
                 ]
-            size = group * momenta
             span = slice(i * size, (i + 1) * size)
             result[span, :] = jnp.dot(
                 pick[span, :], gathered[i], preferred_element_type=F32
@@ -203,16 +190,50 @@
     return body
 
 
-def on_device(left_part, vertex, bubble, cross_map):
+def plain(left_part, vertex, bubble, cross_map):
+    momenta = lax.axis_size("mom")
+    col = lax.axis_index("col")
+    same = lax.axis_index("row") == col
+    left, flipped = left_part[0], vertex[0].T
+    half = left.shape[1]
+    columns = flipped.shape[0]
+    per_device = columns // momenta
+
+    left_far, flipped_far = swap(left, "col"), swap(flipped, "row")
+    scale = bubble.reshape(2, half)
+    near_scale = lax.dynamic_index_in_dim(scale, col, 0, keepdims=True)
+    far_scale = lax.dynamic_index_in_dim(scale, 1 - col, 0, keepdims=True)
+    near = (left.astype(F32) * near_scale).astype(BF)
+    far = (left_far.astype(F32) * far_scale).astype(BF)
+    first = nt(jnp.where(same, flipped, flipped_far), near)
+    first = first + nt(jnp.where(same, flipped_far, flipped), far)
+    rounded = first.astype(BF)
+    rounded_far = swap(rounded, "row")
+    second = nt(jnp.where(same, rounded, rounded_far), near)
+    second = second + nt(jnp.where(same, rounded_far, rounded), far)
+    summed = (flipped.astype(F32) + first + second).astype(BF)
+
+    summed = summed.reshape(momenta, per_device, -1)
+    received = lax.all_to_all(summed, "mom", split_axis=0, concat_axis=0, tiled=True)
+    column = jnp.arange(per_device, dtype=jnp.int32)[:, None]
+    source = (cross_map * per_device + column).reshape(-1, 1)
+    pick = source == jnp.arange(columns, dtype=jnp.int32)[None, :]
+    crossed = jnp.dot(
+        pick.astype(BF), received.reshape(columns, -1), preferred_element_type=F32
+    )
+    return crossed.astype(BF).reshape(per_device, momenta, -1)
+
+
+def tiled(left_part, vertex, bubble, cross_map):
     momenta = lax.axis_size("mom")
     left, vert = left_part[0], vertex[0]
     rows, half = left.shape
     columns = vert.shape[1]
     per_device = columns // momenta
-    cuts = (rows // 2, rows // 2 + rows // 3, rows)
     square = 2 * columns * half
-    starts = (0,) + cuts[:-1]
-    spans = list(zip(starts, cuts))
+    unit = rows // 6
+    cuts = (0, unit, 3 * unit, 5 * unit, rows)
+    spans = list(zip(cuts, cuts[1:]))
 
     pieces = fetch(left, spans[:1])
     pieces += fetch(left, spans[1:])
@@ -234,17 +255,12 @@
         flipped_far,
         flops=square * rows,
     )
-    direct = per_device % 16 == 0 and momenta & (momenta - 1) == 0
-    group = 16 * (2 - per_device // 16 % 2) if direct else per_device
+    group = 16 * (2 - per_device // 16 % 2)
     pick = local(
-        pick_body(group),
-        pltpu.VMEM((columns, momenta * group), BF),
-        cross_map.T,
-    )
-    own, others = [], []
-
-    def arrive(i, halves, first):
-        s, e = spans[i]
+        pick_body(group), pltpu.VMEM((columns, momenta * group), BF), cross_map.T
+    )
+    own, others, total = [], [], None
+    for i, (s, e) in enumerate(spans):
         halves, first, rounded = local(
             chunk_body(s, e),
             [
@@ -262,61 +278,38 @@
         )
         own.append(rounded)
         others.append(swap(rounded, "row"))
-        return halves, first
-
-    halves, first = arrive(0, halves, first)
-    halves, first = arrive(1, halves, first)
-    early = local(
-        early_body(cuts),
-        pltpu.VMEM((columns, cuts[1]), F32),
-        halves,
-        *own,
-        *others,
-        flops=square * 2 * cuts[1],
-    )
-    halves, first = arrive(2, halves, first)
-    late = local(
-        late_body(cuts),
-        pltpu.VMEM((columns, rows), F32),
-        halves,
-        *own,
-        *others[:2],
-        early,
-        flipped,
-        first,
-        flops=square * (rows - cuts[1]) * 3,
-    )
-    partners = xor_partners(momenta) if direct else [0]
-    size = per_device if direct else columns
-    sent = local(
-        last_body(cuts, partners),
-        [pltpu.VMEM((size, rows), BF)] * len(partners),
-        halves,
-        others[2],
-        late,
-        scratch=[pltpu.VMEM((columns, rows), BF)],
-    )
-    if not direct:
-        received = lax.all_to_all(
-            sent[0].reshape(momenta, per_device, rows),
-            "mom",
-            split_axis=0,
-            concat_axis=0,
-            tiled=True,
+        final = e == rows
+        inputs = [*own, *others[: len(own) - final], halves, flipped, first]
+        total = local(
+            add_body(spans, i, final),
+            pltpu.VMEM((columns, rows), F32),
+            *inputs,
+            *([] if total is None else [total]),
+            aliases={} if total is None else {len(inputs): 0},
+            flops=square * 2 * (e - s),
         )
-        crossed = jnp.dot(
-            pick, received.reshape(columns, rows), preferred_element_type=F32
+
+    partners = xor_partners(momenta)
+    order = partners[1:] + partners[:1]
+    sent = []
+    for chosen in (order[:1], order[1:]):
+        sent += local(
+            last_body(spans[-1], chosen),
+            [pltpu.VMEM((per_device, rows), BF)] * len(chosen),
+            halves,
+            others[-1],
+            total,
+            flops=square * unit * len(chosen) // momenta,
         )
-        return crossed.astype(BF).reshape(per_device, momenta, rows)
-
-    got = [sent[0]]
-    for block, k in zip(sent[1:], partners[1:]):
+    got = []
+    for block, k in zip(sent, order[:-1]):
         pairs = [(i, i ^ k) for i in range(momenta)]
         got.append(lax.ppermute(block, "mom", pairs))
+    arrays = [pick, *got, sent[-1]]
     crossed = pl.pallas_call(
-        cross_body(partners, momenta, group),
+        cross_body(order, group),
         out_shape=jax.ShapeDtypeStruct((columns, rows), BF),
-        in_specs=[VMEM] * (1 + momenta),
+        in_specs=[VMEM] * len(arrays),
         out_specs=ANY,
         scratch_shapes=[
             pltpu.VMEM((per_device // group, momenta * group, rows), BF),
@@ -324,7 +317,7 @@
             pltpu.SemaphoreType.DMA((per_device // group,)),
         ],
         compiler_params=LIMIT,
-    )(*[pltpu.with_memory_space_constraint(a, pltpu.VMEM) for a in (pick, *got)])
+    )(*[pltpu.with_memory_space_constraint(a, pltpu.VMEM) for a in arrays])
     return crossed.reshape(per_device, momenta, rows)
 
 
@@ -336,6 +329,18 @@
         P(("col", "mom"), None),
     )
     out_specs = P(("col", "mom"), None, "row")
-    return jax.shard_map(
-        on_device, mesh=mesh, in_specs=in_specs, out_specs=out_specs, check_vma=False
-    )
+
+    def step(body):
+        return jax.shard_map(
+            body, mesh=mesh, in_specs=in_specs, out_specs=out_specs, check_vma=False
+        )
+
+    momenta = mesh.shape["mom"]
+
+    def run(left_part, *rest):
+        per_device = left_part.shape[1] // momenta
+        if per_device % 16 or momenta & (momenta - 1) or momenta < 2:
+            return step(plain)(left_part, *rest)
+        return step(tiled)(left_part, *rest)
+
+    return run

time: 70.6 us -> 74.2 us (1.051)
  waiting for transfers between devices: 39.7 us -> 43.5 us
  starting transfers between devices: 18.4 us -> 17.4 us
    ppermute x7, starting transfers between devices: 13.1 us -> 10.3 us  [tiled(): got.append(lax.ppermute(block, 'mom', pairs))]
    ppermute x7, waiting for transfers between devices: 16.9 us -> 19.5 us  [tiled(): got.append(lax.ppermute(block, 'mom', pairs))]
    ppermute x7 -> x9, starting transfers between devices: 5.24 us -> 7.12 us  [swap(): return lax.ppermute(value, axis, [(0, 1), (1, 0)])]
    ppermute x7 -> x9, waiting for transfers between devices: 22.8 us -> 24 us  [swap(): return lax.ppermute(value, axis, [(0, 1), (1, 0)])]
    pallas_call x9 -> x13, Pallas kernels: 7.49 us -> 8.19 us  [local(): pl.pallas_call(body, out_shape=outs, in_specs=[VMEM] * len(arrays), out_s...]
  transfers between devices with their start and end apart: 14 -> 16, of which waited for: 9 -> 10; matrix products, arithmetic and copies ran while one was open for 0% -> 0% of each run, Pallas kernels for 12% -> 11%
where the time goes in v4:
time: 74.2 us; the launch traced here: 74 us
  waiting for transfers between devices  43.5 us (59%)
  starting transfers between devices  17.4 us (23%)
  Pallas kernels  11.7 us (16%)
  local copies, waits for them, and re-layouts  1.28 us (2%)
    ppermute x9, waiting for transfers between devices, swap(): return lax.ppermute(value, axis, [(0, 1), (1, 0)])  24 us
    ppermute x7, waiting for transfers between devices, tiled(): got.append(lax.ppermute(block, 'mom', pairs))  19.5 us
    ppermute x7, starting transfers between devices, tiled(): got.append(lax.ppermute(block, 'mom', pairs))  10.3 us
    pallas_call x13, Pallas kernels, local(): pl.pallas_call(body, out_shape=outs, in_specs=[VMEM] * len(arrays), out_s...  8.19 us
    ppermute x9, starting transfers between devices, swap(): return lax.ppermute(value, axis, [(0, 1), (1, 0)])  7.12 us
    pallas_call x2, Pallas kernels, fetch(): pl.pallas_call(body, out_shape=[pltpu.VMEM((e - s, array.shape[1]), array...  2.12 us
  transfers between devices with their start and end apart: 16, of which 10 were waited for; matrix products, arithmetic and copies ran while one was open for 0% of the time, Pallas kernels for 11%

profile of v4, /device:TPU:0, one launch (start us, length us, event | category | flops | bytes accessed | tf_op | source)
XLA Modules:
  0.0 74.0 jit_solution(16922155031815498909)
XLA Ops:
  0.0 1.3 %copy-done.1 = bf16[1,768,768]{2,1,0:T(8,128)(2,1)S(1)} copy-done((bf16[1,768,768]{2,1,0:T(8,128)(2,1)S(1)}, bf16[1,768,768]{2,1,0:T(8,128)(2,1)}, u32[]{:S(2)}) %copy-start.1) | copy-done | bytes 1179672
  2.2 0.9 %shard_map.50 = bf16[128,768]{1,0:T(8,128)(2,1)S(1)} custom-call(bf16[768,768]{1,0:T(8,128)(2,1)} %bitcast.4), custom_call_target="tpu_custom_call" | custom-call | tf_op jit(solution)/shard_map/pallas_call | solution.py:55
  3.1 2.6 %collective-permute-start.4 = (bf16[128,768]{1,0:T(8,128)(2,1)S(1)}, bf16[128,768]{1,0:T(8,128)(2,1)S(1)}, u32[]{:S(2)}, u32[]{:S(2)}) collective-permute-start(bf16[128,768]{1,0:T(8,128)(2,1)S(1)} %shard_map.50), channel_id=1, source_target_pairs={{0,1},{1,0},{2,3},{3,2},{4,5},{5,4},{6,7},{7,6},{8,9},{9,8},{10,11... | collective-permute-start | bytes 589832 | tf_op jit(solution)/shard_map/ppermute | solution.py:17
  5.7 1.2 %shard_map.47 = (bf16[256,768]{1,0:T(8,128)(2,1)S(1)}, bf16[256,768]{1,0:T(8,128)(2,1)S(1)}, bf16[128,768]{1,0:T(8,128)(2,1)S(1)}) custom-call(bf16[768,768]{1,0:T(8,128)(2,1)} %bitcast.5), custom_call_target="tpu_custom_call" | custom-call | tf_op jit(solution)/shard_map/pallas_call | solution.py:55
  7.0 1.4 %shard_map.49 = (bf16[2,768,768]{2,1,0:T(8,128)(2,1)S(1)}, f32[768,768]{1,0:T(8,128)S(1)}, bf16[768,768]{1,0:T(8,128)(2,1)S(1)}) custom-call(bf16[768,768]{1,0:T(8,128)(2,1)S(1)} %bitcast.6, f32[1,1536]{1,0:T(1,128)S(1)} %copy-done.2, bf16[768,768]{1,0:T(8,128)(2,1)S(1)} %shard_map.48.flipped.refs_3_.refs_5_.refs_7_.refs_8_, ...), custom_call_target="tpu_custom_call" | custom-call | flops 905969664 | bytes 1048576 | tf_op jit(solution)/shard_map/pallas_call | solution.py:29
  8.4 3.0 %collective-permute-done.4.far = bf16[128,768]{1,0:T(8,128)(2,1)S(1)} collective-permute-done((bf16[128,768]{1,0:T(8,128)(2,1)S(1)}, bf16[128,768]{1,0:T(8,128)(2,1)S(1)}, u32[]{:S(2)}, u32[]{:S(2)}) %collective-permute-start.4) | collective-permute-done | bytes 196640 | tf_op jit(solution)/shard_map/ppermute | solution.py:17
  12.0 1.4 %collective-permute-done.6.refs_1_.refs_2_.refs_3_.refs_4_ = bf16[768,128]{1,0:T(8,128)(2,1)S(1)} collective-permute-done((bf16[768,128]{1,0:T(8,128)(2,1)S(1)}, bf16[768,128]{1,0:T(8,128)(2,1)S(1)}, u32[]{:S(2)}, u32[]{:S(2)}) %collective-permute-start.6) | collective-permute-done | bytes 196640 | tf_op jit(solution)/shard_map/ppermute | solution.py:17
  13.7 6.0 %collective-permute-done.3.far = bf16[256,768]{1,0:T(8,128)(2,1)S(1)} collective-permute-done((bf16[256,768]{1,0:T(8,128)(2,1)S(1)}, bf16[256,768]{1,0:T(8,128)(2,1)S(1)}, u32[]{:S(2)}, u32[]{:S(2)}) %collective-permute-start.3) | collective-permute-done | bytes 393248 | tf_op jit(solution)/shard_map/ppermute | solution.py:17
  20.3 1.8 %collective-permute-start.2 = (bf16[256,768]{1,0:T(8,128)(2,1)S(1)}, bf16[256,768]{1,0:T(8,128)(2,1)S(1)}, u32[]{:S(2)}, u32[]{:S(2)}) collective-permute-start(bf16[256,768]{1,0:T(8,128)(2,1)S(1)} %get-tuple-element.32), channel_id=1, source_target_pairs={{0,1},{1,0},{2,3},{3,2},{4,5},{5,4},{6,7},{7,6},{8,9},{9,8},{10,11... | collective-permute-start | bytes 1179656 | tf_op jit(solution)/shard_map/ppermute | solution.py:17
  22.1 0.8 %shard_map.56.refs_9_ = f32[768,768]{1,0:T(8,128)S(1)} custom-call(bf16[768,128]{1,0:T(8,128)(2,1)S(1)} %get-tuple-element.44.refs_0_, bf16[768,256]{1,0:T(8,128)(2,1)S(1)} %get-tuple-element.45.refs_1_, bf16[768,128]{1,0:T(8,128)(2,1)S(1)} %collective-permute-done.6.refs_1_.refs_2_.refs_3_.refs_4_, ...), custom_call_target="tpu_custom_call", output_to_operand_aliasing={{}: (7, {})} | custom-call | flops 603979776 | bytes 1048576 | tf_op jit(solution)/shard_map/pallas_call | solution.py:29
  22.9 8.9 %collective-permute-done.2.far = bf16[256,768]{1,0:T(8,128)(2,1)S(1)} collective-permute-done((bf16[256,768]{1,0:T(8,128)(2,1)S(1)}, bf16[256,768]{1,0:T(8,128)(2,1)S(1)}, u32[]{:S(2)}, u32[]{:S(2)}) %collective-permute-start.2) | collective-permute-done | bytes 393248 | tf_op jit(solution)/shard_map/ppermute | solution.py:17
  32.4 1.8 %collective-permute-start = (bf16[128,768]{1,0:T(8,128)(2,1)S(1)}, bf16[128,768]{1,0:T(8,128)(2,1)S(1)}, u32[]{:S(2)}, u32[]{:S(2)}) collective-permute-start(bf16[128,768]{1,0:T(8,128)(2,1)S(1)} %get-tuple-element.30), channel_id=1, source_target_pairs={{0,1},{1,0},{2,3},{3,2},{4,5},{5,4},{6,7},{7,6},{8,9},{9,8},{10,11... | collective-permute-start | bytes 589832 | tf_op jit(solution)/shard_map/ppermute | solution.py:17
  34.2 1.2 %shard_map.57.refs_10_ = f32[768,768]{1,0:T(8,128)S(1)} custom-call(bf16[768,128]{1,0:T(8,128)(2,1)S(1)} %get-tuple-element.44.refs_0_, bf16[768,256]{1,0:T(8,128)(2,1)S(1)} %get-tuple-element.45.refs_1_, bf16[768,256]{1,0:T(8,128)(2,1)S(1)} %get-tuple-element.46.refs_2_, ...), custom_call_target="tpu_custom_call", output_to_operand_aliasing={{}: (9, {})} | custom-call | flops 603979776 | bytes 1048576 | tf_op jit(solution)/shard_map/pallas_call | solution.py:29
  35.5 4.3 %collective-permute-done.far = bf16[128,768]{1,0:T(8,128)(2,1)S(1)} collective-permute-done((bf16[128,768]{1,0:T(8,128)(2,1)S(1)}, bf16[128,768]{1,0:T(8,128)(2,1)S(1)}, u32[]{:S(2)}, u32[]{:S(2)}) %collective-permute-start) | collective-permute-done | bytes 196640 | tf_op jit(solution)/shard_map/ppermute | solution.py:17
  40.3 1.0 %shard_map.58.total = f32[768,768]{1,0:T(8,128)S(1)} custom-call(bf16[768,128]{1,0:T(8,128)(2,1)S(1)} %get-tuple-element.44.refs_0_, bf16[768,256]{1,0:T(8,128)(2,1)S(1)} %get-tuple-element.45.refs_1_, bf16[768,256]{1,0:T(8,128)(2,1)S(1)} %get-tuple-element.46.refs_2_, ...), custom_call_target="tpu_custom_call", output_to_operand_aliasing={{}: (10, {})} | custom-call | flops 301989888 | bytes 1048576 | tf_op jit(solution)/shard_map/pallas_call | solution.py:29
  42.3 3.9 %collective-permute-start.10 = (bf16[96,768]{1,0:T(8,128)(2,1)S(1)}, bf16[96,768]{1,0:T(8,128)(2,1)S(1)}, u32[]{:S(2)}, u32[]{:S(2)}) collective-permute-start(bf16[96,768]{1,0:T(8,128)(2,1)S(1)} %get-tuple-element.48), channel_id=1, source_target_pairs={{0,24},{4,28},{8,16},{12,20},{16,8},{20,12},{24,0},{28,4},{1,25},{... | collective-permute-start | bytes 442376 | tf_op jit(solution)/shard_map/ppermute | solution.py:307
  46.5 2.5 %collective-permute-start.12 = (bf16[96,768]{1,0:T(8,128)(2,1)S(1)}, bf16[96,768]{1,0:T(8,128)(2,1)S(1)}, u32[]{:S(2)}, u32[]{:S(2)}) collective-permute-start(bf16[96,768]{1,0:T(8,128)(2,1)S(1)} %get-tuple-element.50), channel_id=1, source_target_pairs={{0,28},{4,24},{8,20},{12,16},{16,12},{20,8},{24,4},{28,0},{1,29},{... | collective-permute-start | bytes 442376 | tf_op jit(solution)/shard_map/ppermute | solution.py:307
  49.0 1.6 %collective-permute-start.13 = (bf16[96,768]{1,0:T(8,128)(2,1)S(1)}, bf16[96,768]{1,0:T(8,128)(2,1)S(1)}, u32[]{:S(2)}, u32[]{:S(2)}) collective-permute-start(bf16[96,768]{1,0:T(8,128)(2,1)S(1)} %get-tuple-element.51), channel_id=1, source_target_pairs={{0,8},{4,12},{8,0},{12,4},{16,24},{20,28},{24,16},{28,20},{1,9},{5... | collective-permute-start | bytes 442376 | tf_op jit(solution)/shard_map/ppermute | solution.py:307
  50.6 1.4 %collective-permute-start.14 = (bf16[96,768]{1,0:T(8,128)(2,1)S(1)}, bf16[96,768]{1,0:T(8,128)(2,1)S(1)}, u32[]{:S(2)}, u32[]{:S(2)}) collective-permute-start(bf16[96,768]{1,0:T(8,128)(2,1)S(1)} %get-tuple-element.52), channel_id=1, source_target_pairs={{0,12},{4,8},{8,4},{12,0},{16,28},{20,24},{24,20},{28,16},{1,13},{... | collective-permute-start | bytes 442376 | tf_op jit(solution)/shard_map/ppermute | solution.py:307
  52.2 0.6 collective-permute-start.15
  52.8 11.2 %collective-permute-done.11.refs_2_ = bf16[96,768]{1,0:T(8,128)(2,1)S(1)} collective-permute-done((bf16[96,768]{1,0:T(8,128)(2,1)S(1)}, bf16[96,768]{1,0:T(8,128)(2,1)S(1)}, u32[]{:S(2)}, u32[]{:S(2)}) %collective-permute-start.11) | collective-permute-done | bytes 147488 | tf_op jit(solution)/shard_map/ppermute | solution.py:307
  64.6 1.6 %collective-permute-done.15.refs_6_ = bf16[96,768]{1,0:T(8,128)(2,1)S(1)} collective-permute-done((bf16[96,768]{1,0:T(8,128)(2,1)S(1)}, bf16[96,768]{1,0:T(8,128)(2,1)S(1)}, u32[]{:S(2)}, u32[]{:S(2)}) %collective-permute-start.15) | collective-permute-done | bytes 147488 | tf_op jit(solution)/shard_map/ppermute | solution.py:307
  66.2 6.5 %collective-permute-done.9.refs_0_ = bf16[96,768]{1,0:T(8,128)(2,1)S(1)} collective-permute-done((bf16[96,768]{1,0:T(8,128)(2,1)S(1)}, bf16[96,768]{1,0:T(8,128)(2,1)S(1)}, u32[]{:S(2)}, u32[]{:S(2)}) %collective-permute-start.9) | collective-permute-done | bytes 147488 | tf_op jit(solution)/shard_map/ppermute | solution.py:307
  72.7 1.4 %shard_map.61 = bf16[768,768]{1,0:T(8,128)(2,1)} custom-call(bf16[768,256]{1,0:T(8,128)(2,1)S(1)} %shard_map.46.pick, bf16[96,768]{1,0:T(8,128)(2,1)S(1)} %collective-permute-done.9.refs_0_, bf16[96,768]{1,0:T(8,128)(2,1)S(1)} %collective-permute-done.10.refs_1_, bf16[96,768]{1,0:T(8,128)(2,1)S(1)} %collective-permute-done.11.refs_2_, ...), custom_call_target="tpu_custom_call" | custom-call | tf_op jit(solution)/shard_map/pallas_call | solution.py:309
  (32 shorter events, 5.8 us)
Async XLA Ops:
  0.0 1.3 %copy-start.1 = (bf16[1,768,768]{2,1,0:T(8,128)(2,1)S(1)}, bf16[1,768,768]{2,1,0:T(8,128)(2,1)}, u32[]{:S(2)}) copy-start(bf16[1,768,768]{2,1,0:T(8,128)(2,1)} %param.5) | copy-start | bytes 3538948
  1.3 5.7 %copy-start = (bf16[1,768,768]{2,1,0:T(8,128)(2,1)S(1)}, bf16[1,768,768]{2,1,0:T(8,128)(2,1)}, u32[]{:S(2)}) copy-start(bf16[1,768,768]{2,1,0:T(8,128)(2,1)} %param.4) | copy-start | bytes 3538948
  1.3 5.7 %copy-start.2 = (f32[1,1536]{1,0:T(1,128)S(1)}, f32[1,1536]{1,0:T(1,128)}, u32[]{:S(2)}) copy-start(f32[1,1536]{1,0:T(1,128)} %bubble.9) | copy-start | bytes 18436
  1.6 5.4 %collective-permute-start.1 = (bf16[768,768]{1,0:T(8,128)(2,1)S(1)}, bf16[768,768]{1,0:T(8,128)(2,1)S(1)}, u32[]{:S(2)}, u32[]{:S(2)}) collective-permute-start(bf16[768,768]{1,0:T(8,128)(2,1)S(1)} %shard_map.48.flipped.refs_3_.refs_5_.refs_7_.refs_8_), channel_id=1, source_target_pairs={{0,2},{2,0},{1,3},{3,1},{4,6},{6,4},{5,7},{7,5},{8,10},{10,8},{9,1... | collective-permute-start | bytes 3538952 | tf_op jit(solution)/shard_map/ppermute | solution.py:17
  3.1 8.3 %collective-permute-start.4 = (bf16[128,768]{1,0:T(8,128)(2,1)S(1)}, bf16[128,768]{1,0:T(8,128)(2,1)S(1)}, u32[]{:S(2)}, u32[]{:S(2)}) collective-permute-start(bf16[128,768]{1,0:T(8,128)(2,1)S(1)} %shard_map.50), channel_id=1, source_target_pairs={{0,1},{1,0},{2,3},{3,2},{4,5},{5,4},{6,7},{7,6},{8,9},{9,8},{10,11... | collective-permute-start | bytes 589832 | tf_op jit(solution)/shard_map/ppermute | solution.py:17
  6.9 12.8 %collective-permute-start.3 = (bf16[256,768]{1,0:T(8,128)(2,1)S(1)}, bf16[256,768]{1,0:T(8,128)(2,1)S(1)}, u32[]{:S(2)}, u32[]{:S(2)}) collective-permute-start(bf16[256,768]{1,0:T(8,128)(2,1)S(1)} %get-tuple-element.33), channel_id=1, source_target_pairs={{0,1},{1,0},{2,3},{3,2},{4,5},{5,4},{6,7},{7,6},{8,9},{9,8},{10,11... | collective-permute-start | bytes 1179656 | tf_op jit(solution)/shard_map/ppermute | solution.py:17
  12.0 1.5 %collective-permute-start.6 = (bf16[768,128]{1,0:T(8,128)(2,1)S(1)}, bf16[768,128]{1,0:T(8,128)(2,1)S(1)}, u32[]{:S(2)}, u32[]{:S(2)}) collective-permute-start(bf16[768,128]{1,0:T(8,128)(2,1)S(1)} %get-tuple-element.44.refs_0_), channel_id=1, source_target_pairs={{0,2},{2,0},{1,3},{3,1},{4,6},{6,4},{5,7},{7,5},{8,10},{10,8},{9,1... | collective-permute-start | bytes 589832 | tf_op jit(solution)/shard_map/ppermute | solution.py:17
  20.2 1.9 %collective-permute-start.7 = (bf16[768,256]{1,0:T(8,128)(2,1)S(1)}, bf16[768,256]{1,0:T(8,128)(2,1)S(1)}, u32[]{:S(2)}, u32[]{:S(2)}) collective-permute-start(bf16[768,256]{1,0:T(8,128)(2,1)S(1)} %get-tuple-element.45.refs_1_), channel_id=1, source_target_pairs={{0,2},{2,0},{1,3},{3,1},{4,6},{6,4},{5,7},{7,5},{8,10},{10,8},{9,1... | collective-permute-start | bytes 1179656 | tf_op jit(solution)/shard_map/ppermute | solution.py:17
  20.3 11.5 %collective-permute-start.2 = (bf16[256,768]{1,0:T(8,128)(2,1)S(1)}, bf16[256,768]{1,0:T(8,128)(2,1)S(1)}, u32[]{:S(2)}, u32[]{:S(2)}) collective-permute-start(bf16[256,768]{1,0:T(8,128)(2,1)S(1)} %get-tuple-element.32), channel_id=1, source_target_pairs={{0,1},{1,0},{2,3},{3,2},{4,5},{5,4},{6,7},{7,6},{8,9},{9,8},{10,11... | collective-permute-start | bytes 1179656 | tf_op jit(solution)/shard_map/ppermute | solution.py:17
  32.3 1.9 %collective-permute-start.8 = (bf16[768,256]{1,0:T(8,128)(2,1)S(1)}, bf16[768,256]{1,0:T(8,128)(2,1)S(1)}, u32[]{:S(2)}, u32[]{:S(2)}) collective-permute-start(bf16[768,256]{1,0:T(8,128)(2,1)S(1)} %get-tuple-element.46.refs_2_), channel_id=1, source_target_pairs={{0,2},{2,0},{1,3},{3,1},{4,6},{6,4},{5,7},{7,5},{8,10},{10,8},{9,1... | collective-permute-start | bytes 1179656 | tf_op jit(solution)/shard_map/ppermute | solution.py:17
  32.4 7.3 %collective-permute-start = (bf16[128,768]{1,0:T(8,128)(2,1)S(1)}, bf16[128,768]{1,0:T(8,128)(2,1)S(1)}, u32[]{:S(2)}, u32[]{:S(2)}) collective-permute-start(bf16[128,768]{1,0:T(8,128)(2,1)S(1)} %get-tuple-element.30), channel_id=1, source_target_pairs={{0,1},{1,0},{2,3},{3,2},{4,5},{5,4},{6,7},{7,6},{8,9},{9,8},{10,11... | collective-permute-start | bytes 589832 | tf_op jit(solution)/shard_map/ppermute | solution.py:17
  40.2 1.5 %collective-permute-start.5 = (bf16[768,128]{1,0:T(8,128)(2,1)S(1)}, bf16[768,128]{1,0:T(8,128)(2,1)S(1)}, u32[]{:S(2)}, u32[]{:S(2)}) collective-permute-start(bf16[768,128]{1,0:T(8,128)(2,1)S(1)} %get-tuple-element.43.refs_3_), channel_id=1, source_target_pairs={{0,2},{2,0},{1,3},{3,1},{4,6},{6,4},{5,7},{7,5},{8,10},{10,8},{9,1... | collective-permute-start | bytes 589832 | tf_op jit(solution)/shard_map/ppermute | solution.py:17
  42.3 9.9 %collective-permute-start.10 = (bf16[96,768]{1,0:T(8,128)(2,1)S(1)}, bf16[96,768]{1,0:T(8,128)(2,1)S(1)}, u32[]{:S(2)}, u32[]{:S(2)}) collective-permute-start(bf16[96,768]{1,0:T(8,128)(2,1)S(1)} %get-tuple-element.48), channel_id=1, source_target_pairs={{0,24},{4,28},{8,16},{12,20},{16,8},{20,12},{24,0},{28,4},{1,25},{... | collective-permute-start | bytes 442376 | tf_op jit(solution)/shard_map/ppermute | solution.py:307
  46.2 17.7 %collective-permute-start.11 = (bf16[96,768]{1,0:T(8,128)(2,1)S(1)}, bf16[96,768]{1,0:T(8,128)(2,1)S(1)}, u32[]{:S(2)}, u32[]{:S(2)}) collective-permute-start(bf16[96,768]{1,0:T(8,128)(2,1)S(1)} %get-tuple-element.49), channel_id=1, source_target_pairs={{0,20},{4,16},{8,28},{12,24},{16,4},{20,0},{24,12},{28,8},{1,21},{... | collective-permute-start | bytes 442376 | tf_op jit(solution)/shard_map/ppermute | solution.py:307
  46.5 17.8 %collective-permute-start.12 = (bf16[96,768]{1,0:T(8,128)(2,1)S(1)}, bf16[96,768]{1,0:T(8,128)(2,1)S(1)}, u32[]{:S(2)}, u32[]{:S(2)}) collective-permute-start(bf16[96,768]{1,0:T(8,128)(2,1)S(1)} %get-tuple-element.50), channel_id=1, source_target_pairs={{0,28},{4,24},{8,20},{12,16},{16,12},{20,8},{24,4},{28,0},{1,29},{... | collective-permute-start | bytes 442376 | tf_op jit(solution)/shard_map/ppermute | solution.py:307
  49.0 15.3 %collective-permute-start.13 = (bf16[96,768]{1,0:T(8,128)(2,1)S(1)}, bf16[96,768]{1,0:T(8,128)(2,1)S(1)}, u32[]{:S(2)}, u32[]{:S(2)}) collective-permute-start(bf16[96,768]{1,0:T(8,128)(2,1)S(1)} %get-tuple-element.51), channel_id=1, source_target_pairs={{0,8},{4,12},{8,0},{12,4},{16,24},{20,28},{24,16},{28,20},{1,9},{5... | collective-permute-start | bytes 442376 | tf_op jit(solution)/shard_map/ppermute | solution.py:307
  50.6 13.4 %copy-start.3 = (s32[96,8]{0,1:T(8,128)S(1)}, s32[96,8]{0,1:T(8,128)}, u32[]{:S(2)}) copy-start(s32[96,8]{0,1:T(8,128)} %param.7) | copy-start | bytes 9220
  50.6 14.0 %collective-permute-start.14 = (bf16[96,768]{1,0:T(8,128)(2,1)S(1)}, bf16[96,768]{1,0:T(8,128)(2,1)S(1)}, u32[]{:S(2)}, u32[]{:S(2)}) collective-permute-start(bf16[96,768]{1,0:T(8,128)(2,1)S(1)} %get-tuple-element.52), channel_id=1, source_target_pairs={{0,12},{4,8},{8,4},{12,0},{16,28},{20,24},{24,20},{28,16},{1,13},{... | collective-permute-start | bytes 442376 | tf_op jit(solution)/shard_map/ppermute | solution.py:307
  52.2 14.0 %collective-permute-start.15 = (bf16[96,768]{1,0:T(8,128)(2,1)S(1)}, bf16[96,768]{1,0:T(8,128)(2,1)S(1)}, u32[]{:S(2)}, u32[]{:S(2)}) collective-permute-start(bf16[96,768]{1,0:T(8,128)(2,1)S(1)} %get-tuple-element.53), channel_id=1, source_target_pairs={{0,4},{4,0},{8,12},{12,8},{16,20},{20,16},{24,28},{28,24},{1,5},{5... | collective-permute-start | bytes 442376 | tf_op jit(solution)/shard_map/ppermute | solution.py:307
  63.9 8.7 %collective-permute-start.9 = (bf16[96,768]{1,0:T(8,128)(2,1)S(1)}, bf16[96,768]{1,0:T(8,128)(2,1)S(1)}, u32[]{:S(2)}, u32[]{:S(2)}) collective-permute-start(bf16[96,768]{1,0:T(8,128)(2,1)S(1)} %shard_map.59), channel_id=1, source_target_pairs={{0,16},{4,20},{8,24},{12,28},{16,0},{20,4},{24,8},{28,12},{1,17},{... | collective-permute-start | bytes 442376 | tf_op jit(solution)/shard_map/ppermute | solution.py:307

commit v5 on v4

--- a/solution.py
+++ b/solution.py
@@ -120,22 +120,22 @@
     return body
 
 
-def last_body(span, partners):
+def last_body(span, steps):
     def body(halves, far, total, *outs):
         row, mom = lax.axis_index("row"), lax.axis_index("mom")
         s, e = span
         size = outs[0].shape[0]
         weights = halves[1 - row, :, s:e]
-        for out, partner in zip(outs, partners):
-            begin = pl.multiple_of((mom ^ partner) * size, size)
+        for out, step in zip(outs, steps):
+            begin = pl.multiple_of(meet(mom, step) * size, size)
             lines = pl.ds(begin, size)
             out[...] = (total[lines, :] + nt(far[lines, :], weights)).astype(BF)
 
     return body
 
 
-def cross_body(partners, group):
-    momenta = len(partners)
+def cross_body(steps, group):
+    momenta = len(steps)
 
     def body(pick, *refs):
         blocks, (out, gathered, result, sem) = refs[:momenta], refs[momenta:]
@@ -144,8 +144,8 @@
         size = group * momenta
         copies = []
         for i in range(groups):
-            for block, partner in zip(blocks, partners):
-                begin = pl.multiple_of((mom ^ partner) * group, group)
+            for block, step in zip(blocks, steps):
+                begin = pl.multiple_of(meet(mom, step) * group, group)
                 gathered[i, pl.ds(begin, group), :] = block[
                     i * group : (i + 1) * group, :
                 ]
@@ -164,11 +164,26 @@
     return body
 
 
-def xor_partners(momenta):
+def team(mom):
+    return ((mom >> 1) ^ (mom >> 2)) & 1
+
+
+def meet(mom, step):
+    outer, inner = step
+    return mom ^ (outer + team(mom) * (inner - outer))
+
+
+def steps_of(momenta):
     def key(k):
         return (-k.bit_length(), int(format(k, "b")[::-1], 2))
 
-    return [0] + sorted(range(1, momenta), key=key)
+    steps = [(k, k) for k in sorted(range(1, momenta), key=key)]
+    if momenta >= 8:
+        far = momenta - 2
+        mixed = [(1, far), (far, 1)]
+        steps = [k for k in steps if k[0] not in (1, far)]
+        steps = mixed[:1] + [(4, 4), (2, 2), (5, 5)] + mixed[1:] + [(3, 3), (7, 7)]
+    return steps
 
 
 def pick_body(group):
@@ -232,7 +247,7 @@
     per_device = columns // momenta
     square = 2 * columns * half
     unit = rows // 6
-    cuts = (0, unit, 3 * unit, 5 * unit, rows)
+    cuts = (0, unit, 3 * unit, 4 * unit, 5 * unit, rows)
     spans = list(zip(cuts, cuts[1:]))
 
     pieces = fetch(left, spans[:1])
@@ -289,8 +304,7 @@
             flops=square * 2 * (e - s),
         )
 
-    partners = xor_partners(momenta)
-    order = partners[1:] + partners[:1]
+    order = steps_of(momenta) + [(0, 0)]
     sent = []
     for chosen in (order[:1], order[1:]):
         sent += local(
@@ -302,8 +316,8 @@
             flops=square * unit * len(chosen) // momenta,
         )
     got = []
-    for block, k in zip(sent, order[:-1]):
-        pairs = [(i, i ^ k) for i in range(momenta)]
+    for block, step in zip(sent, order[:-1]):
+        pairs = [(m, meet(m, step)) for m in range(momenta)]
         got.append(lax.ppermute(block, "mom", pairs))
     arrays = [pick, *got, sent[-1]]
     crossed = pl.pallas_call(
@@ -341,6 +355,8 @@
         per_device = left_part.shape[1] // momenta
         if per_device % 16 or momenta & (momenta - 1) or momenta < 2:
             return step(plain)(left_part, *rest)
-        return step(tiled)(left_part, *rest)
+        return step(tiled)(
+            left_part, *rest
+        )
 
     return run

time: 74.2 us -> 75.4 us (1.016)
  the two profiles are of different devices: /device:TPU:0 before, /device:TPU:19 now
where the time goes in v5:
time: 75.4 us; the launch traced here: 75.2 us
  waiting for transfers between devices  40.2 us (53%)
  starting transfers between devices  20.7 us (27%)
  Pallas kernels  13 us (17%)
  local copies, waits for them, and re-layouts  1.28 us (2%)
    ppermute x11, waiting for transfers between devices, swap(): return lax.ppermute(value, axis, [(0, 1), (1, 0)])  21.1 us
    ppermute x7, waiting for transfers between devices, tiled(): got.append(lax.ppermute(block, 'mom', pairs))  19.1 us
    ppermute x11, starting transfers between devices, swap(): return lax.ppermute(value, axis, [(0, 1), (1, 0)])  11.4 us
    pallas_call x15, Pallas kernels, local(): pl.pallas_call(body, out_shape=outs, in_specs=[VMEM] * len(arrays), out_s...  9.44 us
    ppermute x7, starting transfers between devices, tiled(): got.append(lax.ppermute(block, 'mom', pairs))  9.26 us
    pallas_call x2, Pallas kernels, fetch(): pl.pallas_call(body, out_shape=[pltpu.VMEM((e - s, array.shape[1]), array...  2.17 us
  transfers between devices with their start and end apart: 18, of which 11 were waited for; matrix products, arithmetic and copies ran while one was open for 0% of the time, Pallas kernels for 12%

profile of v5, /device:TPU:19, one launch (start us, length us, event | category | flops | bytes accessed | tf_op | source)
XLA Modules:
  0.0 75.2 jit_solution(17699702096767214516)
XLA Ops:
  0.0 1.3 %copy-done.1 = bf16[1,768,768]{2,1,0:T(8,128)(2,1)S(1)} copy-done((bf16[1,768,768]{2,1,0:T(8,128)(2,1)S(1)}, bf16[1,768,768]{2,1,0:T(8,128)(2,1)}, u32[]{:S(2)}) %copy-start.1) | copy-done | bytes 1179672
  3.3 1.3 %collective-permute-start.5 = (bf16[128,768]{1,0:T(8,128)(2,1)S(1)}, bf16[128,768]{1,0:T(8,128)(2,1)S(1)}, u32[]{:S(2)}, u32[]{:S(2)}) collective-permute-start(bf16[128,768]{1,0:T(8,128)(2,1)S(1)} %shard_map.50), channel_id=1, source_target_pairs={{0,1},{1,0},{2,3},{3,2},{4,5},{5,4},{6,7},{7,6},{8,9},{9,8},{10,11... | collective-permute-start | bytes 589832 | tf_op jit(solution)/shard_map/ppermute | solution.py:17
  4.6 1.2 %shard_map.47 = (bf16[256,768]{1,0:T(8,128)(2,1)S(1)}, bf16[128,768]{1,0:T(8,128)(2,1)S(1)}, bf16[128,768]{1,0:T(8,128)(2,1)S(1)}, bf16[128,768]{1,0:T(8,128)(2,1)S(1)}) custom-call(bf16[768,768]{1,0:T(8,128)(2,1)} %bitcast.5), custom_call_target="tpu_custom_call" | custom-call | tf_op jit(solution)/shard_map/pallas_call | solution.py:55
  6.2 1.4 %shard_map.49 = (bf16[2,768,768]{2,1,0:T(8,128)(2,1)S(1)}, f32[768,768]{1,0:T(8,128)S(1)}, bf16[768,768]{1,0:T(8,128)(2,1)S(1)}) custom-call(bf16[768,768]{1,0:T(8,128)(2,1)S(1)} %bitcast.6, f32[1,1536]{1,0:T(1,128)S(1)} %copy-done.2, bf16[768,768]{1,0:T(8,128)(2,1)S(1)} %shard_map.48.flipped.refs_3_.refs_5_.refs_7_.refs_9_.refs_10_, ...), custom_call_target="tpu_custom_call" | custom-call | flops 905969664 | bytes 1048576 | tf_op jit(solution)/shard_map/pallas_call | solution.py:29
  7.6 2.3 %collective-permute-done.5.far = bf16[128,768]{1,0:T(8,128)(2,1)S(1)} collective-permute-done((bf16[128,768]{1,0:T(8,128)(2,1)S(1)}, bf16[128,768]{1,0:T(8,128)(2,1)S(1)}, u32[]{:S(2)}, u32[]{:S(2)}) %collective-permute-start.5) | collective-permute-done | bytes 196640 | tf_op jit(solution)/shard_map/ppermute | solution.py:17
  10.3 1.4 %collective-permute-start.7 = (bf16[768,128]{1,0:T(8,128)(2,1)S(1)}, bf16[768,128]{1,0:T(8,128)(2,1)S(1)}, u32[]{:S(2)}, u32[]{:S(2)}) collective-permute-start(bf16[768,128]{1,0:T(8,128)(2,1)S(1)} %get-tuple-element.51.refs_0_), channel_id=1, source_target_pairs={{0,2},{2,0},{1,3},{3,1},{4,6},{6,4},{5,7},{7,5},{8,10},{10,8},{9,1... | collective-permute-start | bytes 589832 | tf_op jit(solution)/shard_map/ppermute | solution.py:17
  11.7 1.1 %collective-permute-done.7.refs_1_.refs_2_.refs_3_.refs_4_.refs_5_ = bf16[768,128]{1,0:T(8,128)(2,1)S(1)} collective-permute-done((bf16[768,128]{1,0:T(8,128)(2,1)S(1)}, bf16[768,128]{1,0:T(8,128)(2,1)S(1)}, u32[]{:S(2)}, u32[]{:S(2)}) %collective-permute-start.7) | collective-permute-done | bytes 196640 | tf_op jit(solution)/shard_map/ppermute | solution.py:17
  13.1 5.2 %collective-permute-done.4.far = bf16[256,768]{1,0:T(8,128)(2,1)S(1)} collective-permute-done((bf16[256,768]{1,0:T(8,128)(2,1)S(1)}, bf16[256,768]{1,0:T(8,128)(2,1)S(1)}, u32[]{:S(2)}, u32[]{:S(2)}) %collective-permute-start.4) | collective-permute-done | bytes 393248 | tf_op jit(solution)/shard_map/ppermute | solution.py:17
  19.7 1.2 %collective-permute-start.3 = (bf16[128,768]{1,0:T(8,128)(2,1)S(1)}, bf16[128,768]{1,0:T(8,128)(2,1)S(1)}, u32[]{:S(2)}, u32[]{:S(2)}) collective-permute-start(bf16[128,768]{1,0:T(8,128)(2,1)S(1)} %get-tuple-element.37), channel_id=1, source_target_pairs={{0,1},{1,0},{2,3},{3,2},{4,5},{5,4},{6,7},{7,6},{8,9},{9,8},{10,11... | collective-permute-start | bytes 589832 | tf_op jit(solution)/shard_map/ppermute | solution.py:17
  21.9 4.2 %collective-permute-done.3.far = bf16[128,768]{1,0:T(8,128)(2,1)S(1)} collective-permute-done((bf16[128,768]{1,0:T(8,128)(2,1)S(1)}, bf16[128,768]{1,0:T(8,128)(2,1)S(1)}, u32[]{:S(2)}, u32[]{:S(2)}) %collective-permute-start.3) | collective-permute-done | bytes 196640 | tf_op jit(solution)/shard_map/ppermute | solution.py:17
  27.6 1.2 %collective-permute-start.2 = (bf16[128,768]{1,0:T(8,128)(2,1)S(1)}, bf16[128,768]{1,0:T(8,128)(2,1)S(1)}, u32[]{:S(2)}, u32[]{:S(2)}) collective-permute-start(bf16[128,768]{1,0:T(8,128)(2,1)S(1)} %get-tuple-element.36), channel_id=1, source_target_pairs={{0,1},{1,0},{2,3},{3,2},{4,5},{5,4},{6,7},{7,6},{8,9},{9,8},{10,11... | collective-permute-start | bytes 589832 | tf_op jit(solution)/shard_map/ppermute | solution.py:17
  29.7 4.2 %collective-permute-done.2.far = bf16[128,768]{1,0:T(8,128)(2,1)S(1)} collective-permute-done((bf16[128,768]{1,0:T(8,128)(2,1)S(1)}, bf16[128,768]{1,0:T(8,128)(2,1)S(1)}, u32[]{:S(2)}, u32[]{:S(2)}) %collective-permute-start.2) | collective-permute-done | bytes 196640 | tf_op jit(solution)/shard_map/ppermute | solution.py:17
  35.4 1.2 %collective-permute-start = (bf16[128,768]{1,0:T(8,128)(2,1)S(1)}, bf16[128,768]{1,0:T(8,128)(2,1)S(1)}, u32[]{:S(2)}, u32[]{:S(2)}) collective-permute-start(bf16[128,768]{1,0:T(8,128)(2,1)S(1)} %get-tuple-element.34), channel_id=1, source_target_pairs={{0,1},{1,0},{2,3},{3,2},{4,5},{5,4},{6,7},{7,6},{8,9},{9,8},{10,11... | collective-permute-start | bytes 589832 | tf_op jit(solution)/shard_map/ppermute | solution.py:17
  36.7 1.1 %shard_map.59.refs_12_ = f32[768,768]{1,0:T(8,128)S(1)} custom-call(bf16[768,128]{1,0:T(8,128)(2,1)S(1)} %get-tuple-element.51.refs_0_, bf16[768,256]{1,0:T(8,128)(2,1)S(1)} %get-tuple-element.52.refs_1_, bf16[768,128]{1,0:T(8,128)(2,1)S(1)} %get-tuple-element.53.refs_2_, ...), custom_call_target="tpu_custom_call", output_to_operand_aliasing={{}: (11, {})} | custom-call | flops 301989888 | bytes 1048576 | tf_op jit(solution)/shard_map/pallas_call | solution.py:29
  37.8 4.0 %collective-permute-done.far = bf16[128,768]{1,0:T(8,128)(2,1)S(1)} collective-permute-done((bf16[128,768]{1,0:T(8,128)(2,1)S(1)}, bf16[128,768]{1,0:T(8,128)(2,1)S(1)}, u32[]{:S(2)}, u32[]{:S(2)}) %collective-permute-start) | collective-permute-done | bytes 196640 | tf_op jit(solution)/shard_map/ppermute | solution.py:17
  45.1 1.3 %collective-permute-start.13 = (bf16[96,768]{1,0:T(8,128)(2,1)S(1)}, bf16[96,768]{1,0:T(8,128)(2,1)S(1)}, u32[]{:S(2)}, u32[]{:S(2)}) collective-permute-start(bf16[96,768]{1,0:T(8,128)(2,1)S(1)} %get-tuple-element.57), channel_id=1, source_target_pairs={{0,8},{4,12},{8,0},{12,4},{16,24},{20,28},{24,16},{28,20},{1,9},{5... | collective-permute-start | bytes 442376 | tf_op jit(solution)/shard_map/ppermute | solution.py:321
  46.4 2.3 %collective-permute-start.14 = (bf16[96,768]{1,0:T(8,128)(2,1)S(1)}, bf16[96,768]{1,0:T(8,128)(2,1)S(1)}, u32[]{:S(2)}, u32[]{:S(2)}) collective-permute-start(bf16[96,768]{1,0:T(8,128)(2,1)S(1)} %get-tuple-element.58), channel_id=1, source_target_pairs={{0,20},{4,16},{8,28},{12,24},{16,4},{20,0},{24,12},{28,8},{1,21},{... | collective-permute-start | bytes 442376 | tf_op jit(solution)/shard_map/ppermute | solution.py:321
  48.7 1.2 %collective-permute-start.15 = (bf16[96,768]{1,0:T(8,128)(2,1)S(1)}, bf16[96,768]{1,0:T(8,128)(2,1)S(1)}, u32[]{:S(2)}, u32[]{:S(2)}) collective-permute-start(bf16[96,768]{1,0:T(8,128)(2,1)S(1)} %get-tuple-element.59), channel_id=1, source_target_pairs={{0,24},{4,28},{8,12},{12,8},{16,20},{20,16},{24,0},{28,4},{1,25},{... | collective-permute-start | bytes 442376 | tf_op jit(solution)/shard_map/ppermute | solution.py:321
  51.1 3.3 %collective-permute-start.17 = (bf16[96,768]{1,0:T(8,128)(2,1)S(1)}, bf16[96,768]{1,0:T(8,128)(2,1)S(1)}, u32[]{:S(2)}, u32[]{:S(2)}) collective-permute-start(bf16[96,768]{1,0:T(8,128)(2,1)S(1)} %get-tuple-element.61), channel_id=1, source_target_pairs={{0,28},{4,24},{8,20},{12,16},{16,12},{20,8},{24,4},{28,0},{1,29},{... | collective-permute-start | bytes 442376 | tf_op jit(solution)/shard_map/ppermute | solution.py:321
  54.8 5.7 %collective-permute-done.14.refs_3_ = bf16[96,768]{1,0:T(8,128)(2,1)S(1)} collective-permute-done((bf16[96,768]{1,0:T(8,128)(2,1)S(1)}, bf16[96,768]{1,0:T(8,128)(2,1)S(1)}, u32[]{:S(2)}, u32[]{:S(2)}) %collective-permute-start.14) | collective-permute-done | bytes 147488 | tf_op jit(solution)/shard_map/ppermute | solution.py:321
  60.5 2.1 %collective-permute-done.16.refs_5_ = bf16[96,768]{1,0:T(8,128)(2,1)S(1)} collective-permute-done((bf16[96,768]{1,0:T(8,128)(2,1)S(1)}, bf16[96,768]{1,0:T(8,128)(2,1)S(1)}, u32[]{:S(2)}, u32[]{:S(2)}) %collective-permute-start.16) | collective-permute-done | bytes 147488 | tf_op jit(solution)/shard_map/ppermute | solution.py:321
  62.6 8.0 %collective-permute-done.17.refs_6_ = bf16[96,768]{1,0:T(8,128)(2,1)S(1)} collective-permute-done((bf16[96,768]{1,0:T(8,128)(2,1)S(1)}, bf16[96,768]{1,0:T(8,128)(2,1)S(1)}, u32[]{:S(2)}, u32[]{:S(2)}) %collective-permute-start.17) | collective-permute-done | bytes 147488 | tf_op jit(solution)/shard_map/ppermute | solution.py:321
  70.7 3.2 %collective-permute-done.11.refs_0_ = bf16[96,768]{1,0:T(8,128)(2,1)S(1)} collective-permute-done((bf16[96,768]{1,0:T(8,128)(2,1)S(1)}, bf16[96,768]{1,0:T(8,128)(2,1)S(1)}, u32[]{:S(2)}, u32[]{:S(2)}) %collective-permute-start.11) | collective-permute-done | bytes 147488 | tf_op jit(solution)/shard_map/ppermute | solution.py:321
  73.9 1.4 %shard_map.63 = bf16[768,768]{1,0:T(8,128)(2,1)} custom-call(bf16[768,256]{1,0:T(8,128)(2,1)S(1)} %shard_map.46.pick, bf16[96,768]{1,0:T(8,128)(2,1)S(1)} %collective-permute-done.11.refs_0_, bf16[96,768]{1,0:T(8,128)(2,1)S(1)} %collective-permute-done.12.refs_1_, bf16[96,768]{1,0:T(8,128)(2,1)S(1)} %collective-permute-done.13.refs_2_, ...), custom_call_target="tpu_custom_call" | custom-call | tf_op jit(solution)/shard_map/pallas_call | solution.py:323
  (38 shorter events, 14.1 us)
Async XLA Ops:
  0.0 1.3 %copy-start.1 = (bf16[1,768,768]{2,1,0:T(8,128)(2,1)S(1)}, bf16[1,768,768]{2,1,0:T(8,128)(2,1)}, u32[]{:S(2)}) copy-start(bf16[1,768,768]{2,1,0:T(8,128)(2,1)} %param.5) | copy-start | bytes 3538948
  1.3 4.9 %copy-start = (bf16[1,768,768]{2,1,0:T(8,128)(2,1)S(1)}, bf16[1,768,768]{2,1,0:T(8,128)(2,1)}, u32[]{:S(2)}) copy-start(bf16[1,768,768]{2,1,0:T(8,128)(2,1)} %param.4) | copy-start | bytes 3538948
  1.3 4.9 %copy-start.2 = (f32[1,1536]{1,0:T(1,128)S(1)}, f32[1,1536]{1,0:T(1,128)}, u32[]{:S(2)}) copy-start(f32[1,1536]{1,0:T(1,128)} %bubble.11) | copy-start | bytes 18436
  1.6 4.5 %collective-permute-start.1 = (bf16[768,768]{1,0:T(8,128)(2,1)S(1)}, bf16[768,768]{1,0:T(8,128)(2,1)S(1)}, u32[]{:S(2)}, u32[]{:S(2)}) collective-permute-start(bf16[768,768]{1,0:T(8,128)(2,1)S(1)} %shard_map.48.flipped.refs_3_.refs_5_.refs_7_.refs_9_.refs_10_), channel_id=1, source_target_pairs={{0,2},{2,0},{1,3},{3,1},{4,6},{6,4},{5,7},{7,5},{8,10},{10,8},{9,1... | collective-permute-start | bytes 3538952 | tf_op jit(solution)/shard_map/ppermute | solution.py:17
  3.3 6.5 %collective-permute-start.5 = (bf16[128,768]{1,0:T(8,128)(2,1)S(1)}, bf16[128,768]{1,0:T(8,128)(2,1)S(1)}, u32[]{:S(2)}, u32[]{:S(2)}) collective-permute-start(bf16[128,768]{1,0:T(8,128)(2,1)S(1)} %shard_map.50), channel_id=1, source_target_pairs={{0,1},{1,0},{2,3},{3,2},{4,5},{5,4},{6,7},{7,6},{8,9},{9,8},{10,11... | collective-permute-start | bytes 589832 | tf_op jit(solution)/shard_map/ppermute | solution.py:17
  5.9 12.4 %collective-permute-start.4 = (bf16[256,768]{1,0:T(8,128)(2,1)S(1)}, bf16[256,768]{1,0:T(8,128)(2,1)S(1)}, u32[]{:S(2)}, u32[]{:S(2)}) collective-permute-start(bf16[256,768]{1,0:T(8,128)(2,1)S(1)} %get-tuple-element.38), channel_id=1, source_target_pairs={{0,1},{1,0},{2,3},{3,2},{4,5},{5,4},{6,7},{7,6},{8,9},{9,8},{10,11... | collective-permute-start | bytes 1179656 | tf_op jit(solution)/shard_map/ppermute | solution.py:17
  10.3 2.5 %collective-permute-start.7 = (bf16[768,128]{1,0:T(8,128)(2,1)S(1)}, bf16[768,128]{1,0:T(8,128)(2,1)S(1)}, u32[]{:S(2)}, u32[]{:S(2)}) collective-permute-start(bf16[768,128]{1,0:T(8,128)(2,1)S(1)} %get-tuple-element.51.refs_0_), channel_id=1, source_target_pairs={{0,2},{2,0},{1,3},{3,1},{4,6},{6,4},{5,7},{7,5},{8,10},{10,8},{9,1... | collective-permute-start | bytes 589832 | tf_op jit(solution)/shard_map/ppermute | solution.py:17
  18.8 2.3 %collective-permute-start.8 = (bf16[768,256]{1,0:T(8,128)(2,1)S(1)}, bf16[768,256]{1,0:T(8,128)(2,1)S(1)}, u32[]{:S(2)}, u32[]{:S(2)}) collective-permute-start(bf16[768,256]{1,0:T(8,128)(2,1)S(1)} %get-tuple-element.52.refs_1_), channel_id=1, source_target_pairs={{0,2},{2,0},{1,3},{3,1},{4,6},{6,4},{5,7},{7,5},{8,10},{10,8},{9,1... | collective-permute-start | bytes 1179656 | tf_op jit(solution)/shard_map/ppermute | solution.py:17
  19.7 6.4 %collective-permute-start.3 = (bf16[128,768]{1,0:T(8,128)(2,1)S(1)}, bf16[128,768]{1,0:T(8,128)(2,1)S(1)}, u32[]{:S(2)}, u32[]{:S(2)}) collective-permute-start(bf16[128,768]{1,0:T(8,128)(2,1)S(1)} %get-tuple-element.37), channel_id=1, source_target_pairs={{0,1},{1,0},{2,3},{3,2},{4,5},{5,4},{6,7},{7,6},{8,9},{9,8},{10,11... | collective-permute-start | bytes 589832 | tf_op jit(solution)/shard_map/ppermute | solution.py:17
  26.6 2.2 %collective-permute-start.9 = (bf16[768,128]{1,0:T(8,128)(2,1)S(1)}, bf16[768,128]{1,0:T(8,128)(2,1)S(1)}, u32[]{:S(2)}, u32[]{:S(2)}) collective-permute-start(bf16[768,128]{1,0:T(8,128)(2,1)S(1)} %get-tuple-element.53.refs_2_), channel_id=1, source_target_pairs={{0,2},{2,0},{1,3},{3,1},{4,6},{6,4},{5,7},{7,5},{8,10},{10,8},{9,1... | collective-permute-start | bytes 589832 | tf_op jit(solution)/shard_map/ppermute | solution.py:17
  27.6 6.4 %collective-permute-start.2 = (bf16[128,768]{1,0:T(8,128)(2,1)S(1)}, bf16[128,768]{1,0:T(8,128)(2,1)S(1)}, u32[]{:S(2)}, u32[]{:S(2)}) collective-permute-start(bf16[128,768]{1,0:T(8,128)(2,1)S(1)} %get-tuple-element.36), channel_id=1, source_target_pairs={{0,1},{1,0},{2,3},{3,2},{4,5},{5,4},{6,7},{7,6},{8,9},{9,8},{10,11... | collective-permute-start | bytes 589832 | tf_op jit(solution)/shard_map/ppermute | solution.py:17
  34.4 2.2 %collective-permute-start.10 = (bf16[768,128]{1,0:T(8,128)(2,1)S(1)}, bf16[768,128]{1,0:T(8,128)(2,1)S(1)}, u32[]{:S(2)}, u32[]{:S(2)}) collective-permute-start(bf16[768,128]{1,0:T(8,128)(2,1)S(1)} %get-tuple-element.54.refs_3_), channel_id=1, source_target_pairs={{0,2},{2,0},{1,3},{3,1},{4,6},{6,4},{5,7},{7,5},{8,10},{10,8},{9,1... | collective-permute-start | bytes 589832 | tf_op jit(solution)/shard_map/ppermute | solution.py:17
  35.4 6.4 %collective-permute-start = (bf16[128,768]{1,0:T(8,128)(2,1)S(1)}, bf16[128,768]{1,0:T(8,128)(2,1)S(1)}, u32[]{:S(2)}, u32[]{:S(2)}) collective-permute-start(bf16[128,768]{1,0:T(8,128)(2,1)S(1)} %get-tuple-element.34), channel_id=1, source_target_pairs={{0,1},{1,0},{2,3},{3,2},{4,5},{5,4},{6,7},{7,6},{8,9},{9,8},{10,11... | collective-permute-start | bytes 589832 | tf_op jit(solution)/shard_map/ppermute | solution.py:17
  42.3 2.1 %collective-permute-start.6 = (bf16[768,128]{1,0:T(8,128)(2,1)S(1)}, bf16[768,128]{1,0:T(8,128)(2,1)S(1)}, u32[]{:S(2)}, u32[]{:S(2)}) collective-permute-start(bf16[768,128]{1,0:T(8,128)(2,1)S(1)} %get-tuple-element.50.refs_4_), channel_id=1, source_target_pairs={{0,2},{2,0},{1,3},{3,1},{4,6},{6,4},{5,7},{7,5},{8,10},{10,8},{9,1... | collective-permute-start | bytes 589832 | tf_op jit(solution)/shard_map/ppermute | solution.py:17
  45.0 6.1 %collective-permute-start.12 = (bf16[96,768]{1,0:T(8,128)(2,1)S(1)}, bf16[96,768]{1,0:T(8,128)(2,1)S(1)}, u32[]{:S(2)}, u32[]{:S(2)}) collective-permute-start(bf16[96,768]{1,0:T(8,128)(2,1)S(1)} %get-tuple-element.56), channel_id=1, source_target_pairs={{0,16},{4,20},{8,24},{12,28},{16,0},{20,4},{24,8},{28,12},{1,17},{... | collective-permute-start | bytes 442376 | tf_op jit(solution)/shard_map/ppermute | solution.py:321
  45.1 9.3 %collective-permute-start.13 = (bf16[96,768]{1,0:T(8,128)(2,1)S(1)}, bf16[96,768]{1,0:T(8,128)(2,1)S(1)}, u32[]{:S(2)}, u32[]{:S(2)}) collective-permute-start(bf16[96,768]{1,0:T(8,128)(2,1)S(1)} %get-tuple-element.57), channel_id=1, source_target_pairs={{0,8},{4,12},{8,0},{12,4},{16,24},{20,28},{24,16},{28,20},{1,9},{5... | collective-permute-start | bytes 442376 | tf_op jit(solution)/shard_map/ppermute | solution.py:321
  46.4 14.1 %collective-permute-start.14 = (bf16[96,768]{1,0:T(8,128)(2,1)S(1)}, bf16[96,768]{1,0:T(8,128)(2,1)S(1)}, u32[]{:S(2)}, u32[]{:S(2)}) collective-permute-start(bf16[96,768]{1,0:T(8,128)(2,1)S(1)} %get-tuple-element.58), channel_id=1, source_target_pairs={{0,20},{4,16},{8,28},{12,24},{16,4},{20,0},{24,12},{28,8},{1,21},{... | collective-permute-start | bytes 442376 | tf_op jit(solution)/shard_map/ppermute | solution.py:321
  48.7 11.8 %collective-permute-start.15 = (bf16[96,768]{1,0:T(8,128)(2,1)S(1)}, bf16[96,768]{1,0:T(8,128)(2,1)S(1)}, u32[]{:S(2)}, u32[]{:S(2)}) collective-permute-start(bf16[96,768]{1,0:T(8,128)(2,1)S(1)} %get-tuple-element.59), channel_id=1, source_target_pairs={{0,24},{4,28},{8,12},{12,8},{16,20},{20,16},{24,0},{28,4},{1,25},{... | collective-permute-start | bytes 442376 | tf_op jit(solution)/shard_map/ppermute | solution.py:321
  49.9 4.6 %copy-start.3 = (s32[96,8]{0,1:T(8,128)S(1)}, s32[96,8]{0,1:T(8,128)}, u32[]{:S(2)}) copy-start(s32[96,8]{0,1:T(8,128)} %param.7) | copy-start | bytes 9220
  49.9 12.8 %collective-permute-start.16 = (bf16[96,768]{1,0:T(8,128)(2,1)S(1)}, bf16[96,768]{1,0:T(8,128)(2,1)S(1)}, u32[]{:S(2)}, u32[]{:S(2)}) collective-permute-start(bf16[96,768]{1,0:T(8,128)(2,1)S(1)} %get-tuple-element.60), channel_id=1, source_target_pairs={{0,12},{4,8},{8,4},{12,0},{16,28},{20,24},{24,20},{28,16},{1,13},{... | collective-permute-start | bytes 442376 | tf_op jit(solution)/shard_map/ppermute | solution.py:321
  51.1 19.6 %collective-permute-start.17 = (bf16[96,768]{1,0:T(8,128)(2,1)S(1)}, bf16[96,768]{1,0:T(8,128)(2,1)S(1)}, u32[]{:S(2)}, u32[]{:S(2)}) collective-permute-start(bf16[96,768]{1,0:T(8,128)(2,1)S(1)} %get-tuple-element.61), channel_id=1, source_target_pairs={{0,28},{4,24},{8,20},{12,16},{16,12},{20,8},{24,4},{28,0},{1,29},{... | collective-permute-start | bytes 442376 | tf_op jit(solution)/shard_map/ppermute | solution.py:321
  54.4 19.5 %collective-permute-start.11 = (bf16[96,768]{1,0:T(8,128)(2,1)S(1)}, bf16[96,768]{1,0:T(8,128)(2,1)S(1)}, u32[]{:S(2)}, u32[]{:S(2)}) collective-permute-start(bf16[96,768]{1,0:T(8,128)(2,1)S(1)} %shard_map.61), channel_id=1, source_target_pairs={{0,4},{4,0},{8,16},{12,20},{16,8},{20,12},{24,28},{28,24},{1,5},{5... | collective-permute-start | bytes 442376 | tf_op jit(solution)/shard_map/ppermute | solution.py:321

commit v6 on v5

--- a/solution.py
+++ b/solution.py
@@ -85,7 +85,8 @@
 
 
 def chunk_body(start, stop):
-    def body(far, bubble, other, _, __, halves, first, rounded):
+    def body(far, bubble, other, *refs):
+        halves, first, rounded = refs[-3:]
         col = 1 - lax.axis_index("col")
         half = far.shape[1]
         scale = bubble[:, pl.ds(pl.multiple_of(col * half, half), half)]
@@ -98,19 +99,18 @@
     return body
 
 
-def add_body(spans, i, final):
+def add_body(spans, i):
     def body(*refs):
         row = lax.axis_index("row")
-        count = i + 1
-        own, refs = refs[:count], refs[count:]
-        far, refs = refs[: count - final], refs[count - final :]
+        own, refs = refs[: i + 1], refs[i + 1 :]
+        far, refs = refs[:i], refs[i:]
         halves, flipped, first, total = refs[0], refs[1], refs[2], refs[-1]
         start, stop = spans[i]
-        for s, e in [(0, start)] if start else []:
-            part = total[:, s:e] + nt(own[i][...], halves[row, s:e, start:stop])
-            if not final:
-                part += nt(far[i][...], halves[1 - row, s:e, start:stop])
-            total[:, s:e] = part
+        if i:
+            s, e = spans[i - 1]
+            part = total[:, :start] + nt(own[i][...], halves[row, :start, start:stop])
+            part += nt(far[i - 1][...], halves[1 - row, :start, s:e])
+            total[:, :start] = part
         part = flipped[:, start:stop].astype(F32) + first[:, start:stop]
         for half, terms in ((row, own), (1 - row, far)):
             for term, (s, e) in zip(terms, spans):
@@ -120,16 +120,86 @@
     return body
 
 
-def last_body(span, steps):
-    def body(halves, far, total, *outs):
+def settle_body(span):
+    def body(halves, far, _, total):
+        other = 1 - lax.axis_index("row")
+        s, e = span
+        total[:, :e] += nt(far[...], halves[other, :e, s:e])
+
+    return body
+
+
+def peek_body(step, start):
+    def body(far, bubble, other, first, out):
+        col, mom = 1 - lax.axis_index("col"), lax.axis_index("mom")
+        half, size = far.shape[1], out.shape[0]
+        scale = bubble[:, pl.ds(pl.multiple_of(col * half, half), half)]
+        scaled = (far[...].astype(F32) * scale).astype(BF)
+        lines = pl.ds(pl.multiple_of(meet(mom, step) * size, size), size)
+        out[...] = (first[lines, start:] + nt(other[lines, :], scaled)).astype(BF)
+
+    return body
+
+
+def own_body(spans, step):
+    def body(*refs):
         row, mom = lax.axis_index("row"), lax.axis_index("mom")
+        count = len(spans)
+        own, far, refs = refs[:count], refs[count : 2 * count - 1], refs[2 * count - 1 :]
+        halves, flipped, first, total, size_like, out = refs
+        start, stop = spans[-1]
+        size = size_like.shape[0]
+        lines = pl.ds(pl.multiple_of(meet(mom, step) * size, size), size)
+        out[:, :start] = total[lines, :start] + nt(
+            own[-1][lines, :], halves[row, :start, start:stop]
+        )
+        part = flipped[lines, start:stop].astype(F32) + first[lines, start:stop]
+        for half, terms in ((row, own), (1 - row, far)):
+            for term, (s, e) in zip(terms, spans):
+                part += nt(term[lines, :], halves[half, start:stop, s:e])
+        out[:, start:] = part
+
+    return body
+
+
+def close_body(span):
+    def body(halves, last, part, out):
         s, e = span
+        weights = halves[1 - lax.axis_index("row"), :, s:e]
+        out[...] = (part[...] + nt(last[...], weights)).astype(BF)
+
+    return body
+
+
+def finish_body(spans, steps):
+    def body(*refs):
+        row, mom = lax.axis_index("row"), lax.axis_index("mom")
+        count = len(spans)
+        own, far, refs = refs[:count], refs[count : 2 * count], refs[2 * count :]
+        halves, flipped, first, total = refs[:4]
+        outs = refs[4:]
+        start, stop = spans[-1]
         size = outs[0].shape[0]
-        weights = halves[1 - row, :, s:e]
-        for out, step in zip(outs, steps):
-            begin = pl.multiple_of(meet(mom, step) * size, size)
-            lines = pl.ds(begin, size)
-            out[...] = (total[lines, :] + nt(far[lines, :], weights)).astype(BF)
+        done = None
+        if len(steps) > 2:
+            outs, done = outs[:-1], outs[-1]
+        blocks = [done] if done is not None else outs
+        for out, step in zip(blocks, steps):
+            begin = 0 if done is not None else meet(mom, step) * size
+            lines = pl.ds(pl.multiple_of(begin, size), out.shape[0])
+            part = total[lines, :start]
+            part += nt(own[-1][lines, :], halves[row, :start, start:stop])
+            part += nt(far[-1][lines, :], halves[1 - row, :start, start:stop])
+            out[:, :start] = part.astype(BF)
+            part = flipped[lines, start:stop].astype(F32) + first[lines, start:stop]
+            for half, terms in ((row, own), (1 - row, far)):
+                for term, (s, e) in zip(terms, spans):
+                    part += nt(term[lines, :], halves[half, start:stop, s:e])
+            out[:, start:] = part.astype(BF)
+        if done is not None:
+            for out, step in zip(outs, steps):
+                begin = pl.multiple_of(meet(mom, step) * size, size)
+                out[...] = done[pl.ds(begin, size), :]
 
     return body
 
@@ -150,14 +220,17 @@
                     i * group : (i + 1) * group, :
                 ]
             span = slice(i * size, (i + 1) * size)
-            result[span, :] = jnp.dot(
-                pick[span, :], gathered[i], preferred_element_type=F32
-            ).astype(BF)
-            copy = pltpu.make_async_copy(
-                result.at[span, :], out.at[span, :], sem.at[i]
-            )
-            copy.start()
-            copies.append(copy)
+            width = out.shape[1] // 2
+            for j in range(2):
+                lanes = slice(j * width, (j + 1) * width)
+                result[span, lanes] = jnp.dot(
+                    pick[span, :], gathered[i, :, lanes], preferred_element_type=F32
+                ).astype(BF)
+                copy = pltpu.make_async_copy(
+                    result.at[span, lanes], out.at[span, lanes], sem.at[2 * i + j]
+                )
+                copy.start()
+                copies.append(copy)
         for copy in copies:
             copy.wait()
 
@@ -182,7 +255,7 @@
         far = momenta - 2
         mixed = [(1, far), (far, 1)]
         steps = [k for k in steps if k[0] not in (1, far)]
-        steps = mixed[:1] + [(4, 4), (2, 2), (5, 5)] + mixed[1:] + [(3, 3), (7, 7)]
+        steps = mixed[:1] + [(4, 4), (2, 2), (5, 5), (3, 3)] + mixed[1:] + [(7, 7)]
     return steps
 
 
@@ -274,8 +347,22 @@
     pick = local(
         pick_body(group), pltpu.VMEM((columns, momenta * group), BF), cross_map.T
     )
+    order = steps_of(momenta) + [(0, 0)]
     own, others, total = [], [], None
     for i, (s, e) in enumerate(spans):
+        extra = []
+        if e == rows:
+            peeked = local(
+                peek_body(order[0], s),
+                pltpu.VMEM((per_device, e - s), BF),
+                fars[i],
+                bubble,
+                other,
+                first,
+                flops=square * (e - s) // momenta,
+            )
+            ahead = swap(peeked, "row")
+            extra = [peeked]
         halves, first, rounded = local(
             chunk_body(s, e),
             [
@@ -288,32 +375,69 @@
             other,
             halves,
             first,
+            *extra,
             aliases={3: 0, 4: 1},
             flops=square * (e - s),
         )
         own.append(rounded)
         others.append(swap(rounded, "row"))
-        final = e == rows
-        inputs = [*own, *others[: len(own) - final], halves, flipped, first]
+        if e == rows:
+            break
+        inputs = [*own, *others[:i], halves, flipped, first]
         total = local(
-            add_body(spans, i, final),
+            add_body(spans, i),
             pltpu.VMEM((columns, rows), F32),
             *inputs,
             *([] if total is None else [total]),
             aliases={} if total is None else {len(inputs): 0},
             flops=square * 2 * (e - s),
         )
-
-    order = steps_of(momenta) + [(0, 0)]
-    sent = []
-    for chosen in (order[:1], order[1:]):
+        if i == len(spans) - 2:
+            total = local(
+                settle_body(spans[i]),
+                pltpu.VMEM((columns, rows), F32),
+                halves,
+                others[i],
+                total,
+                aliases={2: 0},
+                flops=square * (e - s),
+            )
+
+    part = local(
+        own_body(spans, order[0]),
+        pltpu.VMEM((per_device, rows), F32),
+        *own,
+        *others[:-1],
+        halves,
+        flipped,
+        first,
+        total,
+        peeked,
+        flops=square * unit // momenta,
+    )
+    sent = [
+        local(
+            close_body(spans[-1]),
+            pltpu.VMEM((per_device, rows), BF),
+            halves,
+            ahead,
+            part,
+            flops=square * unit // momenta,
+        )
+    ]
+    for chosen in (order[1:2], order[2:]):
+        scratch = [pltpu.VMEM((columns, rows), BF)] if len(chosen) > 2 else []
         sent += local(
-            last_body(spans[-1], chosen),
+            finish_body(spans, chosen),
             [pltpu.VMEM((per_device, rows), BF)] * len(chosen),
+            *own,
+            *others,
             halves,
-            others[-1],
+            flipped,
+            first,
             total,
             flops=square * unit * len(chosen) // momenta,
+            scratch=scratch,
         )
     got = []
     for block, step in zip(sent, order[:-1]):
@@ -328,7 +452,7 @@
         scratch_shapes=[
             pltpu.VMEM((per_device // group, momenta * group, rows), BF),
             pltpu.VMEM((columns, rows), BF),
-            pltpu.SemaphoreType.DMA((per_device // group,)),
+            pltpu.SemaphoreType.DMA((2 * per_device // group,)),
         ],
         compiler_params=LIMIT,
     )(*[pltpu.with_memory_space_constraint(a, pltpu.VMEM) for a in arrays])

time: 75.4 us -> 74.2 us (0.984)
  the two profiles are of different devices: /device:TPU:19 before, /device:TPU:0 now
where the time goes in v6:
time: 74.2 us; the launch traced here: 74 us
  waiting for transfers between devices  38.4 us (52%)
  starting transfers between devices  20.2 us (27%)
  Pallas kernels  13.9 us (19%)
  local copies, waits for them, and re-layouts  1.28 us (2%)
    ppermute x12, waiting for transfers between devices, swap(): return lax.ppermute(value, axis, [(0, 1), (1, 0)])  21 us
    ppermute x7, waiting for transfers between devices, tiled(): got.append(lax.ppermute(block, 'mom', pairs))  17.4 us
    ppermute x7, starting transfers between devices, tiled(): got.append(lax.ppermute(block, 'mom', pairs))  11.9 us
    pallas_call x18, Pallas kernels, local(): pl.pallas_call(body, out_shape=outs, in_specs=[VMEM] * len(arrays), out_s...  10.4 us
    ppermute x12, starting transfers between devices, swap(): return lax.ppermute(value, axis, [(0, 1), (1, 0)])  8.26 us
    pallas_call x2, Pallas kernels, fetch(): pl.pallas_call(body, out_shape=[pltpu.VMEM((e - s, array.shape[1]), array...  2.17 us
  transfers between devices with their start and end apart: 19, of which 9 were waited for; matrix products, arithmetic and copies ran while one was open for 0% of the time, Pallas kernels for 15%

profile of v6, /device:TPU:0, one launch (start us, length us, event | category | flops | bytes accessed | tf_op | source)
XLA Modules:
  0.0 74.0 jit_solution(16129710724184376247)
XLA Ops:
  0.0 1.3 %copy-done.1 = bf16[1,768,768]{2,1,0:T(8,128)(2,1)S(1)} copy-done((bf16[1,768,768]{2,1,0:T(8,128)(2,1)S(1)}, bf16[1,768,768]{2,1,0:T(8,128)(2,1)}, u32[]{:S(2)}) %copy-start.1) | copy-done | bytes 1179672
  2.2 1.2 %shard_map.47 = (bf16[256,768]{1,0:T(8,128)(2,1)S(1)}, bf16[128,768]{1,0:T(8,128)(2,1)S(1)}, bf16[128,768]{1,0:T(8,128)(2,1)S(1)}, bf16[128,768]{1,0:T(8,128)(2,1)S(1)}) custom-call(bf16[768,768]{1,0:T(8,128)(2,1)} %bitcast.4), custom_call_target="tpu_custom_call" | custom-call | tf_op jit(solution)/shard_map/pallas_call | solution.py:55
  3.4 2.6 %collective-permute-start.4 = (bf16[256,768]{1,0:T(8,128)(2,1)S(1)}, bf16[256,768]{1,0:T(8,128)(2,1)S(1)}, u32[]{:S(2)}, u32[]{:S(2)}) collective-permute-start(bf16[256,768]{1,0:T(8,128)(2,1)S(1)} %get-tuple-element.37), channel_id=1, source_target_pairs={{0,1},{1,0},{2,3},{3,2},{4,5},{5,4},{6,7},{7,6},{8,9},{9,8},{10,11... | collective-permute-start | bytes 1179656 | tf_op jit(solution)/shard_map/ppermute | solution.py:17
  6.0 0.9 %shard_map.50 = bf16[128,768]{1,0:T(8,128)(2,1)S(1)} custom-call(bf16[768,768]{1,0:T(8,128)(2,1)} %bitcast.5), custom_call_target="tpu_custom_call" | custom-call | tf_op jit(solution)/shard_map/pallas_call | solution.py:55
  7.1 1.4 %shard_map.49 = (bf16[2,768,768]{2,1,0:T(8,128)(2,1)S(1)}, f32[768,768]{1,0:T(8,128)S(1)}, bf16[768,768]{1,0:T(8,128)(2,1)S(1)}) custom-call(bf16[768,768]{1,0:T(8,128)(2,1)S(1)} %bitcast.6, f32[1,1536]{1,0:T(1,128)S(1)} %copy-done.2, bf16[768,768]{1,0:T(8,128)(2,1)S(1)} %shard_map.48.flipped.refs_2_.refs_4_.refs_6_.refs_8_.refs_10_.refs_11_, ...), custom_call_target="tpu_custom_call" | custom-call | flops 905969664 | bytes 1048576 | tf_op jit(solution)/shard_map/pallas_call | solution.py:29
  8.5 11.5 %collective-permute-done.5.far = bf16[128,768]{1,0:T(8,128)(2,1)S(1)} collective-permute-done((bf16[128,768]{1,0:T(8,128)(2,1)S(1)}, bf16[128,768]{1,0:T(8,128)(2,1)S(1)}, u32[]{:S(2)}, u32[]{:S(2)}) %collective-permute-start.5) | collective-permute-done | bytes 196640 | tf_op jit(solution)/shard_map/ppermute | solution.py:17
  21.8 1.7 %collective-permute-start.3 = (bf16[128,768]{1,0:T(8,128)(2,1)S(1)}, bf16[128,768]{1,0:T(8,128)(2,1)S(1)}, u32[]{:S(2)}, u32[]{:S(2)}) collective-permute-start(bf16[128,768]{1,0:T(8,128)(2,1)S(1)} %get-tuple-element.36), channel_id=1, source_target_pairs={{0,1},{1,0},{2,3},{3,2},{4,5},{5,4},{6,7},{7,6},{8,9},{9,8},{10,11... | collective-permute-start | bytes 589832 | tf_op jit(solution)/shard_map/ppermute | solution.py:17
  23.9 1.7 %collective-permute-start = (bf16[128,768]{1,0:T(8,128)(2,1)S(1)}, bf16[128,768]{1,0:T(8,128)(2,1)S(1)}, u32[]{:S(2)}, u32[]{:S(2)}) collective-permute-start(bf16[128,768]{1,0:T(8,128)(2,1)S(1)} %get-tuple-element.33), channel_id=1, source_target_pairs={{0,1},{1,0},{2,3},{3,2},{4,5},{5,4},{6,7},{7,6},{8,9},{9,8},{10,11... | collective-permute-start | bytes 589832 | tf_op jit(solution)/shard_map/ppermute | solution.py:17
  26.3 3.4 %collective-permute-done.3.far = bf16[128,768]{1,0:T(8,128)(2,1)S(1)} collective-permute-done((bf16[128,768]{1,0:T(8,128)(2,1)S(1)}, bf16[128,768]{1,0:T(8,128)(2,1)S(1)}, u32[]{:S(2)}, u32[]{:S(2)}) %collective-permute-start.3) | collective-permute-done | bytes 196640 | tf_op jit(solution)/shard_map/ppermute | solution.py:17
  31.1 2.7 %collective-permute-done.2.far = bf16[128,768]{1,0:T(8,128)(2,1)S(1)} collective-permute-done((bf16[128,768]{1,0:T(8,128)(2,1)S(1)}, bf16[128,768]{1,0:T(8,128)(2,1)S(1)}, u32[]{:S(2)}, u32[]{:S(2)}) %collective-permute-start.2) | collective-permute-done | bytes 196640 | tf_op jit(solution)/shard_map/ppermute | solution.py:17
  34.4 2.8 %collective-permute-done.far = bf16[128,768]{1,0:T(8,128)(2,1)S(1)} collective-permute-done((bf16[128,768]{1,0:T(8,128)(2,1)S(1)}, bf16[128,768]{1,0:T(8,128)(2,1)S(1)}, u32[]{:S(2)}, u32[]{:S(2)}) %collective-permute-start) | collective-permute-done | bytes 196640 | tf_op jit(solution)/shard_map/ppermute | solution.py:17
  37.4 1.1 %shard_map.60._ = f32[768,768]{1,0:T(8,128)S(1)} custom-call(bf16[768,128]{1,0:T(8,128)(2,1)S(1)} %get-tuple-element.49.refs_0_, bf16[768,256]{1,0:T(8,128)(2,1)S(1)} %get-tuple-element.50.refs_1_, bf16[768,128]{1,0:T(8,128)(2,1)S(1)} %get-tuple-element.51.refs_2_, bf16[768,128]{1,0:T(8,128)(2,1)S(1)} %get-tuple-element.52.refs_3_, ...), custom_call_target="tpu_custom_call", output_to_operand_aliasing={{}: (10, {})} | custom-call | flops 301989888 | bytes 1048576 | tf_op jit(solution)/shard_map/pallas_call | solution.py:29
  41.1 1.8 %collective-permute-start.11 = (bf16[96,768]{1,0:T(8,128)(2,1)S(1)}, bf16[96,768]{1,0:T(8,128)(2,1)S(1)}, u32[]{:S(2)}, u32[]{:S(2)}) collective-permute-start(bf16[96,768]{1,0:T(8,128)(2,1)S(1)} %shard_map.63), channel_id=1, source_target_pairs={{0,4},{4,0},{8,16},{12,20},{16,8},{20,12},{24,28},{28,24},{1,5},{5... | collective-permute-start | bytes 442376 | tf_op jit(solution)/shard_map/ppermute | solution.py:445
  42.9 1.4 %shard_map.65 = (bf16[96,768]{1,0:T(8,128)(2,1)S(1)}, bf16[96,768]{1,0:T(8,128)(2,1)S(1)}, bf16[96,768]{1,0:T(8,128)(2,1)S(1)}, bf16[96,768]{1,0:T(8,128)(2,1)S(...) custom-call(bf16[768,128]{1,0:T(8,128)(2,1)S(1)} %get-tuple-element.49.refs_0_, ...), custom_call_target="tpu_custom_call" | custom-call | flops 113246208 | bytes 1048576 | tf_op jit(solution)/shard_map/pallas_call | solution.py:29
  44.3 1.7 %collective-permute-start.14 = (bf16[96,768]{1,0:T(8,128)(2,1)S(1)}, bf16[96,768]{1,0:T(8,128)(2,1)S(1)}, u32[]{:S(2)}, u32[]{:S(2)}) collective-permute-start(bf16[96,768]{1,0:T(8,128)(2,1)S(1)} %get-tuple-element.55), channel_id=1, source_target_pairs={{0,8},{4,12},{8,0},{12,4},{16,24},{20,28},{24,16},{28,20},{1,9},{5... | collective-permute-start | bytes 442376 | tf_op jit(solution)/shard_map/ppermute | solution.py:445
  46.0 2.5 %collective-permute-start.15 = (bf16[96,768]{1,0:T(8,128)(2,1)S(1)}, bf16[96,768]{1,0:T(8,128)(2,1)S(1)}, u32[]{:S(2)}, u32[]{:S(2)}) collective-permute-start(bf16[96,768]{1,0:T(8,128)(2,1)S(1)} %get-tuple-element.56), channel_id=1, source_target_pairs={{0,20},{4,16},{8,28},{12,24},{16,4},{20,0},{24,12},{28,8},{1,21},{... | collective-permute-start | bytes 442376 | tf_op jit(solution)/shard_map/ppermute | solution.py:445
  48.5 1.0 %collective-permute-start.16 = (bf16[96,768]{1,0:T(8,128)(2,1)S(1)}, bf16[96,768]{1,0:T(8,128)(2,1)S(1)}, u32[]{:S(2)}, u32[]{:S(2)}) collective-permute-start(bf16[96,768]{1,0:T(8,128)(2,1)S(1)} %get-tuple-element.57), channel_id=1, source_target_pairs={{0,12},{4,8},{8,4},{12,0},{16,28},{20,24},{24,20},{28,16},{1,13},{... | collective-permute-start | bytes 442376 | tf_op jit(solution)/shard_map/ppermute | solution.py:445
  49.5 1.8 %collective-permute-start.17 = (bf16[96,768]{1,0:T(8,128)(2,1)S(1)}, bf16[96,768]{1,0:T(8,128)(2,1)S(1)}, u32[]{:S(2)}, u32[]{:S(2)}) collective-permute-start(bf16[96,768]{1,0:T(8,128)(2,1)S(1)} %get-tuple-element.58), channel_id=1, source_target_pairs={{0,24},{4,28},{8,12},{12,8},{16,20},{20,16},{24,0},{28,4},{1,25},{... | collective-permute-start | bytes 442376 | tf_op jit(solution)/shard_map/ppermute | solution.py:445
  51.8 2.3 %collective-permute-start.18 = (bf16[96,768]{1,0:T(8,128)(2,1)S(1)}, bf16[96,768]{1,0:T(8,128)(2,1)S(1)}, u32[]{:S(2)}, u32[]{:S(2)}) collective-permute-start(bf16[96,768]{1,0:T(8,128)(2,1)S(1)} %get-tuple-element.59), channel_id=1, source_target_pairs={{0,28},{4,24},{8,20},{12,16},{16,12},{20,8},{24,4},{28,0},{1,29},{... | collective-permute-start | bytes 442376 | tf_op jit(solution)/shard_map/ppermute | solution.py:445
  55.3 2.2 %collective-permute-done.15.refs_3_ = bf16[96,768]{1,0:T(8,128)(2,1)S(1)} collective-permute-done((bf16[96,768]{1,0:T(8,128)(2,1)S(1)}, bf16[96,768]{1,0:T(8,128)(2,1)S(1)}, u32[]{:S(2)}, u32[]{:S(2)}) %collective-permute-start.15) | collective-permute-done | bytes 147488 | tf_op jit(solution)/shard_map/ppermute | solution.py:445
  57.5 5.7 %collective-permute-done.17.refs_5_ = bf16[96,768]{1,0:T(8,128)(2,1)S(1)} collective-permute-done((bf16[96,768]{1,0:T(8,128)(2,1)S(1)}, bf16[96,768]{1,0:T(8,128)(2,1)S(1)}, u32[]{:S(2)}, u32[]{:S(2)}) %collective-permute-start.17) | collective-permute-done | bytes 147488 | tf_op jit(solution)/shard_map/ppermute | solution.py:445
  63.2 3.3 %collective-permute-done.18.refs_6_ = bf16[96,768]{1,0:T(8,128)(2,1)S(1)} collective-permute-done((bf16[96,768]{1,0:T(8,128)(2,1)S(1)}, bf16[96,768]{1,0:T(8,128)(2,1)S(1)}, u32[]{:S(2)}, u32[]{:S(2)}) %collective-permute-start.18) | collective-permute-done | bytes 147488 | tf_op jit(solution)/shard_map/ppermute | solution.py:445
  66.4 6.3 %collective-permute-done.13.refs_1_ = bf16[96,768]{1,0:T(8,128)(2,1)S(1)} collective-permute-done((bf16[96,768]{1,0:T(8,128)(2,1)S(1)}, bf16[96,768]{1,0:T(8,128)(2,1)S(1)}, u32[]{:S(2)}, u32[]{:S(2)}) %collective-permute-start.13) | collective-permute-done | bytes 147488 | tf_op jit(solution)/shard_map/ppermute | solution.py:445
  72.7 1.3 %shard_map.66 = bf16[768,768]{1,0:T(8,128)(2,1)} custom-call(bf16[768,256]{1,0:T(8,128)(2,1)S(1)} %shard_map.46.pick, bf16[96,768]{1,0:T(8,128)(2,1)S(1)} %collective-permute-done.11.refs_0_, bf16[96,768]{1,0:T(8,128)(2,1)S(1)} %collective-permute-done.13.refs_1_, bf16[96,768]{1,0:T(8,128)(2,1)S(1)} %collective-permute-done.14.refs_2_, ...), custom_call_target="tpu_custom_call" | custom-call | tf_op jit(solution)/shard_map/pallas_call | solution.py:447
  (43 shorter events, 10.2 us)
Async XLA Ops:
  0.0 1.3 %copy-start.1 = (bf16[1,768,768]{2,1,0:T(8,128)(2,1)S(1)}, bf16[1,768,768]{2,1,0:T(8,128)(2,1)}, u32[]{:S(2)}) copy-start(bf16[1,768,768]{2,1,0:T(8,128)(2,1)} %param.5) | copy-start | bytes 3538948
  1.3 5.8 %copy-start = (bf16[1,768,768]{2,1,0:T(8,128)(2,1)S(1)}, bf16[1,768,768]{2,1,0:T(8,128)(2,1)}, u32[]{:S(2)}) copy-start(bf16[1,768,768]{2,1,0:T(8,128)(2,1)} %param.4) | copy-start | bytes 3538948
  1.3 5.8 %copy-start.2 = (f32[1,1536]{1,0:T(1,128)S(1)}, f32[1,1536]{1,0:T(1,128)}, u32[]{:S(2)}) copy-start(f32[1,1536]{1,0:T(1,128)} %bubble.13) | copy-start | bytes 18436
  1.6 5.4 %collective-permute-start.1 = (bf16[768,768]{1,0:T(8,128)(2,1)S(1)}, bf16[768,768]{1,0:T(8,128)(2,1)S(1)}, u32[]{:S(2)}, u32[]{:S(2)}) collective-permute-start(bf16[768,768]{1,0:T(8,128)(2,1)S(1)} %shard_map.48.flipped.refs_2_.refs_4_.refs_6_.refs_8_.refs_10_.refs_11_), channel_id=1, source_target_pairs={{0,2},{2,0},{1,3},{3,1},{4,6},{6,4},{5,7},{7,5},{8,10},{10,8},{9,1... | collective-permute-start | bytes 3538952 | tf_op jit(solution)/shard_map/ppermute | solution.py:17
  3.4 17.3 %collective-permute-start.4 = (bf16[256,768]{1,0:T(8,128)(2,1)S(1)}, bf16[256,768]{1,0:T(8,128)(2,1)S(1)}, u32[]{:S(2)}, u32[]{:S(2)}) collective-permute-start(bf16[256,768]{1,0:T(8,128)(2,1)S(1)} %get-tuple-element.37), channel_id=1, source_target_pairs={{0,1},{1,0},{2,3},{3,2},{4,5},{5,4},{6,7},{7,6},{8,9},{9,8},{10,11... | collective-permute-start | bytes 1179656 | tf_op jit(solution)/shard_map/ppermute | solution.py:17
  7.0 13.0 %collective-permute-start.5 = (bf16[128,768]{1,0:T(8,128)(2,1)S(1)}, bf16[128,768]{1,0:T(8,128)(2,1)S(1)}, u32[]{:S(2)}, u32[]{:S(2)}) collective-permute-start(bf16[128,768]{1,0:T(8,128)(2,1)S(1)} %shard_map.50), channel_id=1, source_target_pairs={{0,1},{1,0},{2,3},{3,2},{4,5},{5,4},{6,7},{7,6},{8,9},{9,8},{10,11... | collective-permute-start | bytes 589832 | tf_op jit(solution)/shard_map/ppermute | solution.py:17
  21.3 8.9 %collective-permute-start.8 = (bf16[768,256]{1,0:T(8,128)(2,1)S(1)}, bf16[768,256]{1,0:T(8,128)(2,1)S(1)}, u32[]{:S(2)}, u32[]{:S(2)}) collective-permute-start(bf16[768,256]{1,0:T(8,128)(2,1)S(1)} %get-tuple-element.50.refs_1_), channel_id=1, source_target_pairs={{0,2},{2,0},{1,3},{3,1},{4,6},{6,4},{5,7},{7,5},{8,10},{10,8},{9,1... | collective-permute-start | bytes 1179656 | tf_op jit(solution)/shard_map/ppermute | solution.py:17
  21.3 4.3 %collective-permute-start.7 = (bf16[768,128]{1,0:T(8,128)(2,1)S(1)}, bf16[768,128]{1,0:T(8,128)(2,1)S(1)}, u32[]{:S(2)}, u32[]{:S(2)}) collective-permute-start(bf16[768,128]{1,0:T(8,128)(2,1)S(1)} %get-tuple-element.49.refs_0_), channel_id=1, source_target_pairs={{0,2},{2,0},{1,3},{3,1},{4,6},{6,4},{5,7},{7,5},{8,10},{10,8},{9,1... | collective-permute-start | bytes 589832 | tf_op jit(solution)/shard_map/ppermute | solution.py:17
  21.8 7.8 %collective-permute-start.3 = (bf16[128,768]{1,0:T(8,128)(2,1)S(1)}, bf16[128,768]{1,0:T(8,128)(2,1)S(1)}, u32[]{:S(2)}, u32[]{:S(2)}) collective-permute-start(bf16[128,768]{1,0:T(8,128)(2,1)S(1)} %get-tuple-element.36), channel_id=1, source_target_pairs={{0,1},{1,0},{2,3},{3,2},{4,5},{5,4},{6,7},{7,6},{8,9},{9,8},{10,11... | collective-permute-start | bytes 589832 | tf_op jit(solution)/shard_map/ppermute | solution.py:17
  23.6 10.3 %collective-permute-start.2 = (bf16[128,768]{1,0:T(8,128)(2,1)S(1)}, bf16[128,768]{1,0:T(8,128)(2,1)S(1)}, u32[]{:S(2)}, u32[]{:S(2)}) collective-permute-start(bf16[128,768]{1,0:T(8,128)(2,1)S(1)} %get-tuple-element.35), channel_id=1, source_target_pairs={{0,1},{1,0},{2,3},{3,2},{4,5},{5,4},{6,7},{7,6},{8,9},{9,8},{10,11... | collective-permute-start | bytes 589832 | tf_op jit(solution)/shard_map/ppermute | solution.py:17
  23.9 13.3 %collective-permute-start = (bf16[128,768]{1,0:T(8,128)(2,1)S(1)}, bf16[128,768]{1,0:T(8,128)(2,1)S(1)}, u32[]{:S(2)}, u32[]{:S(2)}) collective-permute-start(bf16[128,768]{1,0:T(8,128)(2,1)S(1)} %get-tuple-element.33), channel_id=1, source_target_pairs={{0,1},{1,0},{2,3},{3,2},{4,5},{5,4},{6,7},{7,6},{8,9},{9,8},{10,11... | collective-permute-start | bytes 589832 | tf_op jit(solution)/shard_map/ppermute | solution.py:17
  30.1 7.3 %collective-permute-start.9 = (bf16[768,128]{1,0:T(8,128)(2,1)S(1)}, bf16[768,128]{1,0:T(8,128)(2,1)S(1)}, u32[]{:S(2)}, u32[]{:S(2)}) collective-permute-start(bf16[768,128]{1,0:T(8,128)(2,1)S(1)} %get-tuple-element.51.refs_2_), channel_id=1, source_target_pairs={{0,2},{2,0},{1,3},{3,1},{4,6},{6,4},{5,7},{7,5},{8,10},{10,8},{9,1... | collective-permute-start | bytes 589832 | tf_op jit(solution)/shard_map/ppermute | solution.py:17
  34.3 4.1 %collective-permute-start.10 = (bf16[768,128]{1,0:T(8,128)(2,1)S(1)}, bf16[768,128]{1,0:T(8,128)(2,1)S(1)}, u32[]{:S(2)}, u32[]{:S(2)}) collective-permute-start(bf16[768,128]{1,0:T(8,128)(2,1)S(1)} %get-tuple-element.52.refs_3_), channel_id=1, source_target_pairs={{0,2},{2,0},{1,3},{3,1},{4,6},{6,4},{5,7},{7,5},{8,10},{10,8},{9,1... | collective-permute-start | bytes 589832 | tf_op jit(solution)/shard_map/ppermute | solution.py:17
  39.4 3.5 %collective-permute-start.12 = (bf16[768,128]{1,0:T(8,128)(2,1)S(1)}, bf16[768,128]{1,0:T(8,128)(2,1)S(1)}, u32[]{:S(2)}, u32[]{:S(2)}) collective-permute-start(bf16[768,128]{1,0:T(8,128)(2,1)S(1)} %get-tuple-element.53.refs_4_), channel_id=1, source_target_pairs={{0,2},{2,0},{1,3},{3,1},{4,6},{6,4},{5,7},{7,5},{8,10},{10,8},{9,1... | collective-permute-start | bytes 589832 | tf_op jit(solution)/shard_map/ppermute | solution.py:17
  39.5 1.5 %collective-permute-start.6 = (bf16[96,128]{1,0:T(8,128)(2,1)S(1)}, bf16[96,128]{1,0:T(8,128)(2,1)S(1)}, u32[]{:S(2)}, u32[]{:S(2)}) collective-permute-start(bf16[96,128]{1,0:T(8,128)(2,1)S(1)} %shard_map.55.refs_2_.refs_13_), channel_id=1, source_target_pairs={{0,2},{2,0},{1,3},{3,1},{4,6},{6,4},{5,7},{7,5},{8,10},{10,8},{9,1... | collective-permute-start | bytes 73736 | tf_op jit(solution)/shard_map/ppermute | solution.py:17
  41.1 10.6 %collective-permute-start.11 = (bf16[96,768]{1,0:T(8,128)(2,1)S(1)}, bf16[96,768]{1,0:T(8,128)(2,1)S(1)}, u32[]{:S(2)}, u32[]{:S(2)}) collective-permute-start(bf16[96,768]{1,0:T(8,128)(2,1)S(1)} %shard_map.63), channel_id=1, source_target_pairs={{0,4},{4,0},{8,16},{12,20},{16,8},{20,12},{24,28},{28,24},{1,5},{5... | collective-permute-start | bytes 442376 | tf_op jit(solution)/shard_map/ppermute | solution.py:445
  44.3 9.8 %collective-permute-start.14 = (bf16[96,768]{1,0:T(8,128)(2,1)S(1)}, bf16[96,768]{1,0:T(8,128)(2,1)S(1)}, u32[]{:S(2)}, u32[]{:S(2)}) collective-permute-start(bf16[96,768]{1,0:T(8,128)(2,1)S(1)} %get-tuple-element.55), channel_id=1, source_target_pairs={{0,8},{4,12},{8,0},{12,4},{16,24},{20,28},{24,16},{28,20},{1,9},{5... | collective-permute-start | bytes 442376 | tf_op jit(solution)/shard_map/ppermute | solution.py:445
  46.0 11.5 %collective-permute-start.15 = (bf16[96,768]{1,0:T(8,128)(2,1)S(1)}, bf16[96,768]{1,0:T(8,128)(2,1)S(1)}, u32[]{:S(2)}, u32[]{:S(2)}) collective-permute-start(bf16[96,768]{1,0:T(8,128)(2,1)S(1)} %get-tuple-element.56), channel_id=1, source_target_pairs={{0,20},{4,16},{8,28},{12,24},{16,4},{20,0},{24,12},{28,8},{1,21},{... | collective-permute-start | bytes 442376 | tf_op jit(solution)/shard_map/ppermute | solution.py:445
  48.5 9.0 %collective-permute-start.16 = (bf16[96,768]{1,0:T(8,128)(2,1)S(1)}, bf16[96,768]{1,0:T(8,128)(2,1)S(1)}, u32[]{:S(2)}, u32[]{:S(2)}) collective-permute-start(bf16[96,768]{1,0:T(8,128)(2,1)S(1)} %get-tuple-element.57), channel_id=1, source_target_pairs={{0,12},{4,8},{8,4},{12,0},{16,28},{20,24},{24,20},{28,16},{1,13},{... | collective-permute-start | bytes 442376 | tf_op jit(solution)/shard_map/ppermute | solution.py:445
  49.5 5.4 %copy-start.3 = (s32[96,8]{0,1:T(8,128)S(1)}, s32[96,8]{0,1:T(8,128)}, u32[]{:S(2)}) copy-start(s32[96,8]{0,1:T(8,128)} %param.7) | copy-start | bytes 9220
  49.5 13.7 %collective-permute-start.17 = (bf16[96,768]{1,0:T(8,128)(2,1)S(1)}, bf16[96,768]{1,0:T(8,128)(2,1)S(1)}, u32[]{:S(2)}, u32[]{:S(2)}) collective-permute-start(bf16[96,768]{1,0:T(8,128)(2,1)S(1)} %get-tuple-element.58), channel_id=1, source_target_pairs={{0,24},{4,28},{8,12},{12,8},{16,20},{20,16},{24,0},{28,4},{1,25},{... | collective-permute-start | bytes 442376 | tf_op jit(solution)/shard_map/ppermute | solution.py:445
  51.8 14.7 %collective-permute-start.18 = (bf16[96,768]{1,0:T(8,128)(2,1)S(1)}, bf16[96,768]{1,0:T(8,128)(2,1)S(1)}, u32[]{:S(2)}, u32[]{:S(2)}) collective-permute-start(bf16[96,768]{1,0:T(8,128)(2,1)S(1)} %get-tuple-element.59), channel_id=1, source_target_pairs={{0,28},{4,24},{8,20},{12,16},{16,12},{20,8},{24,4},{28,0},{1,29},{... | collective-permute-start | bytes 442376 | tf_op jit(solution)/shard_map/ppermute | solution.py:445
  54.1 18.6 %collective-permute-start.13 = (bf16[96,768]{1,0:T(8,128)(2,1)S(1)}, bf16[96,768]{1,0:T(8,128)(2,1)S(1)}, u32[]{:S(2)}, u32[]{:S(2)}) collective-permute-start(bf16[96,768]{1,0:T(8,128)(2,1)S(1)} %shard_map.64), channel_id=1, source_target_pairs={{0,16},{4,20},{8,24},{12,28},{16,0},{20,4},{24,8},{28,12},{1,17},{... | collective-permute-start | bytes 442376 | tf_op jit(solution)/shard_map/ppermute | solution.py:445

commit v7 on v6

--- a/solution.py
+++ b/solution.py
@@ -11,6 +11,7 @@
 HBM = pl.BlockSpec(memory_space=pltpu.HBM)
 ANY = pl.BlockSpec(memory_space=pl.ANY)
 BF, F32 = jnp.bfloat16, jnp.float32
+PARTS = (1, 3, 1, 1)
 
 
 def swap(value, axis):
@@ -255,7 +256,7 @@
         far = momenta - 2
         mixed = [(1, far), (far, 1)]
         steps = [k for k in steps if k[0] not in (1, far)]
-        steps = mixed[:1] + [(4, 4), (2, 2), (5, 5), (3, 3)] + mixed[1:] + [(7, 7)]
+        steps = mixed[:1] + [(5, 5), (2, 2), (4, 4), (3, 3)] + mixed[1:] + [(7, 7)]
     return steps
 
 
@@ -319,8 +320,8 @@
     columns = vert.shape[1]
     per_device = columns // momenta
     square = 2 * columns * half
-    unit = rows // 6
-    cuts = (0, unit, 3 * unit, 4 * unit, 5 * unit, rows)
+    unit = rows // sum(PARTS)
+    cuts = [unit * sum(PARTS[:i]) for i in range(len(PARTS) + 1)]
     spans = list(zip(cuts, cuts[1:]))
 
     pieces = fetch(left, spans[:1])
@@ -476,11 +477,11 @@
     momenta = mesh.shape["mom"]
 
     def run(left_part, *rest):
-        per_device = left_part.shape[1] // momenta
-        if per_device % 16 or momenta & (momenta - 1) or momenta < 2:
+        rows = left_part.shape[1] // mesh.shape["row"]
+        columns = left_part.shape[1] // mesh.shape["col"]
+        fits = rows % (128 * sum(PARTS)) == 0 and columns % (16 * momenta) == 0
+        if not fits or momenta & (momenta - 1) or momenta < 4:
             return step(plain)(left_part, *rest)
-        return step(tiled)(
-            left_part, *rest
-        )
+        return step(tiled)(left_part, *rest)
 
     return run

time: 74.2 us -> 74.2 us (level)
  waiting for transfers between devices: 38.4 us -> 40.6 us
  starting transfers between devices: 20.2 us -> 18.5 us
    ppermute x12 -> x10, waiting for transfers between devices: 21 us -> 23.8 us  [swap(): return lax.ppermute(value, axis, [(0, 1), (1, 0)])]
    ppermute x12 -> x10, starting transfers between devices: 8.26 us -> 6.46 us  [swap(): return lax.ppermute(value, axis, [(0, 1), (1, 0)])]
    pallas_call x18 -> x16, Pallas kernels: 10.4 us -> 9.95 us  [local(): pl.pallas_call(body, out_shape=outs, in_specs=[VMEM] * len(arrays), out_s...]
  transfers between devices with their start and end apart: 19 -> 17, of which waited for: 9 -> 9; matrix products, arithmetic and copies ran while one was open for 0% -> 0% of each run, Pallas kernels for 15% -> 14%
where the time goes in v7:
time: 74.2 us; the launch traced here: 74 us
  waiting for transfers between devices  40.6 us (55%)
  starting transfers between devices  18.5 us (25%)
  Pallas kernels  13.4 us (18%)
  local copies, waits for them, and re-layouts  1.28 us (2%)
    ppermute x10, waiting for transfers between devices, swap(): return lax.ppermute(value, axis, [(0, 1), (1, 0)])  23.8 us
    ppermute x7, waiting for transfers between devices, tiled(): got.append(lax.ppermute(block, 'mom', pairs))  16.8 us
    ppermute x7, starting transfers between devices, tiled(): got.append(lax.ppermute(block, 'mom', pairs))  12 us
    pallas_call x16, Pallas kernels, local(): pl.pallas_call(body, out_shape=outs, in_specs=[VMEM] * len(arrays), out_s...  9.95 us
    ppermute x10, starting transfers between devices, swap(): return lax.ppermute(value, axis, [(0, 1), (1, 0)])  6.46 us
    pallas_call x2, Pallas kernels, fetch(): pl.pallas_call(body, out_shape=[pltpu.VMEM((e - s, array.shape[1]), array...  2.12 us
  transfers between devices with their start and end apart: 17, of which 9 were waited for; matrix products, arithmetic and copies ran while one was open for 0% of the time, Pallas kernels for 14%

profile of v7, /device:TPU:0, one launch (start us, length us, event | category | flops | bytes accessed | tf_op | source)
XLA Modules:
  0.0 74.0 jit_solution(17965450975034060305)
XLA Ops:
  0.0 1.3 %copy-done.1 = bf16[1,768,768]{2,1,0:T(8,128)(2,1)S(1)} copy-done((bf16[1,768,768]{2,1,0:T(8,128)(2,1)S(1)}, bf16[1,768,768]{2,1,0:T(8,128)(2,1)}, u32[]{:S(2)}) %copy-start.1) | copy-done | bytes 1179672
  2.2 1.2 %shard_map.47 = (bf16[384,768]{1,0:T(8,128)(2,1)S(1)}, bf16[128,768]{1,0:T(8,128)(2,1)S(1)}, bf16[128,768]{1,0:T(8,128)(2,1)S(1)}) custom-call(bf16[768,768]{1,0:T(8,128)(2,1)} %bitcast.4), custom_call_target="tpu_custom_call" | custom-call | tf_op jit(solution)/shard_map/pallas_call | solution.py:56
  3.4 2.6 %collective-permute-start.3 = (bf16[384,768]{1,0:T(8,128)(2,1)S(1)}, bf16[384,768]{1,0:T(8,128)(2,1)S(1)}, u32[]{:S(2)}, u32[]{:S(2)}) collective-permute-start(bf16[384,768]{1,0:T(8,128)(2,1)S(1)} %get-tuple-element.32), channel_id=1, source_target_pairs={{0,1},{1,0},{2,3},{3,2},{4,5},{5,4},{6,7},{7,6},{8,9},{9,8},{10,11... | collective-permute-start | bytes 1769480 | tf_op jit(solution)/shard_map/ppermute | solution.py:18
  6.0 0.9 %shard_map.50 = bf16[128,768]{1,0:T(8,128)(2,1)S(1)} custom-call(bf16[768,768]{1,0:T(8,128)(2,1)} %bitcast.5), custom_call_target="tpu_custom_call" | custom-call | tf_op jit(solution)/shard_map/pallas_call | solution.py:56
  7.0 1.4 %shard_map.49 = (bf16[2,768,768]{2,1,0:T(8,128)(2,1)S(1)}, f32[768,768]{1,0:T(8,128)S(1)}, bf16[768,768]{1,0:T(8,128)(2,1)S(1)}) custom-call(bf16[768,768]{1,0:T(8,128)(2,1)S(1)} %bitcast.6, f32[1,1536]{1,0:T(1,128)S(1)} %copy-done.2, bf16[768,768]{1,0:T(8,128)(2,1)S(1)} %shard_map.48.flipped.refs_2_.refs_4_.refs_6_.refs_8_.refs_9_, ...), custom_call_target="tpu_custom_call" | custom-call | flops 905969664 | bytes 1048576 | tf_op jit(solution)/shard_map/pallas_call | solution.py:30
  8.4 15.7 %collective-permute-done.4.far = bf16[128,768]{1,0:T(8,128)(2,1)S(1)} collective-permute-done((bf16[128,768]{1,0:T(8,128)(2,1)S(1)}, bf16[128,768]{1,0:T(8,128)(2,1)S(1)}, u32[]{:S(2)}, u32[]{:S(2)}) %collective-permute-start.4) | collective-permute-done | bytes 196640 | tf_op jit(solution)/shard_map/ppermute | solution.py:18
  24.9 0.8 %shard_map.52 = (bf16[2,768,768]{2,1,0:T(8,128)(2,1)S(1)}, f32[768,768]{1,0:T(8,128)S(1)}, bf16[768,384]{1,0:T(8,128)(2,1)S(1)}) custom-call(bf16[384,768]{1,0:T(8,128)(2,1)S(1)} %collective-permute-done.3.far, f32[1,1536]{1,0:T(1,128)S(1)} %copy-done.2, bf16[768,768]{1,0:T(8,128)(2,1)S(1)} %get-tuple-element.30.other, ...), custom_call_target="tpu_custom_call", output_to_operand_aliasing={{0}: (3, {}), {1}: (4, {})} | custom-call | flops 452984832 | bytes 1048576 | tf_op jit(solution)/shard_map/pallas_call | solution.py:30
  26.3 1.7 %collective-permute-start.2 = (bf16[128,768]{1,0:T(8,128)(2,1)S(1)}, bf16[128,768]{1,0:T(8,128)(2,1)S(1)}, u32[]{:S(2)}, u32[]{:S(2)}) collective-permute-start(bf16[128,768]{1,0:T(8,128)(2,1)S(1)} %get-tuple-element.31), channel_id=1, source_target_pairs={{0,1},{1,0},{2,3},{3,2},{4,5},{5,4},{6,7},{7,6},{8,9},{9,8},{10,11... | collective-permute-start | bytes 589832 | tf_op jit(solution)/shard_map/ppermute | solution.py:18
  28.3 1.1 %shard_map.57.refs_8_ = f32[768,768]{1,0:T(8,128)S(1)} custom-call(bf16[768,128]{1,0:T(8,128)(2,1)S(1)} %get-tuple-element.42.refs_0_, bf16[768,384]{1,0:T(8,128)(2,1)S(1)} %get-tuple-element.43.refs_1_, bf16[768,128]{1,0:T(8,128)(2,1)S(1)} %collective-permute-done.6.refs_2_.refs_3_.refs_4_, ...), custom_call_target="tpu_custom_call", output_to_operand_aliasing={{}: (6, {})} | custom-call | flops 905969664 | bytes 1048576 | tf_op jit(solution)/shard_map/pallas_call | solution.py:30
  29.4 4.7 %collective-permute-done.2.far = bf16[128,768]{1,0:T(8,128)(2,1)S(1)} collective-permute-done((bf16[128,768]{1,0:T(8,128)(2,1)S(1)}, bf16[128,768]{1,0:T(8,128)(2,1)S(1)}, u32[]{:S(2)}, u32[]{:S(2)}) %collective-permute-start.2) | collective-permute-done | bytes 196640 | tf_op jit(solution)/shard_map/ppermute | solution.py:18
  34.6 2.8 %collective-permute-done.far = bf16[128,768]{1,0:T(8,128)(2,1)S(1)} collective-permute-done((bf16[128,768]{1,0:T(8,128)(2,1)S(1)}, bf16[128,768]{1,0:T(8,128)(2,1)S(1)}, u32[]{:S(2)}, u32[]{:S(2)}) %collective-permute-start) | collective-permute-done | bytes 196640 | tf_op jit(solution)/shard_map/ppermute | solution.py:18
  37.6 1.3 %shard_map.58._ = f32[768,768]{1,0:T(8,128)S(1)} custom-call(bf16[768,128]{1,0:T(8,128)(2,1)S(1)} %get-tuple-element.42.refs_0_, bf16[768,384]{1,0:T(8,128)(2,1)S(1)} %get-tuple-element.43.refs_1_, bf16[768,128]{1,0:T(8,128)(2,1)S(1)} %get-tuple-element.44.refs_2_, ...), custom_call_target="tpu_custom_call", output_to_operand_aliasing={{}: (8, {})} | custom-call | flops 301989888 | bytes 1048576 | tf_op jit(solution)/shard_map/pallas_call | solution.py:30
  41.6 1.8 %collective-permute-start.9 = (bf16[96,768]{1,0:T(8,128)(2,1)S(1)}, bf16[96,768]{1,0:T(8,128)(2,1)S(1)}, u32[]{:S(2)}, u32[]{:S(2)}) collective-permute-start(bf16[96,768]{1,0:T(8,128)(2,1)S(1)} %shard_map.61), channel_id=1, source_target_pairs={{0,4},{4,0},{8,16},{12,20},{16,8},{20,12},{24,28},{28,24},{1,5},{5... | collective-permute-start | bytes 442376 | tf_op jit(solution)/shard_map/ppermute | solution.py:446
  43.4 1.4 %shard_map.63 = (bf16[96,768]{1,0:T(8,128)(2,1)S(1)}, bf16[96,768]{1,0:T(8,128)(2,1)S(1)}, bf16[96,768]{1,0:T(8,128)(2,1)S(1)}, bf16[96,768]{1,0:T(8,128)(2,1)S(...) custom-call(bf16[768,128]{1,0:T(8,128)(2,1)S(1)} %get-tuple-element.42.refs_0_, ...), custom_call_target="tpu_custom_call" | custom-call | flops 113246208 | bytes 1048576 | tf_op jit(solution)/shard_map/pallas_call | solution.py:30
  44.7 1.7 %collective-permute-start.12 = (bf16[96,768]{1,0:T(8,128)(2,1)S(1)}, bf16[96,768]{1,0:T(8,128)(2,1)S(1)}, u32[]{:S(2)}, u32[]{:S(2)}) collective-permute-start(bf16[96,768]{1,0:T(8,128)(2,1)S(1)} %get-tuple-element.47), channel_id=1, source_target_pairs={{0,8},{4,12},{8,0},{12,4},{16,24},{20,28},{24,16},{28,20},{1,9},{5... | collective-permute-start | bytes 442376 | tf_op jit(solution)/shard_map/ppermute | solution.py:446
  46.5 2.5 %collective-permute-start.13 = (bf16[96,768]{1,0:T(8,128)(2,1)S(1)}, bf16[96,768]{1,0:T(8,128)(2,1)S(1)}, u32[]{:S(2)}, u32[]{:S(2)}) collective-permute-start(bf16[96,768]{1,0:T(8,128)(2,1)S(1)} %get-tuple-element.48), channel_id=1, source_target_pairs={{0,16},{4,20},{8,24},{12,28},{16,0},{20,4},{24,8},{28,12},{1,17},{... | collective-permute-start | bytes 442376 | tf_op jit(solution)/shard_map/ppermute | solution.py:446
  49.3 2.5 %collective-permute-start.15 = (bf16[96,768]{1,0:T(8,128)(2,1)S(1)}, bf16[96,768]{1,0:T(8,128)(2,1)S(1)}, u32[]{:S(2)}, u32[]{:S(2)}) collective-permute-start(bf16[96,768]{1,0:T(8,128)(2,1)S(1)} %get-tuple-element.50), channel_id=1, source_target_pairs={{0,24},{4,28},{8,12},{12,8},{16,20},{20,16},{24,0},{28,4},{1,25},{... | collective-permute-start | bytes 442376 | tf_op jit(solution)/shard_map/ppermute | solution.py:446
  52.2 2.1 %collective-permute-start.16 = (bf16[96,768]{1,0:T(8,128)(2,1)S(1)}, bf16[96,768]{1,0:T(8,128)(2,1)S(1)}, u32[]{:S(2)}, u32[]{:S(2)}) collective-permute-start(bf16[96,768]{1,0:T(8,128)(2,1)S(1)} %get-tuple-element.51), channel_id=1, source_target_pairs={{0,28},{4,24},{8,20},{12,16},{16,12},{20,8},{24,4},{28,0},{1,29},{... | collective-permute-start | bytes 442376 | tf_op jit(solution)/shard_map/ppermute | solution.py:446
  54.3 1.2 %collective-permute-start.11 = (bf16[96,768]{1,0:T(8,128)(2,1)S(1)}, bf16[96,768]{1,0:T(8,128)(2,1)S(1)}, u32[]{:S(2)}, u32[]{:S(2)}) collective-permute-start(bf16[96,768]{1,0:T(8,128)(2,1)S(1)} %shard_map.62), channel_id=1, source_target_pairs={{0,20},{4,16},{8,28},{12,24},{16,4},{20,0},{24,12},{28,8},{1,21},{... | collective-permute-start | bytes 442376 | tf_op jit(solution)/shard_map/ppermute | solution.py:446
  56.4 1.0 %collective-permute-done.14.refs_4_ = bf16[96,768]{1,0:T(8,128)(2,1)S(1)} collective-permute-done((bf16[96,768]{1,0:T(8,128)(2,1)S(1)}, bf16[96,768]{1,0:T(8,128)(2,1)S(1)}, u32[]{:S(2)}, u32[]{:S(2)}) %collective-permute-start.14) | collective-permute-done | bytes 147488 | tf_op jit(solution)/shard_map/ppermute | solution.py:446
  57.4 5.6 %collective-permute-done.15.refs_5_ = bf16[96,768]{1,0:T(8,128)(2,1)S(1)} collective-permute-done((bf16[96,768]{1,0:T(8,128)(2,1)S(1)}, bf16[96,768]{1,0:T(8,128)(2,1)S(1)}, u32[]{:S(2)}, u32[]{:S(2)}) %collective-permute-start.15) | collective-permute-done | bytes 147488 | tf_op jit(solution)/shard_map/ppermute | solution.py:446
  62.9 3.3 %collective-permute-done.16.refs_6_ = bf16[96,768]{1,0:T(8,128)(2,1)S(1)} collective-permute-done((bf16[96,768]{1,0:T(8,128)(2,1)S(1)}, bf16[96,768]{1,0:T(8,128)(2,1)S(1)}, u32[]{:S(2)}, u32[]{:S(2)}) %collective-permute-start.16) | collective-permute-done | bytes 147488 | tf_op jit(solution)/shard_map/ppermute | solution.py:446
  66.2 6.5 %collective-permute-done.11.refs_1_ = bf16[96,768]{1,0:T(8,128)(2,1)S(1)} collective-permute-done((bf16[96,768]{1,0:T(8,128)(2,1)S(1)}, bf16[96,768]{1,0:T(8,128)(2,1)S(1)}, u32[]{:S(2)}, u32[]{:S(2)}) %collective-permute-start.11) | collective-permute-done | bytes 147488 | tf_op jit(solution)/shard_map/ppermute | solution.py:446
  72.7 1.3 %shard_map.64 = bf16[768,768]{1,0:T(8,128)(2,1)} custom-call(bf16[768,256]{1,0:T(8,128)(2,1)S(1)} %shard_map.46.pick, bf16[96,768]{1,0:T(8,128)(2,1)S(1)} %collective-permute-done.9.refs_0_, bf16[96,768]{1,0:T(8,128)(2,1)S(1)} %collective-permute-done.11.refs_1_, bf16[96,768]{1,0:T(8,128)(2,1)S(1)} %collective-permute-done.12.refs_2_, ...), custom_call_target="tpu_custom_call" | custom-call | tf_op jit(solution)/shard_map/pallas_call | solution.py:448
  (37 shorter events, 7.6 us)
Async XLA Ops:
  0.0 1.3 %copy-start.1 = (bf16[1,768,768]{2,1,0:T(8,128)(2,1)S(1)}, bf16[1,768,768]{2,1,0:T(8,128)(2,1)}, u32[]{:S(2)}) copy-start(bf16[1,768,768]{2,1,0:T(8,128)(2,1)} %param.5) | copy-start | bytes 3538948
  1.3 5.7 %copy-start = (bf16[1,768,768]{2,1,0:T(8,128)(2,1)S(1)}, bf16[1,768,768]{2,1,0:T(8,128)(2,1)}, u32[]{:S(2)}) copy-start(bf16[1,768,768]{2,1,0:T(8,128)(2,1)} %param.4) | copy-start | bytes 3538948
  1.3 5.7 %copy-start.2 = (f32[1,1536]{1,0:T(1,128)S(1)}, f32[1,1536]{1,0:T(1,128)}, u32[]{:S(2)}) copy-start(f32[1,1536]{1,0:T(1,128)} %bubble.11) | copy-start | bytes 18436
  1.6 5.4 %collective-permute-start.1 = (bf16[768,768]{1,0:T(8,128)(2,1)S(1)}, bf16[768,768]{1,0:T(8,128)(2,1)S(1)}, u32[]{:S(2)}, u32[]{:S(2)}) collective-permute-start(bf16[768,768]{1,0:T(8,128)(2,1)S(1)} %shard_map.48.flipped.refs_2_.refs_4_.refs_6_.refs_8_.refs_9_), channel_id=1, source_target_pairs={{0,2},{2,0},{1,3},{3,1},{4,6},{6,4},{5,7},{7,5},{8,10},{10,8},{9,1... | collective-permute-start | bytes 3538952 | tf_op jit(solution)/shard_map/ppermute | solution.py:18
  3.4 21.5 %collective-permute-start.3 = (bf16[384,768]{1,0:T(8,128)(2,1)S(1)}, bf16[384,768]{1,0:T(8,128)(2,1)S(1)}, u32[]{:S(2)}, u32[]{:S(2)}) collective-permute-start(bf16[384,768]{1,0:T(8,128)(2,1)S(1)} %get-tuple-element.32), channel_id=1, source_target_pairs={{0,1},{1,0},{2,3},{3,2},{4,5},{5,4},{6,7},{7,6},{8,9},{9,8},{10,11... | collective-permute-start | bytes 1769480 | tf_op jit(solution)/shard_map/ppermute | solution.py:18
  6.9 17.3 %collective-permute-start.4 = (bf16[128,768]{1,0:T(8,128)(2,1)S(1)}, bf16[128,768]{1,0:T(8,128)(2,1)S(1)}, u32[]{:S(2)}, u32[]{:S(2)}) collective-permute-start(bf16[128,768]{1,0:T(8,128)(2,1)S(1)} %shard_map.50), channel_id=1, source_target_pairs={{0,1},{1,0},{2,3},{3,2},{4,5},{5,4},{6,7},{7,6},{8,9},{9,8},{10,11... | collective-permute-start | bytes 589832 | tf_op jit(solution)/shard_map/ppermute | solution.py:18
  25.7 11.9 %collective-permute-start.7 = (bf16[768,384]{1,0:T(8,128)(2,1)S(1)}, bf16[768,384]{1,0:T(8,128)(2,1)S(1)}, u32[]{:S(2)}, u32[]{:S(2)}) collective-permute-start(bf16[768,384]{1,0:T(8,128)(2,1)S(1)} %get-tuple-element.43.refs_1_), channel_id=1, source_target_pairs={{0,2},{2,0},{1,3},{3,1},{4,6},{6,4},{5,7},{7,5},{8,10},{10,8},{9,1... | collective-permute-start | bytes 1769480 | tf_op jit(solution)/shard_map/ppermute | solution.py:18
  25.8 2.5 %collective-permute-start.6 = (bf16[768,128]{1,0:T(8,128)(2,1)S(1)}, bf16[768,128]{1,0:T(8,128)(2,1)S(1)}, u32[]{:S(2)}, u32[]{:S(2)}) collective-permute-start(bf16[768,128]{1,0:T(8,128)(2,1)S(1)} %get-tuple-element.42.refs_0_), channel_id=1, source_target_pairs={{0,2},{2,0},{1,3},{3,1},{4,6},{6,4},{5,7},{7,5},{8,10},{10,8},{9,1... | collective-permute-start | bytes 589832 | tf_op jit(solution)/shard_map/ppermute | solution.py:18
  26.3 7.8 %collective-permute-start.2 = (bf16[128,768]{1,0:T(8,128)(2,1)S(1)}, bf16[128,768]{1,0:T(8,128)(2,1)S(1)}, u32[]{:S(2)}, u32[]{:S(2)}) collective-permute-start(bf16[128,768]{1,0:T(8,128)(2,1)S(1)} %get-tuple-element.31), channel_id=1, source_target_pairs={{0,1},{1,0},{2,3},{3,2},{4,5},{5,4},{6,7},{7,6},{8,9},{9,8},{10,11... | collective-permute-start | bytes 589832 | tf_op jit(solution)/shard_map/ppermute | solution.py:18
  28.0 9.4 %collective-permute-start = (bf16[128,768]{1,0:T(8,128)(2,1)S(1)}, bf16[128,768]{1,0:T(8,128)(2,1)S(1)}, u32[]{:S(2)}, u32[]{:S(2)}) collective-permute-start(bf16[128,768]{1,0:T(8,128)(2,1)S(1)} %get-tuple-element.29), channel_id=1, source_target_pairs={{0,1},{1,0},{2,3},{3,2},{4,5},{5,4},{6,7},{7,6},{8,9},{9,8},{10,11... | collective-permute-start | bytes 589832 | tf_op jit(solution)/shard_map/ppermute | solution.py:18
  34.5 4.4 %collective-permute-start.8 = (bf16[768,128]{1,0:T(8,128)(2,1)S(1)}, bf16[768,128]{1,0:T(8,128)(2,1)S(1)}, u32[]{:S(2)}, u32[]{:S(2)}) collective-permute-start(bf16[768,128]{1,0:T(8,128)(2,1)S(1)} %get-tuple-element.44.refs_2_), channel_id=1, source_target_pairs={{0,2},{2,0},{1,3},{3,1},{4,6},{6,4},{5,7},{7,5},{8,10},{10,8},{9,1... | collective-permute-start | bytes 589832 | tf_op jit(solution)/shard_map/ppermute | solution.py:18
  39.8 3.5 %collective-permute-start.10 = (bf16[768,128]{1,0:T(8,128)(2,1)S(1)}, bf16[768,128]{1,0:T(8,128)(2,1)S(1)}, u32[]{:S(2)}, u32[]{:S(2)}) collective-permute-start(bf16[768,128]{1,0:T(8,128)(2,1)S(1)} %get-tuple-element.45.refs_3_), channel_id=1, source_target_pairs={{0,2},{2,0},{1,3},{3,1},{4,6},{6,4},{5,7},{7,5},{8,10},{10,8},{9,1... | collective-permute-start | bytes 589832 | tf_op jit(solution)/shard_map/ppermute | solution.py:18
  39.9 1.5 %collective-permute-start.5 = (bf16[96,128]{1,0:T(8,128)(2,1)S(1)}, bf16[96,128]{1,0:T(8,128)(2,1)S(1)}, u32[]{:S(2)}, u32[]{:S(2)}) collective-permute-start(bf16[96,128]{1,0:T(8,128)(2,1)S(1)} %shard_map.54.refs_2_.refs_11_), channel_id=1, source_target_pairs={{0,2},{2,0},{1,3},{3,1},{4,6},{6,4},{5,7},{7,5},{8,10},{10,8},{9,1... | collective-permute-start | bytes 73736 | tf_op jit(solution)/shard_map/ppermute | solution.py:18
  41.6 10.7 %collective-permute-start.9 = (bf16[96,768]{1,0:T(8,128)(2,1)S(1)}, bf16[96,768]{1,0:T(8,128)(2,1)S(1)}, u32[]{:S(2)}, u32[]{:S(2)}) collective-permute-start(bf16[96,768]{1,0:T(8,128)(2,1)S(1)} %shard_map.61), channel_id=1, source_target_pairs={{0,4},{4,0},{8,16},{12,20},{16,8},{20,12},{24,28},{28,24},{1,5},{5... | collective-permute-start | bytes 442376 | tf_op jit(solution)/shard_map/ppermute | solution.py:446
  44.7 9.6 %collective-permute-start.12 = (bf16[96,768]{1,0:T(8,128)(2,1)S(1)}, bf16[96,768]{1,0:T(8,128)(2,1)S(1)}, u32[]{:S(2)}, u32[]{:S(2)}) collective-permute-start(bf16[96,768]{1,0:T(8,128)(2,1)S(1)} %get-tuple-element.47), channel_id=1, source_target_pairs={{0,8},{4,12},{8,0},{12,4},{16,24},{20,28},{24,16},{28,20},{1,9},{5... | collective-permute-start | bytes 442376 | tf_op jit(solution)/shard_map/ppermute | solution.py:446
  46.5 9.9 %collective-permute-start.13 = (bf16[96,768]{1,0:T(8,128)(2,1)S(1)}, bf16[96,768]{1,0:T(8,128)(2,1)S(1)}, u32[]{:S(2)}, u32[]{:S(2)}) collective-permute-start(bf16[96,768]{1,0:T(8,128)(2,1)S(1)} %get-tuple-element.48), channel_id=1, source_target_pairs={{0,16},{4,20},{8,24},{12,28},{16,0},{20,4},{24,8},{28,12},{1,17},{... | collective-permute-start | bytes 442376 | tf_op jit(solution)/shard_map/ppermute | solution.py:446
  49.0 8.4 %collective-permute-start.14 = (bf16[96,768]{1,0:T(8,128)(2,1)S(1)}, bf16[96,768]{1,0:T(8,128)(2,1)S(1)}, u32[]{:S(2)}, u32[]{:S(2)}) collective-permute-start(bf16[96,768]{1,0:T(8,128)(2,1)S(1)} %get-tuple-element.49), channel_id=1, source_target_pairs={{0,12},{4,8},{8,4},{12,0},{16,28},{20,24},{24,20},{28,16},{1,13},{... | collective-permute-start | bytes 442376 | tf_op jit(solution)/shard_map/ppermute | solution.py:446
  49.3 6.2 %copy-start.3 = (s32[96,8]{0,1:T(8,128)S(1)}, s32[96,8]{0,1:T(8,128)}, u32[]{:S(2)}) copy-start(s32[96,8]{0,1:T(8,128)} %param.7) | copy-start | bytes 9220
  49.3 13.6 %collective-permute-start.15 = (bf16[96,768]{1,0:T(8,128)(2,1)S(1)}, bf16[96,768]{1,0:T(8,128)(2,1)S(1)}, u32[]{:S(2)}, u32[]{:S(2)}) collective-permute-start(bf16[96,768]{1,0:T(8,128)(2,1)S(1)} %get-tuple-element.50), channel_id=1, source_target_pairs={{0,24},{4,28},{8,12},{12,8},{16,20},{20,16},{24,0},{28,4},{1,25},{... | collective-permute-start | bytes 442376 | tf_op jit(solution)/shard_map/ppermute | solution.py:446
  52.2 14.0 %collective-permute-start.16 = (bf16[96,768]{1,0:T(8,128)(2,1)S(1)}, bf16[96,768]{1,0:T(8,128)(2,1)S(1)}, u32[]{:S(2)}, u32[]{:S(2)}) collective-permute-start(bf16[96,768]{1,0:T(8,128)(2,1)S(1)} %get-tuple-element.51), channel_id=1, source_target_pairs={{0,28},{4,24},{8,20},{12,16},{16,12},{20,8},{24,4},{28,0},{1,29},{... | collective-permute-start | bytes 442376 | tf_op jit(solution)/shard_map/ppermute | solution.py:446
  54.3 18.4 %collective-permute-start.11 = (bf16[96,768]{1,0:T(8,128)(2,1)S(1)}, bf16[96,768]{1,0:T(8,128)(2,1)S(1)}, u32[]{:S(2)}, u32[]{:S(2)}) collective-permute-start(bf16[96,768]{1,0:T(8,128)(2,1)S(1)} %shard_map.62), channel_id=1, source_target_pairs={{0,20},{4,16},{8,28},{12,24},{16,4},{20,0},{24,12},{28,8},{1,21},{... | collective-permute-start | bytes 442376 | tf_op jit(solution)/shard_map/ppermute | solution.py:446
